TPU v7x, 32 devices: a whole 2x2x4 slice. The times are simulated.
32 devices in a mesh: seq: 16 (over z, y, x), fsdp: 2 (over core).
Axes of the slice: x: 2, y: 2, z: 4, core: 2. Of those that a mesh axis runs over, the one named last changes fastest.
Arguments:
- inputs: bfloat16 [2, 2048, 1536], P('fsdp', 'seq'), may hold values from -6 to 6
- segment_ids: int32 [2, 2048], P('fsdp', 'seq'), may hold values from 0 to 3, never falling along the last dimension, each value on 1 to 1024 neighbouring positions
- cotangent: bfloat16 [2, 2048, 1536], P('fsdp', 'seq'), may hold values from -6 to 6
- norm_mixer: bfloat16 [1536], P(('seq', 'fsdp')), may hold values from 0.5 to 1.5
- in_proj: bfloat16 [1536, 6144], P(('seq', 'fsdp')), may hold values from -0.15625 to 0.15625
- conv_weight: bfloat16 [4, 3072], P(None, ('seq', 'fsdp')), may hold values from -3 to 3
- conv_bias: bfloat16 [3072], P(('seq', 'fsdp')), may hold values from -3 to 3
- state_proj: bfloat16 [3072, 128], P(('seq', 'fsdp')), may hold values from -0.109375 to 0.109375
- step_proj: bfloat16 [96, 3072], P(None, ('seq', 'fsdp')), may hold values from -0.625 to 0.625
- step_bias: bfloat16 [3072], P(('seq', 'fsdp')), may hold values from -5 to -1
- decay_log: bfloat16 [3072, 16], P(('seq', 'fsdp')), may hold values from -7 to 0.5
- skip_gain: bfloat16 [3072], P(('seq', 'fsdp')), may hold values from 0.5 to 1.5
- mixer_out: bfloat16 [3072, 1536], P(('seq', 'fsdp')), may hold values from -0.109375 to 0.109375
- norm_ffn_one: bfloat16 [1536], P(('seq', 'fsdp')), may hold values from 0.5 to 1.5
- gate_up_one: bfloat16 [1536, 8192], P(('seq', 'fsdp')), may hold values from -0.15625 to 0.15625
- down_one: bfloat16 [4096, 1536], P(('seq', 'fsdp')), may hold values from -0.09375 to 0.09375
- norm_attn: bfloat16 [1536], P(('seq', 'fsdp')), may hold values from 0.5 to 1.5
- qkv_proj: bfloat16 [1536, 4608], P(('seq', 'fsdp')), may hold values from -0.15625 to 0.15625
- attn_out: bfloat16 [1536, 1536], P(('seq', 'fsdp')), may hold values from -1.25 to 1.25
- norm_ffn_two: bfloat16 [1536], P(('seq', 'fsdp')), may hold values from 0.5 to 1.5
- gate_up_two: bfloat16 [1536, 8192], P(('seq', 'fsdp')), may hold values from -0.15625 to 0.15625
- down_two: bfloat16 [4096, 1536], P(('seq', 'fsdp')), may hold values from -0.09375 to 0.09375
Outputs:
- outputs: bfloat16 [2, 2048, 1536], P('fsdp', 'seq')
- grad_inputs: float32 [2, 2048, 1536], P('fsdp', 'seq')
- grad_norm_mixer: float32 [1536], P(('seq', 'fsdp'))
- grad_in_proj: float32 [1536, 6144], P(('seq', 'fsdp'))
- grad_conv_weight: float32 [4, 3072], P(None, ('seq', 'fsdp'))
- grad_conv_bias: float32 [3072], P(('seq', 'fsdp'))
- grad_state_proj: float32 [3072, 128], P(('seq', 'fsdp'))
- grad_step_proj: float32 [96, 3072], P(None, ('seq', 'fsdp'))
- grad_step_bias: float32 [3072], P(('seq', 'fsdp'))
- grad_decay_log: float32 [3072, 16], P(('seq', 'fsdp'))
- grad_skip_gain: float32 [3072], P(('seq', 'fsdp'))
- grad_mixer_out: float32 [3072, 1536], P(('seq', 'fsdp'))
- grad_norm_ffn_one: float32 [1536], P(('seq', 'fsdp'))
- grad_gate_up_one: float32 [1536, 8192], P(('seq', 'fsdp'))
- grad_down_one: float32 [4096, 1536], P(('seq', 'fsdp'))
- grad_norm_attn: float32 [1536], P(('seq', 'fsdp'))
- grad_qkv_proj: float32 [1536, 4608], P(('seq', 'fsdp'))
- grad_attn_out: float32 [1536, 1536], P(('seq', 'fsdp'))
- grad_norm_ffn_two: float32 [1536], P(('seq', 'fsdp'))
- grad_gate_up_two: float32 [1536, 8192], P(('seq', 'fsdp'))
- grad_down_two: float32 [4096, 1536], P(('seq', 'fsdp'))
Inputs may be any that keep to these rules, and one draw needn't show every extreme that they name: `segment_ids`: along a stream the ids never fall; a document (one id within one sequence of 2048 tokens) holds at most 1024 tokens.
All inputs are finite; a program needn't handle non-finite values.
Results may differ from a plain program's by a relative error of at most 0.024.
Values may be sent and summed in bfloat16 or wider, within the bound.
A program may use at most 576 MiB of HBM per device.

v0:
```python
import math

import jax
import jax.numpy as jnp
from jax import lax
from jax.sharding import PartitionSpec as P

H = 12
HD = 128
WIN = 2048
SEQ_MAX = 8192


EPS = 1e-05
HIGH = lax.Precision.HIGHEST
NEGATIVE = -1e30


def shifted(x, axis, by):
    length = lax.axis_size(axis)
    pairs = [(i, i + by) for i in range(length) if 0 <= i + by < length]
    return lax.ppermute(x, axis, pairs)


def carried_in(x, axis, join, neutral):
    place = lax.axis_index(axis)
    gathered = jax.tree.map(
        lambda a, kind: lax.all_gather(a.astype(kind), axis), x, (jnp.bfloat16, jnp.bfloat16)
    )
    state = jax.tree.map(lambda a, e: jnp.zeros_like(a) + jnp.asarray(e, a.dtype), x, neutral)

    def carried_one(step, state):
        return join(
            state,
            jax.tree.map(
                lambda a, own: lax.dynamic_index_in_dim(a, step, 0, False).astype(own.dtype),
                gathered,
                x,
            ),
        )

    return lax.fori_loop(0, place, carried_one, state)


def prefix(x, axis, join, neutral):
    count = lax.axis_size(axis)
    place = lax.axis_index(axis)
    ahead = count - 1 - place
    gathered = jax.tree.map(
        lambda a, kind: lax.all_gather(a.astype(kind), axis),
        x,
        jax.tree.map(lambda a: jnp.bfloat16 if a.dtype == jnp.float32 else a.dtype, x),
    )
    state = jax.tree.map(lambda a, e: jnp.zeros_like(a) + jnp.asarray(e, a.dtype), x, neutral)

    def prefix_one(step, state):
        source = count - 1 - step
        return join(
            state,
            jax.tree.map(
                lambda a, own: lax.dynamic_index_in_dim(a, source, 0, False).astype(own.dtype),
                gathered,
                x,
            ),
        )

    return lax.fori_loop(0, ahead, prefix_one, state)


def for_sending(x):

    def short(part):
        return part.astype(jnp.bfloat16) if part.dtype == jnp.float32 else part

    return jax.tree.map(short, x)


def as_low(values):
    return values.astype(jnp.bfloat16)


def matmul(left_side, right_side):
    return jnp.dot(left_side, right_side, preferred_element_type=jnp.float32)


def left_grad(grad_low, weight):
    return lax.dot_general(
        grad_low, weight, (((1,), (1,)), ((), ())), preferred_element_type=jnp.float32
    )


def weight_grad(inputs_low, grad_low):
    return lax.dot_general(
        inputs_low, grad_low, (((0,), (0,)), ((), ())), preferred_element_type=jnp.float32
    )


def rms_norm(values, norm_gain):
    return values * lax.rsqrt(jnp.mean(values * values, axis=-1, keepdims=True) + EPS) * norm_gain


def rope_angles(positions):
    half_size = HD // 2
    inverse = jnp.exp(jnp.arange(half_size, dtype=jnp.float32) * (-math.log(10000.0) * 2.0 / HD))
    return positions.astype(jnp.float32)[:, None] * inverse[None, :]


def rotate(values, angles):
    half_size = values.shape[-1] // 2
    cosine = jnp.cos(angles)[:, None, :]
    sine_part = jnp.sin(angles)[:, None, :]
    first_half = values[..., :half_size]
    second_half = values[..., half_size:]
    return jnp.concatenate(
        [
            first_half * cosine - second_half * sine_part,
            second_half * cosine + first_half * sine_part,
        ],
        axis=-1,
    )


def scan_tokens(step_rate, u_values, in_mat, out_mat, keep_flag, decay_rate, block_size):
    tokens, inner_width = step_rate.shape

    def token_step(state_now, token_item):
        rate_now, input_now, in_now, out_now, keep_now = token_item
        state_now = (
            jnp.exp(rate_now[:, None] * decay_rate) * keep_now * state_now
            + (rate_now * input_now)[:, None] * in_now[None, :]
        )
        return (state_now, jnp.dot(state_now, out_now, precision=HIGH))

    def block_step(state_now, block_items):
        return lax.scan(token_step, state_now, block_items)

    blocked = tuple(
        (
            member.reshape((tokens // block_size, block_size) + member.shape[1:])
            for member in (step_rate, u_values, in_mat, out_mat, keep_flag)
        )
    )
    state_now, outputs = lax.scan(jax.checkpoint(block_step), jnp.zeros_like(decay_rate), blocked)
    return (outputs.reshape(tokens, inner_width), state_now)


def chain_states(earlier_part, later_part):
    return (earlier_part[0] * later_part[0], later_part[0] * earlier_part[1] + later_part[1])


def conv_apply(ext_values, conv_full, bias_full, conv_mask):
    tokens = conv_mask.shape[1]
    total_sum = jnp.broadcast_to(bias_full[None, :], (tokens, bias_full.shape[0]))
    for offset in range(conv_full.shape[0]):
        total_sum = (
            total_sum
            + conv_full[offset] * ext_values[offset : offset + tokens] * conv_mask[offset][:, None]
        )
    return jax.nn.silu(total_sum)


def local_scan(
    step_pre, bias_full, log_full, u_values, in_mat, out_mat, keep_flag, alive_flag, lower_tri
):
    step_rate = jax.nn.softplus(step_pre + bias_full)
    decay_rate = -jnp.exp(log_full)
    zero_out, local_state = scan_tokens(
        step_rate,
        u_values,
        in_mat,
        out_mat,
        keep_flag,
        decay_rate,
        math.gcd(step_rate.shape[0], 32),
    )
    cumulated = jnp.dot(lower_tri, step_rate, precision=HIGH)
    carried_last = alive_flag[-1] * jnp.exp(cumulated[-1][:, None] * decay_rate)
    return (decay_rate, cumulated, zero_out, local_state, carried_last)


def carry_terms(cumulated, decay_rate, alive_flag):
    return jnp.exp(cumulated[:, :, None] * decay_rate[None, :, :]) * alive_flag[:, None, None]


def finish_outputs(
    zero_out, cumulated, decay_rate, alive_flag, state_in, out_mat, skip_full, u_values
):
    carried = carry_terms(cumulated, decay_rate, alive_flag)
    return (
        zero_out
        + jnp.sum(carried * state_in[None] * out_mat[:, None, :], axis=-1)
        + skip_full * u_values
    )


def selective(
    step_pre,
    bias_full,
    log_full,
    u_values,
    in_mat,
    out_mat,
    skip_full,
    state_in,
    keep_flag,
    alive_flag,
    lower_tri,
):
    decay_rate, cumulated, zero_out, local_state, carried_last = local_scan(
        step_pre, bias_full, log_full, u_values, in_mat, out_mat, keep_flag, alive_flag, lower_tri
    )
    y_values = finish_outputs(
        zero_out, cumulated, decay_rate, alive_flag, state_in, out_mat, skip_full, u_values
    )
    return (y_values, local_state + carried_last * state_in)


def mixer_forward(layer_in, weights, seg_float, positions, seq_len):
    (
        norm_gain,
        in_proj,
        conv_weight,
        conv_bias,
        state_proj,
        step_proj,
        step_bias,
        decay_log,
        skip_gain,
        mixer_out,
    ) = weights
    tokens = layer_in.shape[0]
    inner_width = in_proj.shape[1] // 2
    tap_count = conv_weight.shape[0] - 1
    rank_width = step_proj.shape[0]
    state_width = decay_log.shape[1]
    normed = as_low(rms_norm(layer_in, norm_gain.astype(jnp.float32)))
    mixed_proj = matmul(normed, in_proj)
    stream_part = mixed_proj[:, :inner_width]
    rim_values, rim_segs = (
        shifted(stream_part[tokens - tap_count :].astype(jnp.bfloat16), "seq", 1).astype(
            jnp.float32
        ),
        shifted(seg_float[tokens - tap_count :].astype(jnp.bfloat16), "seq", 1).astype(jnp.float32),
    )
    ext_values = jnp.concatenate([rim_values, stream_part], axis=0)
    ext_segs = jnp.concatenate([rim_segs, seg_float], axis=0)
    ext_pos = positions[0] - tap_count + jnp.arange(tokens + tap_count, dtype=jnp.int32)
    sequence_now = positions // seq_len
    conv_mask = jnp.stack(
        [
            (
                (ext_pos[offset : offset + tokens] >= 0)
                & (ext_segs[offset : offset + tokens] == seg_float)
                & (ext_pos[offset : offset + tokens] // seq_len == sequence_now)
            ).astype(jnp.float32)
            for offset in range(tap_count + 1)
        ]
    )
    starts = (positions % seq_len == 0) | (
        ext_segs[tap_count - 1 : tap_count - 1 + tokens] != seg_float
    )
    keep_flag = jnp.where(starts, 0.0, 1.0).astype(jnp.float32)
    lower_tri = (jnp.arange(tokens)[:, None] >= jnp.arange(tokens)[None, :]).astype(jnp.float32)
    alive_flag = (jnp.dot(lower_tri, starts.astype(jnp.float32), precision=HIGH) == 0).astype(
        jnp.float32
    )
    u_values = conv_apply(
        ext_values, conv_weight.astype(jnp.float32), conv_bias.astype(jnp.float32), conv_mask
    )
    u_low = as_low(u_values)
    projected = matmul(u_low, state_proj)
    dt_low = as_low(projected[:, :rank_width])
    in_mat = projected[:, rank_width : rank_width + state_width]
    out_mat = projected[:, rank_width + state_width :]
    step_pre = matmul(dt_low, step_proj)
    decay_rate, cumulated, zero_out, local_state, carried_last = local_scan(
        step_pre,
        step_bias.astype(jnp.float32),
        decay_log.astype(jnp.float32),
        u_values,
        in_mat,
        out_mat,
        keep_flag,
        alive_flag,
        lower_tri,
    )
    chain_out = carried_in(
        (carried_last, local_state),
        "seq",
        chain_states,
        (jnp.ones_like(local_state), jnp.zeros_like(local_state)),
    )
    state_in = chain_out[1]
    y_values = finish_outputs(
        zero_out,
        cumulated,
        decay_rate,
        alive_flag,
        state_in,
        out_mat,
        skip_gain.astype(jnp.float32),
        u_values,
    )
    gated_low = as_low(y_values * jax.nn.silu(mixed_proj[:, inner_width:]))
    result = layer_in + matmul(gated_low, mixer_out)
    kept_values = (
        normed,
        mixed_proj,
        ext_values,
        conv_mask,
        keep_flag,
        alive_flag,
        lower_tri,
        u_values,
        u_low,
        dt_low,
        projected,
        step_pre,
        state_in,
        carried_last,
        y_values,
        gated_low,
    )
    return (result, kept_values)


def mixer_back(grad_out, layer_in, weights, kept_values):
    (
        norm_gain,
        in_proj,
        conv_weight,
        conv_bias,
        state_proj,
        step_proj,
        step_bias,
        decay_log,
        skip_gain,
        mixer_out,
    ) = weights
    (
        normed,
        mixed_proj,
        ext_values,
        conv_mask,
        keep_flag,
        alive_flag,
        lower_tri,
        u_values,
        u_low,
        dt_low,
        projected,
        step_pre,
        state_in,
        carried_last,
        y_values,
        gated_low,
    ) = kept_values
    tokens = layer_in.shape[0]
    inner_width = in_proj.shape[1] // 2
    tap_count = conv_weight.shape[0] - 1
    rank_width = step_proj.shape[0]
    state_width = decay_log.shape[1]
    bias_full = step_bias.astype(jnp.float32)
    log_full = decay_log.astype(jnp.float32)
    skip_full = skip_gain.astype(jnp.float32)
    in_mat = projected[:, rank_width : rank_width + state_width]
    out_mat = projected[:, rank_width + state_width :]
    grad_low = as_low(grad_out)
    grad_mixer_out = weight_grad(gated_low, grad_low)
    grad_gated = left_grad(grad_low, mixer_out)
    gate_back = jax.vjp(
        lambda y_part, z_part: y_part * jax.nn.silu(z_part), y_values, mixed_proj[:, inner_width:]
    )[1]
    grad_y, grad_gate = gate_back(grad_gated)
    step_rate = jax.nn.softplus(step_pre + bias_full)
    decay_rate = -jnp.exp(log_full)
    cumulated = jnp.dot(lower_tri, step_rate, precision=HIGH)
    own_grad = jnp.sum(
        carry_terms(cumulated, decay_rate, alive_flag) * grad_y[:, :, None] * out_mat[:, None, :],
        axis=0,
    )
    chain_out = prefix(
        (carried_last, own_grad),
        "seq",
        chain_states,
        (jnp.ones_like(own_grad), jnp.zeros_like(own_grad)),
    )

    def scan_part(pre_step, bias_step, log_decay, inputs_u, mat_in, mat_out, gain_skip):
        return selective(
            pre_step,
            bias_step,
            log_decay,
            inputs_u,
            mat_in,
            mat_out,
            gain_skip,
            state_in,
            keep_flag,
            alive_flag,
            lower_tri,
        )

    scan_back = jax.vjp(
        scan_part, step_pre, bias_full, log_full, u_values, in_mat, out_mat, skip_full
    )[1]
    grad_pre, grad_step_bias, grad_decay_log, grad_u_scan, grad_in_mat, grad_out_mat, grad_skip = (
        scan_back((grad_y, chain_out[1]))
    )
    pre_low = as_low(grad_pre)
    grad_step_proj = weight_grad(dt_low, pre_low)
    proj_low = as_low(
        jnp.concatenate([left_grad(pre_low, step_proj), grad_in_mat, grad_out_mat], axis=1)
    )
    grad_state_proj = weight_grad(u_low, proj_low)
    grad_u = grad_u_scan + left_grad(proj_low, state_proj)
    conv_back = jax.vjp(
        lambda ext_part, weight_part, bias_part: conv_apply(
            ext_part, weight_part, bias_part, conv_mask
        ),
        ext_values,
        conv_weight.astype(jnp.float32),
        conv_bias.astype(jnp.float32),
    )[1]
    grad_ext, grad_conv_weight, grad_conv_bias = conv_back(grad_u)
    rim_grad = shifted(for_sending(grad_ext[:tap_count]), "seq", -1)
    grad_stream = grad_ext[tap_count:] + jnp.concatenate(
        [jnp.zeros((tokens - tap_count, inner_width), jnp.float32), rim_grad], axis=0
    )
    mixed_low = as_low(jnp.concatenate([grad_stream, grad_gate], axis=1))
    grad_in_proj = weight_grad(normed, mixed_low)
    norm_back = jax.vjp(rms_norm, layer_in, norm_gain.astype(jnp.float32))[1]
    grad_acts, grad_norm = norm_back(left_grad(mixed_low, in_proj))
    return (
        grad_out + grad_acts,
        (
            grad_norm,
            grad_in_proj,
            grad_conv_weight,
            grad_conv_bias,
            grad_state_proj,
            grad_step_proj,
            grad_step_bias,
            grad_decay_log,
            grad_skip,
            grad_mixer_out,
        ),
    )


def feed_forward(layer_in, norm_gain, gate_up, down_proj):
    hidden_width = down_proj.shape[0]
    normed = as_low(rms_norm(layer_in, norm_gain.astype(jnp.float32)))
    hidden_pre = matmul(normed, gate_up)
    hidden = as_low(jax.nn.silu(hidden_pre[:, :hidden_width]) * hidden_pre[:, hidden_width:])
    return (layer_in + matmul(hidden, down_proj), (normed, hidden_pre, hidden))


def feed_back(grad_out, layer_in, norm_gain, gate_up, down_proj, kept_values):
    normed, hidden_pre, hidden = kept_values
    hidden_width = down_proj.shape[0]
    grad_low = as_low(grad_out)
    grad_down = weight_grad(hidden, grad_low)
    grad_hidden = left_grad(grad_low, down_proj)
    swiglu_back = jax.vjp(
        lambda pre_acts: jax.nn.silu(pre_acts[:, :hidden_width]) * pre_acts[:, hidden_width:],
        hidden_pre,
    )[1]
    pre_low = as_low(swiglu_back(grad_hidden)[0])
    grad_gate_up = weight_grad(normed, pre_low)
    norm_back = jax.vjp(rms_norm, layer_in, norm_gain.astype(jnp.float32))[1]
    grad_acts, grad_norm = norm_back(left_grad(pre_low, gate_up))
    return (grad_out + grad_acts, grad_norm, grad_gate_up, grad_down)


def attention_forward(layer_in, weights, seg_float, positions, seq_len):
    norm_gain, qkv_proj, attn_out = weights
    tokens = layer_in.shape[0]
    model_width = attn_out.shape[0]
    score_scale = HD ** (-0.5)
    normed = as_low(rms_norm(layer_in, norm_gain.astype(jnp.float32)))
    qkv_all = matmul(normed, qkv_proj)
    angles = rope_angles(positions % seq_len)
    queries = as_low(rotate(qkv_all[:, :model_width].reshape(tokens, H, HD), angles))
    keys_own = as_low(
        rotate(qkv_all[:, model_width : 2 * model_width].reshape(tokens, H, HD), angles)
    )
    values_own = as_low(qkv_all[:, 2 * model_width :].reshape(tokens, H, HD))
    seg_low = as_low(seg_float)
    hop_count = WIN // tokens
    key_parts, value_parts, seg_parts = ([], [], [])
    for distance in range(hop_count, 0, -1):
        rim_keys, rim_values, rim_segs = shifted((keys_own, values_own, seg_low), "seq", distance)
        key_parts.append(rim_keys)
        value_parts.append(rim_values)
        seg_parts.append(rim_segs)
    all_keys = jnp.concatenate(key_parts + [keys_own], axis=0)
    all_values = jnp.concatenate(value_parts + [values_own], axis=0)
    all_segs = jnp.concatenate(seg_parts + [seg_low], axis=0).astype(jnp.float32)
    key_pos = positions[0] - WIN + jnp.arange(WIN + tokens, dtype=jnp.int32)
    distance_back = positions[:, None] - key_pos[None, :]
    key_mask = (
        (key_pos[None, :] >= 0)
        & (distance_back >= 0)
        & (distance_back < WIN)
        & (all_segs[None, :] == seg_float[:, None])
        & (key_pos[None, :] // seq_len == (positions // seq_len)[:, None])
    )
    scores = (
        jnp.einsum("thd,shd->hts", queries, all_keys, preferred_element_type=jnp.float32)
        * score_scale
    )
    masked = jnp.where(key_mask[None], scores, NEGATIVE)
    top_score = jnp.max(masked, axis=-1, keepdims=True)
    exp_scores = jnp.exp(masked - top_score)
    exp_total = jnp.sum(exp_scores, axis=-1, keepdims=True)
    soft_weights = exp_scores / exp_total
    log_total = top_score + jnp.log(exp_total)
    attended = jnp.einsum(
        "hts,shd->thd", as_low(soft_weights), all_values, preferred_element_type=jnp.float32
    )
    att_low = as_low(attended).reshape(tokens, model_width)
    result = layer_in + matmul(att_low, attn_out)
    return (result, (normed, angles, queries, all_keys, all_values, key_mask, log_total, att_low))


def attention_back(grad_out, layer_in, weights, kept_values):
    norm_gain, qkv_proj, attn_out = weights
    normed, angles, queries, all_keys, all_values, key_mask, log_total, att_low = kept_values
    tokens = layer_in.shape[0]
    model_width = attn_out.shape[0]
    score_scale = HD ** (-0.5)
    hop_count = WIN // tokens
    grad_low = as_low(grad_out)
    grad_attn_out = weight_grad(att_low, grad_low)
    grad_att = as_low(left_grad(grad_low, attn_out)).reshape(tokens, H, HD)
    scores = (
        jnp.einsum("thd,shd->hts", queries, all_keys, preferred_element_type=jnp.float32)
        * score_scale
    )
    soft_weights = jnp.exp(jnp.where(key_mask[None], scores, NEGATIVE) - log_total)
    grad_probs = jnp.einsum(
        "thd,shd->hts", grad_att, all_values, preferred_element_type=jnp.float32
    )
    grad_values = jnp.einsum(
        "hts,thd->shd", as_low(soft_weights), grad_att, preferred_element_type=jnp.float32
    )
    rowdot = jnp.sum(soft_weights * grad_probs, axis=-1, keepdims=True)
    grad_scores = as_low(soft_weights * (grad_probs - rowdot))
    grad_queries = (
        jnp.einsum("hts,shd->thd", grad_scores, all_keys, preferred_element_type=jnp.float32)
        * score_scale
    )
    grad_keys = (
        jnp.einsum("hts,thd->shd", grad_scores, queries, preferred_element_type=jnp.float32)
        * score_scale
    )
    keys_total = grad_keys[WIN:]
    values_total = grad_values[WIN:]
    for distance in range(1, hop_count + 1):
        offset = (hop_count - distance) * tokens
        back_keys, back_values = (
            shifted(
                grad_keys[offset : offset + tokens].astype(jnp.bfloat16), "seq", -distance
            ).astype(jnp.float32),
            shifted(
                grad_values[offset : offset + tokens].astype(jnp.bfloat16), "seq", -distance
            ).astype(jnp.float32),
        )
        keys_total = keys_total + back_keys
        values_total = values_total + back_values
    qkv_low = as_low(
        jnp.concatenate(
            [
                rotate(grad_queries, -angles).reshape(tokens, model_width),
                rotate(keys_total, -angles).reshape(tokens, model_width),
                values_total.reshape(tokens, model_width),
            ],
            axis=1,
        )
    )
    grad_qkv_proj = weight_grad(normed, qkv_low)
    norm_back = jax.vjp(rms_norm, layer_in, norm_gain.astype(jnp.float32))[1]
    grad_acts, grad_norm = norm_back(left_grad(qkv_low, qkv_proj))
    return (grad_out + grad_acts, grad_norm, grad_qkv_proj, grad_attn_out)


def fetch_lower(shards):
    return (
        lax.all_gather(shards[0], ("seq", "fsdp"), axis=0, tiled=True),
        lax.all_gather(shards[1], ("seq", "fsdp"), axis=0, tiled=True),
        lax.all_gather(shards[2], ("seq", "fsdp"), axis=1, tiled=True),
        lax.all_gather(shards[3], ("seq", "fsdp"), axis=0, tiled=True),
        lax.all_gather(shards[4], ("seq", "fsdp"), axis=0, tiled=True),
        lax.all_gather(shards[5], ("seq", "fsdp"), axis=1, tiled=True),
        lax.all_gather(shards[6], ("seq", "fsdp"), axis=0, tiled=True),
        lax.all_gather(shards[7], ("seq", "fsdp"), axis=0, tiled=True),
        lax.all_gather(shards[8], ("seq", "fsdp"), axis=0, tiled=True),
        lax.all_gather(shards[9], ("seq", "fsdp"), axis=0, tiled=True),
        lax.all_gather(shards[10], ("seq", "fsdp"), axis=0, tiled=True),
        lax.all_gather(shards[11], ("seq", "fsdp"), axis=0, tiled=True),
        lax.all_gather(shards[12], ("seq", "fsdp"), axis=0, tiled=True),
    )


def local(
    inputs,
    segment_ids,
    cotangent,
    norm_mixer,
    in_proj,
    conv_weight,
    conv_bias,
    state_proj,
    step_proj,
    step_bias,
    decay_log,
    skip_gain,
    mixer_out,
    norm_ffn_one,
    gate_up_one,
    down_one,
    norm_attn,
    qkv_proj,
    attn_out,
    norm_ffn_two,
    gate_up_two,
    down_two,
):
    tokens = inputs.shape[1]
    seq_len = min(SEQ_MAX, tokens * lax.axis_size("seq"))
    positions = lax.axis_index("seq") * tokens + jnp.arange(tokens, dtype=jnp.int32)
    seg_float = segment_ids[0].astype(jnp.float32)
    layer_in = inputs[0].astype(jnp.float32)
    shards = (
        norm_mixer,
        in_proj,
        conv_weight,
        conv_bias,
        state_proj,
        step_proj,
        step_bias,
        decay_log,
        skip_gain,
        mixer_out,
        norm_ffn_one,
        gate_up_one,
        down_one,
    )
    lower_full = fetch_lower(shards)
    after_mixer, mixer_kept = mixer_forward(
        layer_in, lower_full[:10], seg_float, positions, seq_len
    )
    after_ffn, ffn_one_kept = feed_forward(
        after_mixer, lower_full[10], lower_full[11], lower_full[12]
    )
    upper_full = (
        lax.all_gather(norm_attn, ("seq", "fsdp"), axis=0, tiled=True),
        lax.all_gather(qkv_proj, ("seq", "fsdp"), axis=0, tiled=True),
        lax.all_gather(attn_out, ("seq", "fsdp"), axis=0, tiled=True),
        lax.all_gather(norm_ffn_two, ("seq", "fsdp"), axis=0, tiled=True),
        lax.all_gather(gate_up_two, ("seq", "fsdp"), axis=0, tiled=True),
        lax.all_gather(down_two, ("seq", "fsdp"), axis=0, tiled=True),
    )
    after_attn, attn_kept = attention_forward(
        after_ffn, upper_full[:3], seg_float, positions, seq_len
    )
    final_out, ffn_two_kept = feed_forward(after_attn, upper_full[3], upper_full[4], upper_full[5])
    grad_now = cotangent[0].astype(jnp.float32)
    grad_now, grad_norm_four, grad_gate_four, grad_down_four = feed_back(
        grad_now, after_attn, upper_full[3], upper_full[4], upper_full[5], ffn_two_kept
    )
    grad_now, grad_norm_three, grad_qkv_all, grad_out_attn = attention_back(
        grad_now, after_ffn, upper_full[:3], attn_kept
    )
    upper_grads = (
        lax.psum_scatter(grad_norm_three, ("seq", "fsdp"), scatter_dimension=0, tiled=True),
        lax.psum_scatter(grad_qkv_all, ("seq", "fsdp"), scatter_dimension=0, tiled=True),
        lax.psum_scatter(grad_out_attn, ("seq", "fsdp"), scatter_dimension=0, tiled=True),
        lax.psum_scatter(grad_norm_four, ("seq", "fsdp"), scatter_dimension=0, tiled=True),
        lax.psum_scatter(grad_gate_four, ("seq", "fsdp"), scatter_dimension=0, tiled=True),
        lax.psum_scatter(grad_down_four, ("seq", "fsdp"), scatter_dimension=0, tiled=True),
    )
    lower_back = fetch_lower(shards)
    grad_now, grad_norm_second, grad_gate_second, grad_down_second = feed_back(
        grad_now, after_mixer, lower_back[10], lower_back[11], lower_back[12], ffn_one_kept
    )
    grad_now, mixer_grads = mixer_back(grad_now, layer_in, lower_back[:10], mixer_kept)
    lower_grads = (
        lax.psum_scatter(mixer_grads[0], ("seq", "fsdp"), scatter_dimension=0, tiled=True),
        lax.psum_scatter(mixer_grads[1], ("seq", "fsdp"), scatter_dimension=0, tiled=True),
        lax.psum_scatter(mixer_grads[2], ("seq", "fsdp"), scatter_dimension=1, tiled=True),
        lax.psum_scatter(mixer_grads[3], ("seq", "fsdp"), scatter_dimension=0, tiled=True),
        lax.psum_scatter(mixer_grads[4], ("seq", "fsdp"), scatter_dimension=0, tiled=True),
        lax.psum_scatter(mixer_grads[5], ("seq", "fsdp"), scatter_dimension=1, tiled=True),
        lax.psum_scatter(mixer_grads[6], ("seq", "fsdp"), scatter_dimension=0, tiled=True),
        lax.psum_scatter(mixer_grads[7], ("seq", "fsdp"), scatter_dimension=0, tiled=True),
        lax.psum_scatter(mixer_grads[8], ("seq", "fsdp"), scatter_dimension=0, tiled=True),
        lax.psum_scatter(mixer_grads[9], ("seq", "fsdp"), scatter_dimension=0, tiled=True),
        lax.psum_scatter(grad_norm_second, ("seq", "fsdp"), scatter_dimension=0, tiled=True),
        lax.psum_scatter(grad_gate_second, ("seq", "fsdp"), scatter_dimension=0, tiled=True),
        lax.psum_scatter(grad_down_second, ("seq", "fsdp"), scatter_dimension=0, tiled=True),
    )
    return (
        (final_out.astype(jnp.bfloat16)[None], grad_now[None])
        + tuple(lower_grads)
        + tuple(upper_grads)
    )


def solution(mesh):
    placed = (
        P("fsdp", "seq", None),
        P("fsdp", "seq"),
        P("fsdp", "seq", None),
        P(("seq", "fsdp")),
        P(("seq", "fsdp"), None),
        P(None, ("seq", "fsdp")),
        P(("seq", "fsdp")),
        P(("seq", "fsdp"), None),
        P(None, ("seq", "fsdp")),
        P(("seq", "fsdp")),
        P(("seq", "fsdp"), None),
        P(("seq", "fsdp")),
        P(("seq", "fsdp"), None),
        P(("seq", "fsdp")),
        P(("seq", "fsdp"), None),
        P(("seq", "fsdp"), None),
        P(("seq", "fsdp")),
        P(("seq", "fsdp"), None),
        P(("seq", "fsdp"), None),
        P(("seq", "fsdp")),
        P(("seq", "fsdp"), None),
        P(("seq", "fsdp"), None),
    )
    return jax.shard_map(
        local,
        mesh=mesh,
        in_specs=placed,
        out_specs=(
            P("fsdp", "seq", None),
            P("fsdp", "seq", None),
            P(("seq", "fsdp")),
            P(("seq", "fsdp"), None),
            P(None, ("seq", "fsdp")),
            P(("seq", "fsdp")),
            P(("seq", "fsdp"), None),
            P(None, ("seq", "fsdp")),
            P(("seq", "fsdp")),
            P(("seq", "fsdp"), None),
            P(("seq", "fsdp")),
            P(("seq", "fsdp"), None),
            P(("seq", "fsdp")),
            P(("seq", "fsdp"), None),
            P(("seq", "fsdp"), None),
            P(("seq", "fsdp")),
            P(("seq", "fsdp"), None),
            P(("seq", "fsdp"), None),
            P(("seq", "fsdp")),
            P(("seq", "fsdp"), None),
            P(("seq", "fsdp"), None),
        ),
        check_vma=False,
    )
```

profile of v0, /device:TPU:1, one launch (start us, length us, event | category | flops | bytes accessed | tf_op | source)
XLA Modules:
  0.0 6931.3 jit_solution(12323909454501965571)
XLA Ops:
  247.0 422.3 %while.213 = (s32[]{:T(128)}, f32[3072,16]{0,1:T(8,128)S(1)}, f32[4,32,3072]{2,1,0:T(8,128)}, f32[4,32,3072]{2,1,0:T(8,128)}, f32[4,32,3072]{2,1,0:T(8,128)S(1)}...) while((s32[]{:T(128)}, f32[3072,16]{0,1:T(8,128)S(1)}, ...), condition=%wide.region_4.5_spmd, body=%wide.region_1.4_spmd.sunk | while | flops 838660 | bytes 3302730 | solution.py:143
  248.7 102.0 %while.221 = (s32[]{:T(128)}, f32[3072,16]{0,1:T(8,128)S(1)}, f32[32,3072]{1,0:T(8,128)}, f32[32,3072]{1,0:T(8,128)S(1)}, f32[3072,16]{0,1:T(8,128)S(1)}, /*inde...) while((s32[]{:T(128)}, f32[3072,16]{0,1:T(8,128)S(1)}, ...), condition=%wide.region_3.3_spmd, body=%wide.region_2.2_spmd.sunk | while | flops 838658 | bytes 934741 | solution.py:135
  354.3 102.0 %while.221 = (s32[]{:T(128)}, f32[3072,16]{0,1:T(8,128)S(1)}, f32[32,3072]{1,0:T(8,128)}, f32[32,3072]{1,0:T(8,128)S(1)}, f32[3072,16]{0,1:T(8,128)S(1)}, /*inde...) while((s32[]{:T(128)}, f32[3072,16]{0,1:T(8,128)S(1)}, ...), condition=%wide.region_3.3_spmd, body=%wide.region_2.2_spmd.sunk | while | flops 838658 | bytes 934741 | solution.py:135
  459.8 102.0 %while.221 = (s32[]{:T(128)}, f32[3072,16]{0,1:T(8,128)S(1)}, f32[32,3072]{1,0:T(8,128)}, f32[32,3072]{1,0:T(8,128)S(1)}, f32[3072,16]{0,1:T(8,128)S(1)}, /*inde...) while((s32[]{:T(128)}, f32[3072,16]{0,1:T(8,128)S(1)}, ...), condition=%wide.region_3.3_spmd, body=%wide.region_2.2_spmd.sunk | while | flops 838658 | bytes 934741 | solution.py:135
  565.4 102.0 %while.221 = (s32[]{:T(128)}, f32[3072,16]{0,1:T(8,128)S(1)}, f32[32,3072]{1,0:T(8,128)}, f32[32,3072]{1,0:T(8,128)S(1)}, f32[3072,16]{0,1:T(8,128)S(1)}, /*inde...) while((s32[]{:T(128)}, f32[3072,16]{0,1:T(8,128)S(1)}, ...), condition=%wide.region_3.3_spmd, body=%wide.region_2.2_spmd.sunk | while | flops 838658 | bytes 934741 | solution.py:135
  748.1 62.4 all-gather.19.cloned.1.call-done
  816.1 150.5 %all-gather.21.cloned.1.call-done = bf16[1536,8192]{1,0:T(8,128)(2,1)} async-done(((bf16[48,8192]{1,0:T(8,128)(2,1)}), bf16[1536,8192]{1,0:T(8,128)(2,1)}) %all-gather.21.cloned.1.call-update) | async-done | bytes 25165840 | tf_op jit(solution)/shard_map/all_gather | solution.py:601
  979.3 84.2 %all-gather.23.cloned.1.call-done = bf16[4096,1536]{1,0:T(8,128)(2,1)} async-done(((bf16[128,1536]{1,0:T(8,128)(2,1)}), bf16[4096,1536]{1,0:T(8,128)(2,1)}) %all-gather.23.cloned.1.call-update) | async-done | bytes 12582928 | tf_op jit(solution)/shard_map/all_gather | solution.py:602
  1070.0 97.9 %all-gather.25.cloned.1.call-done = bf16[1536,4608]{1,0:T(8,128)(2,1)} async-done(((bf16[48,4608]{1,0:T(8,128)(2,1)}), bf16[1536,4608]{1,0:T(8,128)(2,1)}) %all-gather.25.cloned.1.call-update) | async-done | bytes 14155792 | tf_op jit(solution)/shard_map/all_gather | solution.py:659
  1598.6 117.8 %all-gather.31.cloned.1.call-done = bf16[4096,1536]{1,0:T(8,128)(2,1)} async-done(((bf16[128,1536]{1,0:T(8,128)(2,1)}), bf16[4096,1536]{1,0:T(8,128)(2,1)}) %all-gather.31.cloned.1.call-update) | async-done | bytes 12582928 | tf_op jit(solution)/shard_map/all_gather | solution.py:663
  1808.2 112.8 %collective-permute-done.76 = bf16[128,12,128]{0,2,1:T(8,128)(2,1)S(1)} collective-permute-done((bf16[128,12,128]{0,2,1:T(8,128)(2,1)S(1)}, bf16[128,12,128]{0,2,1:T(8,128)(2,1)S(1)}, u32[]{:S(2)}, u32[]{:S(2)}) %collective-permute-start.76) | collective-permute-done | bytes 393248 | tf_op jit(solution)/shard_map/ppermute | solution.py:22
  2220.0 189.6 %while.217 = (s32[]{:T(128)}, f32[3072,16]{0,1:T(8,128)S(1)}, f32[4,3072,16]{1,2,0:T(8,128)}, f32[4,32,3072]{2,1,0:T(8,128)}, f32[4,32,3072]{2,1,0:T(8,128)S(1)}...) while((s32[]{:T(128)}, f32[3072,16]{0,1:T(8,128)S(1)}, ...), condition=%wide.region_23.24_spmd, body=%wide.region_20.23_spmd.sunk | while | flops 248836 | bytes 2671370 | solution.py:143
  2431.9 1684.2 %while.220 = (s32[]{:T(128)}, f32[3072,16]{0,1:T(8,128)}, f32[3072,16]{0,1:T(8,128)S(1)}, f32[4,32,3072]{2,1,0:T(8,128)}, f32[4,32,3072]{2,1,0:T(8,128)}, /*inde...) while((s32[]{:T(128)}, f32[3072,16]{0,1:T(8,128)}, ...), condition=%wide.region_32.33_spmd.clone, body=%wide.region_24.32_spmd.clone.sunk | while | flops 1779194 | bytes 12872911 | solution.py:143
  2437.2 133.2 %while.223 = (s32[]{:T(128)}, f32[3072,16]{0,1:T(8,128)S(1)}, f32[32,3072,1]{1,2,0:T(1,128)}, f32[32,3072,16]{1,2,0:T(8,128)}, f32[32,3072,16]{1,2,0:T(8,128)}, ...) while((s32[]{:T(128)}, f32[3072,16]{0,1:T(8,128)S(1)}, ...), condition=%wide.region_26.26_spmd, body=%wide.region_25.25_spmd.sunk | while | flops 350210 | bytes 1550709 | solution.py:135
  2571.4 278.2 %while.224 = (s32[]{:T(128)}, f32[3072,16]{0,1:T(8,128)S(1)}, f32[3072,16]{0,1:T(8,128)S(1)}, f32[32,3072]{1,0:T(8,128)S(1)}, f32[32,3072]{1,0:T(8,128)S(1)}, /*...) while((s32[]{:T(128)}, f32[3072,16]{0,1:T(8,128)S(1)}, ...), condition=%wide.region_31.31_spmd.clone, body=%wide.region_27.30_spmd.clone.sunk | while | flops 1330164 | bytes 2435011 | solution.py:135
  2857.6 133.2 %while.223 = (s32[]{:T(128)}, f32[3072,16]{0,1:T(8,128)S(1)}, f32[32,3072,1]{1,2,0:T(1,128)}, f32[32,3072,16]{1,2,0:T(8,128)}, f32[32,3072,16]{1,2,0:T(8,128)}, ...) while((s32[]{:T(128)}, f32[3072,16]{0,1:T(8,128)S(1)}, ...), condition=%wide.region_26.26_spmd, body=%wide.region_25.25_spmd.sunk | while | flops 350210 | bytes 1550709 | solution.py:135
  2991.7 278.2 %while.224 = (s32[]{:T(128)}, f32[3072,16]{0,1:T(8,128)S(1)}, f32[3072,16]{0,1:T(8,128)S(1)}, f32[32,3072]{1,0:T(8,128)S(1)}, f32[32,3072]{1,0:T(8,128)S(1)}, /*...) while((s32[]{:T(128)}, f32[3072,16]{0,1:T(8,128)S(1)}, ...), condition=%wide.region_31.31_spmd.clone, body=%wide.region_27.30_spmd.clone.sunk | while | flops 1330164 | bytes 2435011 | solution.py:135
  3278.8 133.2 %while.223 = (s32[]{:T(128)}, f32[3072,16]{0,1:T(8,128)S(1)}, f32[32,3072,1]{1,2,0:T(1,128)}, f32[32,3072,16]{1,2,0:T(8,128)}, f32[32,3072,16]{1,2,0:T(8,128)}, ...) while((s32[]{:T(128)}, f32[3072,16]{0,1:T(8,128)S(1)}, ...), condition=%wide.region_26.26_spmd, body=%wide.region_25.25_spmd.sunk | while | flops 350210 | bytes 1550709 | solution.py:135
  3412.9 278.2 %while.224 = (s32[]{:T(128)}, f32[3072,16]{0,1:T(8,128)S(1)}, f32[3072,16]{0,1:T(8,128)S(1)}, f32[32,3072]{1,0:T(8,128)S(1)}, f32[32,3072]{1,0:T(8,128)S(1)}, /*...) while((s32[]{:T(128)}, f32[3072,16]{0,1:T(8,128)S(1)}, ...), condition=%wide.region_31.31_spmd.clone, body=%wide.region_27.30_spmd.clone.sunk | while | flops 1330164 | bytes 2435011 | solution.py:135
  3700.0 133.2 %while.223 = (s32[]{:T(128)}, f32[3072,16]{0,1:T(8,128)S(1)}, f32[32,3072,1]{1,2,0:T(1,128)}, f32[32,3072,16]{1,2,0:T(8,128)}, f32[32,3072,16]{1,2,0:T(8,128)}, ...) while((s32[]{:T(128)}, f32[3072,16]{0,1:T(8,128)S(1)}, ...), condition=%wide.region_26.26_spmd, body=%wide.region_25.25_spmd.sunk | while | flops 350210 | bytes 1550709 | solution.py:135
  3834.1 278.2 %while.224 = (s32[]{:T(128)}, f32[3072,16]{0,1:T(8,128)S(1)}, f32[3072,16]{0,1:T(8,128)S(1)}, f32[32,3072]{1,0:T(8,128)S(1)}, f32[32,3072]{1,0:T(8,128)S(1)}, /*...) while((s32[]{:T(128)}, f32[3072,16]{0,1:T(8,128)S(1)}, ...), condition=%wide.region_31.31_spmd.clone, body=%wide.region_27.30_spmd.clone.sunk | while | flops 1330164 | bytes 2435011 | solution.py:135
  4287.0 67.8 all-reduce.28
  4364.3 94.8 %reduce-scatter.39.cloned.1.call-done = f32[96,96]{1,0:T(8,128)} async-done(((f32[3072,96]{1,0:T(8,128)}), f32[96,96]{1,0:T(8,128)}) %reduce-scatter.39.cloned.1.call-update) | async-done | bytes 36880
  4460.6 100.2 %reduce-scatter.21.cloned.1.call-done = f32[96,128]{1,0:T(8,128)} async-done(((f32[3072,128]{1,0:T(8,128)}), f32[96,128]{1,0:T(8,128)}) %reduce-scatter.21.cloned.1.call-update) | async-done | bytes 49168 | tf_op jit(solution)/shard_map/reduce_scatter | solution.py:694
  4560.8 140.9 %reduce-scatter.31.cloned.1.call-done = f32[48,1536]{1,0:T(8,128)} async-done(((f32[1536,1536]{1,0:T(8,128)}), f32[48,1536]{1,0:T(8,128)}) %reduce-scatter.31.cloned.1.call-update) | async-done | bytes 294928 | tf_op jit(solution)/shard_map/reduce_scatter | solution.py:679
  4701.7 214.3 %reduce-scatter.23.cloned.1.call-done = f32[96,1536]{1,0:T(8,128)} async-done(((f32[3072,1536]{1,0:T(8,128)}), f32[96,1536]{1,0:T(8,128)}) %reduce-scatter.23.cloned.1.call-update) | async-done | bytes 589840 | tf_op jit(solution)/shard_map/reduce_scatter | solution.py:699
  4916.0 253.4 %reduce-scatter.35.cloned.1.call-done = f32[128,1536]{1,0:T(8,128)} async-done(((f32[4096,1536]{1,0:T(8,128)}), f32[128,1536]{1,0:T(8,128)}) %reduce-scatter.35.cloned.1.call-update) | async-done | bytes 786448 | tf_op jit(solution)/shard_map/reduce_scatter | solution.py:682
  5169.4 252.0 %reduce-scatter.27.cloned.1.call-done = f32[128,1536]{1,0:T(8,128)} async-done(((f32[4096,1536]{1,0:T(8,128)}), f32[128,1536]{1,0:T(8,128)}) %reduce-scatter.27.cloned.1.call-update) | async-done | bytes 786448 | tf_op jit(solution)/shard_map/reduce_scatter | solution.py:702
  5421.4 271.2 %reduce-scatter.29.cloned.1.call-done = f32[48,4608]{1,0:T(8,128)} async-done(((f32[1536,4608]{1,0:T(8,128)}), f32[48,4608]{1,0:T(8,128)}) %reduce-scatter.29.cloned.1.call-update) | async-done | bytes 884752 | tf_op jit(solution)/shard_map/reduce_scatter | solution.py:678
  5692.7 355.6 %reduce-scatter.19.cloned.1.call-done = f32[48,6144]{1,0:T(8,128)} async-done(((f32[1536,6144]{1,0:T(8,128)}), f32[48,6144]{1,0:T(8,128)}) %reduce-scatter.19.cloned.1.call-update) | async-done | bytes 1179664 | tf_op jit(solution)/shard_map/reduce_scatter | solution.py:691
  6048.3 438.5 %reduce-scatter.33.cloned.1.call-done = f32[48,8192]{1,0:T(8,128)} async-done(((f32[1536,8192]{1,0:T(8,128)}), f32[48,8192]{1,0:T(8,128)}) %reduce-scatter.33.cloned.1.call-update) | async-done | bytes 1572880 | tf_op jit(solution)/shard_map/reduce_scatter | solution.py:681
  6486.7 437.5 %reduce-scatter.25.cloned.1.call-done = f32[48,8192]{1,0:T(8,128)} async-done(((f32[1536,8192]{1,0:T(8,128)}), f32[48,8192]{1,0:T(8,128)}) %reduce-scatter.25.cloned.1.call-update) | async-done | bytes 1572880 | tf_op jit(solution)/shard_map/reduce_scatter | solution.py:701
  (5033 shorter events, 3838.7 us)
Async XLA Ops:
  7.2 217.3 %all-gather.17.cloned.1.call-start = ((), (), s32[]{:S(2)}) async-start(), calls=%async_computation.12 | async-start | bytes 19464192 | tf_op jit(solution)/shard_map/all_gather | solution.py:591
  8.0 701.3 %all-gather.33.cloned.1.call-start = ((), (), s32[]{:S(2)}) async-start(), calls=%async_computation.29 | async-start | bytes 1671168 | tf_op jit(solution)/shard_map/all_gather | solution.py:28
  8.7 214.8 %collective-permute-start.1 = (bf16[3]{0:T(256)(128)(2,1)S(1)}, bf16[3]{0:T(256)(128)(2,1)S(1)}, u32[]{:S(2)}, u32[]{:S(2)}) collective-permute-start(bf16[3]{0:T(256)(128)(2,1)S(1)} %slice_bitcast_fusion), channel_id=1, source_target_pairs={{0,2},{2,4},{4,6},{6,8},{8,10},{10,12},{12,14},{14,16},{16,18},{18... | collective-permute-start | bytes 26 | tf_op jit(solution)/shard_map/ppermute | solution.py:22
  245.3 480.3 %all-gather.35.cloned.1.call-start = ((), (), s32[]{:S(2)}) async-start(), calls=%async_computation.30 | async-start | bytes 1671168 | tf_op jit(solution)/shard_map/all_gather | solution.py:28
  669.9 140.6 %all-gather.19.cloned.1.call-start = ((), (), s32[]{:S(2)}) async-start(), calls=%async_computation.13 | async-start | bytes 9732096 | tf_op jit(solution)/shard_map/all_gather | solution.py:599
  670.5 296.0 %all-gather.21.cloned.1.call-start = ((), (), s32[]{:S(2)}) async-start(), calls=%async_computation.14 | async-start | bytes 25952256 | tf_op jit(solution)/shard_map/all_gather | solution.py:601
  671.1 392.3 %all-gather.23.cloned.1.call-start = ((), (), s32[]{:S(2)}) async-start(), calls=%async_computation.15 | async-start | bytes 12976128 | tf_op jit(solution)/shard_map/all_gather | solution.py:602
  671.7 496.2 %all-gather.25.cloned.1.call-start = ((), (), s32[]{:S(2)}) async-start(), calls=%async_computation.16 | async-start | bytes 14598144 | tf_op jit(solution)/shard_map/all_gather | solution.py:659
  672.4 891.8 %all-gather.27.cloned.1.call-start = ((), (), s32[]{:S(2)}) async-start(), calls=%async_computation.17 | async-start | bytes 4866048 | tf_op jit(solution)/shard_map/all_gather | solution.py:660
  673.2 911.8 %all-gather.29.cloned.1.call-start = ((), (), s32[]{:S(2)}) async-start(), calls=%async_computation.18 | async-start | bytes 25952256 | tf_op jit(solution)/shard_map/all_gather | solution.py:662
  673.9 1042.6 %all-gather.31.cloned.1.call-start = ((), (), s32[]{:S(2)}) async-start(), calls=%async_computation.19 | async-start | bytes 12976128 | tf_op jit(solution)/shard_map/all_gather | solution.py:663
  674.5 1735.8 %all-gather.37.cloned.1.call-start = ((), (), s32[]{:S(2)}) async-start(), calls=%async_computation.31 | async-start | bytes 1671168 | tf_op jit(solution)/shard_map/all_gather | solution.py:50
  1406.5 97.6 %collective-permute-start.42 = (bf16[128,12,128]{2,0,1:T(8,128)(2,1)S(1)}, bf16[128,12,128]{2,0,1:T(8,128)(2,1)S(1)}, u32[]{:S(2)}, u32[]{:S(2)}) collective-permute-start(bf16[128,12,128]{2,0,1:T(8,128)(2,1)S(1)} %pad_maximum_fusion.8), channel_id=1, source_target_pairs={{0,16},{2,18},{4,20},{6,22},{8,24},{10,26},{12,28},{14,30},{1,17},... | collective-permute-start | bytes 1179656 | tf_op jit(solution)/shard_map/ppermute | solution.py:22
  1411.3 94.2 %collective-permute-start.43 = (bf16[128,12,128]{2,0,1:T(8,128)(2,1)S(1)}, bf16[128,12,128]{2,0,1:T(8,128)(2,1)S(1)}, u32[]{:S(2)}, u32[]{:S(2)}) collective-permute-start(bf16[128,12,128]{2,0,1:T(8,128)(2,1)S(1)} %pad_maximum_fusion.8), channel_id=1, source_target_pairs={{0,14},{2,16},{4,18},{6,20},{8,22},{10,24},{12,26},{14,28},{16,30}... | collective-permute-start | bytes 1179656 | tf_op jit(solution)/shard_map/ppermute | solution.py:22
  1802.3 118.7 %collective-permute-start.76 = (bf16[128,12,128]{0,2,1:T(8,128)(2,1)S(1)}, bf16[128,12,128]{0,2,1:T(8,128)(2,1)S(1)}, u32[]{:S(2)}, u32[]{:S(2)}) collective-permute-start(bf16[128,12,128]{0,2,1:T(8,128)(2,1)S(1)} %copy-done.93), channel_id=1, source_target_pairs={{22,0},{24,2},{26,4},{28,6},{30,8},{23,1},{25,3},{27,5},{29,7},{31... | collective-permute-start | bytes 1179656 | tf_op jit(solution)/shard_map/ppermute | solution.py:22
  1803.6 118.7 %collective-permute-start.65 = (bf16[128,12,128]{0,2,1:T(8,128)(2,1)S(1)}, bf16[128,12,128]{0,2,1:T(8,128)(2,1)S(1)}, u32[]{:S(2)}, u32[]{:S(2)}) collective-permute-start(bf16[128,12,128]{0,2,1:T(8,128)(2,1)S(1)} %get-tuple-element.1903), channel_id=1, source_target_pairs={} | collective-permute-start | bytes 1179656 | tf_op jit(solution)/shard_map/ppermute | solution.py:22
  1804.3 119.3 %collective-permute-start.64 = (bf16[128,12,128]{0,2,1:T(8,128)(2,1)S(1)}, bf16[128,12,128]{0,2,1:T(8,128)(2,1)S(1)}, u32[]{:S(2)}, u32[]{:S(2)}) collective-permute-start(bf16[128,12,128]{0,2,1:T(8,128)(2,1)S(1)} %get-tuple-element.1904), channel_id=1, source_target_pairs={{30,0},{31,1}} | collective-permute-start | bytes 1179656 | tf_op jit(solution)/shard_map/ppermute | solution.py:22
  1805.6 119.3 %collective-permute-start.63 = (bf16[128,12,128]{0,2,1:T(8,128)(2,1)S(1)}, bf16[128,12,128]{0,2,1:T(8,128)(2,1)S(1)}, u32[]{:S(2)}, u32[]{:S(2)}) collective-permute-start(bf16[128,12,128]{0,2,1:T(8,128)(2,1)S(1)} %get-tuple-element.1905), channel_id=1, source_target_pairs={{28,0},{30,2},{29,1},{31,3}} | collective-permute-start | bytes 1179656 | tf_op jit(solution)/shard_map/ppermute | solution.py:22
  1806.9 119.3 %collective-permute-start.62 = (bf16[128,12,128]{0,2,1:T(8,128)(2,1)S(1)}, bf16[128,12,128]{0,2,1:T(8,128)(2,1)S(1)}, u32[]{:S(2)}, u32[]{:S(2)}) collective-permute-start(bf16[128,12,128]{0,2,1:T(8,128)(2,1)S(1)} %get-tuple-element.1906), channel_id=1, source_target_pairs={{26,0},{28,2},{30,4},{27,1},{29,3},{31,5}} | collective-permute-start | bytes 1179656 | tf_op jit(solution)/shard_map/ppermute | solution.py:22
  2017.8 95.0 %collective-permute-start.73 = (bf16[128,12,128]{0,2,1:T(8,128)(2,1)S(1)}, bf16[128,12,128]{0,2,1:T(8,128)(2,1)S(1)}, u32[]{:S(2)}, u32[]{:S(2)}) collective-permute-start(bf16[128,12,128]{0,2,1:T(8,128)(2,1)S(1)} %copy-done.90), channel_id=1, source_target_pairs={{16,0},{18,2},{20,4},{22,6},{24,8},{26,10},{28,12},{30,14},{17,1},... | collective-permute-start | bytes 1179656 | tf_op jit(solution)/shard_map/ppermute | solution.py:22
  2220.0 2141.4 %reduce-scatter.37.cloned.1.call-start = ((), (), s32[]{:S(2)}) async-start(), calls=%async_computation.32 | async-start | bytes 1622016
  4133.1 229.8 %reduce-scatter.41.cloned.1.call-start = ((), (), s32[]{:S(2)}) async-start(), calls=%async_computation.34 | async-start | bytes 1622016
  4134.9 324.2 %reduce-scatter.39.cloned.1.call-start = ((), (), s32[]{:S(2)}) async-start(), calls=%async_computation.33 | async-start | bytes 1622016
  4136.6 424.2 %reduce-scatter.21.cloned.1.call-start = ((), (), s32[]{:S(2)}) async-start(), calls=%async_computation.21 | async-start | bytes 1622016 | tf_op jit(solution)/shard_map/reduce_scatter | solution.py:694
  4138.3 563.5 %reduce-scatter.31.cloned.1.call-start = ((), (), s32[]{:S(2)}) async-start(), calls=%async_computation.26 | async-start | bytes 9732096 | tf_op jit(solution)/shard_map/reduce_scatter | solution.py:679
  4143.4 772.6 %reduce-scatter.23.cloned.1.call-start = ((), (), s32[]{:S(2)}) async-start(), calls=%async_computation.22 | async-start | bytes 19464192 | tf_op jit(solution)/shard_map/reduce_scatter | solution.py:699
  4152.6 1016.8 %reduce-scatter.35.cloned.1.call-start = ((), (), s32[]{:S(2)}) async-start(), calls=%async_computation.28 | async-start | bytes 25952256 | tf_op jit(solution)/shard_map/reduce_scatter | solution.py:682
  4164.1 1257.4 %reduce-scatter.27.cloned.1.call-start = ((), (), s32[]{:S(2)}) async-start(), calls=%async_computation.24 | async-start | bytes 25952256 | tf_op jit(solution)/shard_map/reduce_scatter | solution.py:702
  4176.2 1516.5 %reduce-scatter.29.cloned.1.call-start = ((), (), s32[]{:S(2)}) async-start(), calls=%async_computation.25 | async-start | bytes 29196288 | tf_op jit(solution)/shard_map/reduce_scatter | solution.py:678
  4190.8 1857.5 %reduce-scatter.19.cloned.1.call-start = ((), (), s32[]{:S(2)}) async-start(), calls=%async_computation.20 | async-start | bytes 38928384 | tf_op jit(solution)/shard_map/reduce_scatter | solution.py:691
  4222.2 2264.5 %reduce-scatter.33.cloned.1.call-start = ((), (), s32[]{:S(2)}) async-start(), calls=%async_computation.27 | async-start | bytes 51904512 | tf_op jit(solution)/shard_map/reduce_scatter | solution.py:681
  4245.4 2678.9 %reduce-scatter.25.cloned.1.call-start = ((), (), s32[]{:S(2)}) async-start(), calls=%async_computation.23 | async-start | bytes 51904512 | tf_op jit(solution)/shard_map/reduce_scatter | solution.py:701
  (240 other events, 13001.8 us)
Sparse Core Ops, SparseCore 0:
  11.0 128.9 all-gather.16
  245.4 55.3 all-gather.32
  670.1 55.4 all-gather.34
  728.3 82.2 all-gather.18
  813.3 153.2 all-gather.20
  969.3 94.1 all-gather.22
  1066.3 101.4 all-gather.24
  1170.7 157.9 all-gather.26
  1331.6 253.3 all-gather.28
  1587.7 128.7 all-gather.30
  2220.1 92.0 all-gather.36
  4133.2 123.3 reduce-scatter.36
  4261.9 96.0 reduce-scatter.40
  4363.0 96.0 reduce-scatter.38
  4464.8 96.0 reduce-scatter.20
  4567.2 134.5 reduce-scatter.30
  4709.7 206.2 reduce-scatter.22
  4924.0 245.3 reduce-scatter.34
  5176.4 245.0 reduce-scatter.26
  5429.4 263.2 reduce-scatter.28
  5700.8 347.3 reduce-scatter.18
  6055.2 431.4 reduce-scatter.32
  6493.8 430.4 reduce-scatter.24
where the time goes:
time: 6980 us; the launch traced here: 6930 us
  waiting for transfers between devices  3480 us (50%)
  local copies, waits for them, and re-layouts  1290 us (18%)
  other arithmetic  990 us (14%)
  matrix products  517 us (7%)
  starting transfers between devices  344 us (5%)
  blocking collectives  272 us (4%)
    dynamic_slice x1152, local copies, waits for them, and re-layouts, block_step(): return lax.scan(token_step, state_now, block_items)  696 us
    reduce_scatter x1, waiting for transfers between devices, local(): lax.psum_scatter(grad_gate_four, ('seq', 'fsdp'), scatter_dimension=0, ti...  438 us
    reduce_scatter x1, waiting for transfers between devices, local(): lax.psum_scatter(grad_gate_second, ('seq', 'fsdp'), scatter_dimension=0,...  438 us
    ppermute x83, waiting for transfers between devices, shifted(): return lax.ppermute(x, axis, pairs)  373 us
    dynamic_update_slice x768, local copies, waits for them, and re-layouts, block_step(): return lax.scan(token_step, state_now, block_items)  359 us
    reduce_scatter x1, waiting for transfers between devices, local(): lax.psum_scatter(mixer_grads[1], ('seq', 'fsdp'), scatter_dimension=0, ti...  356 us
    ppermute x83, starting transfers between devices, shifted(): return lax.ppermute(x, axis, pairs)  343 us
    dynamic_update_slice x256, other arithmetic, block_step(): return lax.scan(token_step, state_now, block_items)  292 us

commit v1 on v0

v1 whole, which is shorter than its diff:
```python
import functools
import math

import jax
import jax.numpy as jnp
from jax import lax
from jax.experimental import pallas as pl
from jax.experimental.pallas import tpu as pltpu
from jax.sharding import Mesh
from jax.sharding import PartitionSpec as P

W = 4
H = 12
HD = 128
WIN = 2048
SEQ_MAX = 8192
EPS = 1e-05
NEG = -1e30
BIG = 1e30
LOG2E = 1.4426950408889634
BF = jnp.bfloat16
F32 = jnp.float32
MESH = pl.DeviceIdType.MESH
HALO = 16
SUB = 64
MIB = 1 << 20


def vmem():
    return pl.BlockSpec(memory_space=pltpu.VMEM)


def hbm():
    return pl.BlockSpec(memory_space=pl.ANY)


def smem():
    return pl.BlockSpec(memory_space=pltpu.SMEM)


def here():
    return lax.axis_index("t"), lax.axis_index("p"), lax.axis_index("c")


def greet(device):
    pl.semaphore_signal(
        pltpu.get_barrier_semaphore(), inc=1, device_id=device, device_id_type=MESH
    )


def arrive(count):
    pl.semaphore_wait(pltpu.get_barrier_semaphore(), count)


def arrive_some(count):
    @pl.when(count > 0)
    def _():
        arrive(count)


def remote(src, dst, send, recv, device):
    return pltpu.make_async_remote_copy(
        src_ref=src,
        dst_ref=dst,
        send_sem=send,
        recv_sem=recv,
        device_id=device,
        device_id_type=MESH,
    )


def flip(p, d):
    return lax.bitwise_xor(p, d)


def dma(*shape):
    return pltpu.SemaphoreType.DMA(shape)


def talk(cid, limit=40):
    return pltpu.CompilerParams(
        collective_id=cid, has_side_effects=True, vmem_limit_bytes=limit * MIB
    )


def alone(limit=56):
    return pltpu.CompilerParams(vmem_limit_bytes=limit * MIB)


def out(shape, dtype=F32):
    return jax.ShapeDtypeStruct(shape, dtype)


def unit(x):
    return x * lax.rsqrt(jnp.mean(x * x, axis=-1, keepdims=True) + EPS)


def start_body(
    T, x, seg, par, win, nh, seg_out, par_out, win_out, nbuf, zbuf,
    s_n, r_n, s_h, r_h, s_s, r_s, s_p, r_p, s_w, r_w, s_l,
):
    t, p, c = here()
    B = x.shape[0]
    count = 0
    for dt in range(T):
        tt = lax.rem(t + dt, T)
        for dp in range(W):
            pp = flip(p, dp)
            if dt or dp:
                greet((tt, pp, c))
                count += 1
            if dt == 0 or dp == 0:
                greet((tt, pp, 1 - c))
                count += 1
    nbuf[...] = unit(x[...].astype(F32)).astype(BF)
    zbuf[...] = jnp.zeros_like(zbuf)
    arrive(count)
    half = lax.div(p, 2)
    slot = lax.rem(p, 2) * 2 + c
    for q in range(W):
        mine = (p == q) & (half == c)

        @pl.when(jnp.logical_not(mine))
        def _():
            remote(win.at[q], win_out.at[slot], s_w.at[q], r_w.at[slot], (t, q, half)).start()

        @pl.when(mine)
        def _():
            pltpu.make_async_copy(win.at[q], win_out.at[slot], s_w.at[q]).start()

    rows = pl.ds(pl.multiple_of(HALO + p * B, HALO), B)
    copies = []
    for d in range(1, W):
        copies.append(remote(nbuf, nh.at[rows], s_n.at[d], r_n.at[d], (t, flip(p, d), c)))
    for dt in range(T):
        for dc in range(2):
            if dt or dc:
                copies.append(
                    remote(
                        par, par_out.at[t * 2 + c], s_p.at[dt, dc], r_p.at[dt, dc],
                        (lax.rem(t + dt, T), p, flip(c, dc)),
                    )
                )
    for dt in range(T):
        for dp in range(W):
            if dt or dp:
                copies.append(
                    remote(
                        seg, seg_out.at[t * W + p], s_s.at[dt, dp], r_s.at[dt, dp],
                        (lax.rem(t + dt, T), flip(p, dp), c),
                    )
                )
    for copy in copies:
        copy.start()
    last = (p == W - 1) & (t < T - 1)
    tail = nbuf.at[pl.ds(B - HALO, HALO)]
    head = nh.at[pl.ds(0, HALO)]

    def rim(q):
        return remote(tail, head, s_h.at[q], r_h, (lax.rem(t + 1, T), q, c))

    @pl.when(last)
    def _():
        for q in range(W):
            rim(q).start()

    local = [
        pltpu.make_async_copy(nbuf, nh.at[rows], s_l.at[0]),
        pltpu.make_async_copy(par, par_out.at[t * 2 + c], s_l.at[1]),
        pltpu.make_async_copy(seg, seg_out.at[t * W + p], s_l.at[2]),
    ]
    for copy in local:
        copy.start()

    @pl.when(t == 0)
    def _():
        clear = pltpu.make_async_copy(zbuf, head, s_l.at[3])
        clear.start()
        clear.wait()

    for copy in local:
        copy.wait()
    for copy in copies:
        copy.wait()

    @pl.when(last)
    def _():
        for q in range(W):
            rim(q).wait_send()

    @pl.when(t > 0)
    def _():
        rim(0).wait_recv()

    for q in range(W):
        mine = (p == q) & (half == c)

        @pl.when(jnp.logical_not(mine))
        def _():
            remote(win.at[q], win_out.at[slot], s_w.at[q], r_w.at[slot], (t, q, half)).wait_send()

        @pl.when(mine)
        def _():
            pltpu.make_async_copy(win.at[q], win_out.at[slot], s_w.at[q]).wait()

    for j in range(W):
        own = (half == c) & (slot == j)

        @pl.when(jnp.logical_not(own))
        def _():
            remote(win.at[0], win_out.at[j], s_w.at[0], r_w.at[j], (t, 0, half)).wait_recv()


def start_call(T, x, seg, par, win):
    B, D = x.shape
    return pl.pallas_call(
        functools.partial(start_body, T),
        out_shape=(
            out((HALO + W * B, D), BF),
            out((W * T,) + seg.shape, jnp.int32),
            out((2 * T,) + par.shape, BF),
            out(win.shape, BF),
        ),
        in_specs=[vmem(), hbm(), hbm(), hbm()],
        out_specs=(hbm(), hbm(), hbm(), hbm()),
        scratch_shapes=[
            pltpu.VMEM((B, D), BF),
            pltpu.VMEM((HALO, D), BF),
            dma(W), dma(W), dma(W), pltpu.SemaphoreType.DMA,
            dma(T, W), dma(T, W), dma(T, 2), dma(T, 2), dma(W), dma(W), dma(4),
        ],
        compiler_params=talk(0),
        name="start",
    )(x, seg, par, win)


def spread_body(n, back, *refs):
    srcs, dsts = refs[:n], refs[n : 2 * n]
    s_w, r_w = refs[2 * n :]
    t, p, c = here()
    half = lax.div(p, 2)
    pair = lax.rem(p, 2) * 2 + c
    both = half == c

    def there(q):
        if back:
            return (t, c * 2 + q // 2, jnp.int32(q % 2))
        return (t, jnp.int32(q), half)

    def comes(j):
        if back:
            return (t, jnp.int32(j), half)
        return (t, c * 2 + j // 2, jnp.int32(j % 2))

    slot = p if back else pair
    for q in range(W):
        to, source = there(q), comes(q)
        own = both & ((pair == q) if back else (p == q))
        from_me = both & ((p == q) if back else (pair == q))

        @pl.when(jnp.logical_not(from_me))
        def _():
            greet(source)

    arrive(W - both.astype(jnp.int32))
    for q in range(W):
        own = both & ((pair == q) if back else (p == q))
        for a in range(n):

            @pl.when(jnp.logical_not(own))
            def _():
                remote(
                    srcs[a].at[q], dsts[a].at[slot], s_w.at[a, q], r_w.at[a, slot], there(q)
                ).start()

            @pl.when(own)
            def _():
                pltpu.make_async_copy(srcs[a].at[q], dsts[a].at[slot], s_w.at[a, q]).start()

    for q in range(W):
        own = both & ((pair == q) if back else (p == q))
        from_me = both & ((p == q) if back else (pair == q))
        for a in range(n):

            @pl.when(jnp.logical_not(own))
            def _():
                remote(
                    srcs[a].at[q], dsts[a].at[slot], s_w.at[a, q], r_w.at[a, slot], there(q)
                ).wait_send()

            @pl.when(own)
            def _():
                pltpu.make_async_copy(srcs[a].at[q], dsts[a].at[slot], s_w.at[a, q]).wait()

            @pl.when(jnp.logical_not(from_me))
            def _():
                remote(
                    srcs[a].at[q], dsts[a].at[q], s_w.at[a, q], r_w.at[a, q], there(q)
                ).wait_recv()


def spread_call(cid, back, arrays):
    n = len(arrays)
    return pl.pallas_call(
        functools.partial(spread_body, n, back),
        out_shape=tuple(out(a.shape, a.dtype) for a in arrays),
        in_specs=[hbm()] * n,
        out_specs=(hbm(),) * n,
        scratch_shapes=[dma(n, W), dma(n, W)],
        compiler_params=talk(cid),
        name="spread%d" % cid,
    )(*arrays)


def plane_gather_body(x, o, ss, rs, ls):
    t, p, c = here()
    B = x.shape[0]
    for d in range(1, W):
        greet((t, flip(p, d), c))
    arrive(W - 1)
    rows = o.at[pl.ds(pl.multiple_of(p * B, B), B)]
    copies = [remote(x, rows, ss.at[d], rs.at[d], (t, flip(p, d), c)) for d in range(1, W)]
    local = pltpu.make_async_copy(x, rows, ls)
    for copy in copies + [local]:
        copy.start()
    for copy in copies + [local]:
        copy.wait()


def plane_gather(cid, x):
    return pl.pallas_call(
        plane_gather_body,
        out_shape=out((W * x.shape[0], x.shape[1]), x.dtype),
        in_specs=[hbm()],
        out_specs=hbm(),
        scratch_shapes=[dma(W), dma(W), pltpu.SemaphoreType.DMA],
        compiler_params=talk(cid),
        name="gather%d" % cid,
    )(x)


def plane_sum_body(x, o, sb, recv, ss, rs):
    t, p, c = here()
    for d in range(1, W):
        greet((t, flip(p, d), c))
    sb[...] = x[...].astype(BF)
    arrive(W - 1)
    copies = [
        remote(sb, recv.at[d - 1], ss.at[d - 1], rs.at[d - 1], (t, flip(p, d), c))
        for d in range(1, W)
    ]
    for copy in copies:
        copy.start()
    for copy in copies:
        copy.wait()
    total = x[...]
    for d in range(W - 1):
        total = total + recv[d].astype(F32)
    o[...] = total


def plane_sum(cid, x):
    return pl.pallas_call(
        plane_sum_body,
        out_shape=out(x.shape),
        in_specs=[vmem()],
        out_specs=vmem(),
        scratch_shapes=[
            pltpu.VMEM(x.shape, BF),
            pltpu.VMEM((W - 1,) + x.shape, BF),
            dma(W - 1),
            dma(W - 1),
        ],
        compiler_params=talk(cid),
        name="plane_sum%d" % cid,
    )(x)


def turn_body(back, gather, parts, *refs):
    refs = list(refs)
    part = refs.pop(0)
    x = refs.pop(0)
    g = refs.pop(0) if back else None
    o = refs.pop(0)
    gath = refs.pop(0) if gather else None
    own, recv, sbuf, ss, rs, ls, ss2, rs2, ls2 = refs
    t, p, c = here()
    B = x.shape[0]
    rows = B // parts
    for d in range(1, W):
        greet((t, flip(p, d), c))
    local = pltpu.make_async_copy(part.at[pl.ds(pl.multiple_of(p * B, B), B)], own, ls)
    local.start()
    arrive(W - 1)
    first = {}
    for k in range(parts):
        for d in range(1, W):
            q = flip(p, d)
            first[k, d] = remote(
                part.at[pl.ds(pl.multiple_of(q * B + k * rows, rows), rows)],
                recv.at[d - 1, pl.ds(k * rows, rows)],
                ss.at[d - 1, k],
                rs.at[d - 1, k],
                (t, q, c),
            )
            first[k, d].start()
    local.wait()
    later = []
    for k in range(parts):
        for d in range(1, W):
            first[k, d].wait_recv()
        cut = pl.ds(k * rows, rows)
        total = own[cut, :].astype(F32)
        for d in range(W - 1):
            total = total + recv[d, cut, :].astype(F32)
        value = x[cut, :]
        if back:
            r = lax.rsqrt(jnp.mean(value * value, axis=-1, keepdims=True) + EPS)
            hat = value * r
            new = g[cut, :] + r * (total - hat * jnp.mean(total * hat, axis=-1, keepdims=True))
        else:
            new = value + total
        o[cut, :] = new.astype(o.dtype)
        if gather:
            sbuf[cut, :] = (new if back else unit(new)).astype(BF)
            place = gath.at[pl.ds(pl.multiple_of(p * B + k * rows, rows), rows)]
            for d in range(1, W):
                later.append(
                    remote(sbuf.at[cut], place, ss2.at[d - 1, k], rs2.at[d - 1, k], (t, flip(p, d), c))
                )
            later.append(pltpu.make_async_copy(sbuf.at[cut], place, ls2.at[k]))
            for copy in later[-W:]:
                copy.start()
    for copy in first.values():
        copy.wait_send()
    for copy in later:
        copy.wait()


def turn(cid, part, x, g=None, gather=True, dtype=F32, parts=2):
    B, D = x.shape
    back = g is not None
    shapes = [out((B, D), dtype)]
    specs = [vmem()]
    if gather:
        shapes.append(out((W * B, D), BF))
        specs.append(hbm())
    args = (part, x) + ((g,) if back else ())
    return pl.pallas_call(
        functools.partial(turn_body, back, gather, parts),
        out_shape=tuple(shapes),
        in_specs=[hbm()] + [vmem()] * (len(args) - 1),
        out_specs=tuple(specs),
        scratch_shapes=[
            pltpu.VMEM((B, D), BF),
            pltpu.VMEM((W - 1, B, D), BF),
            pltpu.VMEM((B, D), BF),
            dma(W - 1, parts), dma(W - 1, parts), pltpu.SemaphoreType.DMA,
            dma(W - 1, parts), dma(W - 1, parts), dma(parts),
        ],
        compiler_params=talk(cid),
        name="turn%d" % cid,
    )(*args)


def chain_body(T, back, v, a2, h, recv, ss, rs):
    t, p, c = here()
    sign = -1 if back else 1
    for k in range(1, T):
        source = t - sign * k

        @pl.when((source >= 0) & (source < T))
        def _():
            greet((lax.rem(source + T, T), p, c))

    arrive_some(t if back else T - 1 - t)

    def send(k):
        to = lax.rem(t + sign * k + T, T)
        return remote(v, recv.at[k - 1], ss.at[k - 1], rs.at[k - 1], (to, p, c))

    for k in range(1, T):
        to = t + sign * k

        @pl.when((to >= 0) & (to < T))
        def _():
            send(k).start()

    h[...] = jnp.zeros_like(h)
    for k in range(T - 1, 0, -1):
        source = t - sign * k

        @pl.when((source >= 0) & (source < T))
        def _():
            send(k).wait_recv()
            decay = jnp.exp2(a2[...] * recv[k - 1, 16:17, :]) * recv[k - 1, 17:18, :]
            h[...] = recv[k - 1, 0:16, :] + decay * h[...]

    for k in range(1, T):
        to = t + sign * k

        @pl.when((to >= 0) & (to < T))
        def _():
            send(k).wait_send()


def chain(cid, T, back, v, a2):
    return pl.pallas_call(
        functools.partial(chain_body, T, back),
        out_shape=out(a2.shape),
        in_specs=[vmem(), vmem()],
        out_specs=vmem(),
        scratch_shapes=[pltpu.VMEM((T - 1,) + v.shape, F32), dma(T - 1), dma(T - 1)],
        compiler_params=talk(cid),
        name="chain%d" % cid,
    )(v, a2)


def rope(w, cosine, sine):
    return w * cosine + pltpu.roll(w, HD // 2, 1) * sine


def keys_body(T, hops, qkv, cosine, sine, q, k_all, v_all, ss, rs):
    t, p, c = here()
    CH = q.shape[0]
    width = q.shape[1]
    for d in range(1, hops + 1):

        @pl.when(t >= d)
        def _():
            greet((lax.rem(t - d + T, T), p, c))

    mine = pl.ds(hops * CH, CH)
    for h in range(width // HD):
        cols = pl.ds(h * HD, HD)
        q[:, cols] = rope(qkv[:, cols], cosine[...], sine[...]).astype(BF)
        k_all[mine, cols] = rope(
            qkv[:, pl.ds(width + h * HD, HD)], cosine[...], sine[...]
        ).astype(BF)
    v_all[mine, :] = qkv[:, pl.ds(2 * width, width)].astype(BF)
    arrive_some(jnp.minimum(hops, T - 1 - t))

    def send(a, d):
        ref = (k_all, v_all)[a]
        return remote(
            ref.at[mine],
            ref.at[pl.ds((hops - d) * CH, CH)],
            ss.at[a, d - 1],
            rs.at[a, d - 1],
            (lax.rem(t + d, T), p, c),
        )

    for d in range(1, hops + 1):

        @pl.when(t + d < T)
        def _():
            send(0, d).start()
            send(1, d).start()

    for d in range(1, hops + 1):

        @pl.when(t < d)
        def _():
            k_all[pl.ds((hops - d) * CH, CH), :] = jnp.zeros((CH, width), BF)
            v_all[pl.ds((hops - d) * CH, CH), :] = jnp.zeros((CH, width), BF)

        @pl.when(t >= d)
        def _():
            send(0, d).wait_recv()
            send(1, d).wait_recv()

        @pl.when(t + d < T)
        def _():
            send(0, d).wait_send()
            send(1, d).wait_send()


def keys_call(cid, T, hops, qkv, cosine, sine):
    CH = qkv.shape[0]
    width = qkv.shape[1] // 3
    return pl.pallas_call(
        functools.partial(keys_body, T, hops),
        out_shape=(
            out((CH, width), BF),
            out(((hops + 1) * CH, width), BF),
            out(((hops + 1) * CH, width), BF),
        ),
        in_specs=[vmem()] * 3,
        out_specs=(vmem(),) * 3,
        scratch_shapes=[dma(2, hops), dma(2, hops)],
        compiler_params=talk(cid),
        name="keys",
    )(qkv, cosine, sine)


def keys_back_body(T, hops, dq, dk, dv, cosine, sine, dqkv, sb, recv, ss, rs):
    t, p, c = here()
    CH = dq.shape[0]
    width = dq.shape[1]
    for d in range(1, hops + 1):

        @pl.when(t + d < T)
        def _():
            greet((lax.rem(t + d, T), p, c))

    for d in range(1, hops + 1):
        rows = pl.ds((hops - d) * CH, CH)
        sb[0, d - 1] = dk[rows, :].astype(BF)
        sb[1, d - 1] = dv[rows, :].astype(BF)
    arrive_some(jnp.minimum(hops, t))

    def send(a, d):
        return remote(
            sb.at[a, d - 1],
            recv.at[a, d - 1],
            ss.at[a, d - 1],
            rs.at[a, d - 1],
            (lax.rem(t - d + T, T), p, c),
        )

    for d in range(1, hops + 1):

        @pl.when(t >= d)
        def _():
            send(0, d).start()
            send(1, d).start()

    mine = pl.ds(hops * CH, CH)
    for h in range(width // HD):
        cols = pl.ds(h * HD, HD)
        dqkv[:, cols] = rope(dq[:, cols], cosine[...], -sine[...]).astype(BF)
    for d in range(1, hops + 1):

        @pl.when(t + d < T)
        def _():
            send(0, d).wait_recv()
            send(1, d).wait_recv()

        @pl.when(t + d >= T)
        def _():
            recv[0, d - 1] = jnp.zeros((CH, width), BF)
            recv[1, d - 1] = jnp.zeros((CH, width), BF)

        @pl.when(t >= d)
        def _():
            send(0, d).wait_send()
            send(1, d).wait_send()

    for h in range(width // HD):
        cols = pl.ds(h * HD, HD)
        k_sum = dk[mine, cols]
        v_sum = dv[mine, cols]
        for d in range(hops):
            k_sum = k_sum + recv[0, d, :, cols].astype(F32)
            v_sum = v_sum + recv[1, d, :, cols].astype(F32)
        dqkv[:, pl.ds(width + h * HD, HD)] = rope(k_sum, cosine[...], -sine[...]).astype(BF)
        dqkv[:, pl.ds(2 * width + h * HD, HD)] = v_sum.astype(BF)


def keys_back_call(cid, T, hops, dq, dk, dv, cosine, sine):
    CH, width = dq.shape
    return pl.pallas_call(
        functools.partial(keys_back_body, T, hops),
        out_shape=out((CH, 3 * width), BF),
        in_specs=[vmem()] * 5,
        out_specs=vmem(),
        scratch_shapes=[
            pltpu.VMEM((2, hops, CH, width), BF),
            pltpu.VMEM((2, hops, CH, width), BF),
            dma(2, hops),
            dma(2, hops),
        ],
        compiler_params=talk(cid, 48),
        name="keys_back",
    )(dq, dk, dv, cosine, sine)


def rim_body(T, x, o, recv, ss, rs):
    t, p, c = here()

    @pl.when(t < T - 1)
    def _():
        greet((lax.rem(t + 1, T), p, c))

    def send():
        return remote(x, recv, ss, rs, (lax.rem(t + T - 1, T), p, c))

    @pl.when(t > 0)
    def _():
        arrive(1)
        send().start()
        send().wait_send()

    o[...] = jnp.zeros_like(o)

    @pl.when(t < T - 1)
    def _():
        send().wait_recv()
        o[...] = recv[...]


def rim_back(cid, T, x):
    return pl.pallas_call(
        functools.partial(rim_body, T),
        out_shape=out(x.shape),
        in_specs=[vmem()],
        out_specs=vmem(),
        scratch_shapes=[pltpu.VMEM(x.shape, F32), pltpu.SemaphoreType.DMA, pltpu.SemaphoreType.DMA],
        compiler_params=talk(cid),
        name="rim_back",
    )(x)


def small_body(T, x, o, recv, ss, rs):
    t, p, c = here()
    peers = [(dt, dc) for dt in range(T) for dc in range(2) if dt or dc]

    def device(dt, dc):
        return lax.rem(t + dt, T), flip(c, dc)

    for dt, dc in peers:
        tt, cc = device(dt, dc)
        greet((tt, p, cc))
    arrive(len(peers))
    copies = []
    for i, (dt, dc) in enumerate(peers):
        tt, cc = device(dt, dc)
        copies.append(remote(x.at[tt * 2 + cc], recv.at[i], ss.at[i], rs.at[i], (tt, p, cc)))
        copies[-1].start()
    total = x[t * 2 + c].astype(F32)
    for i, copy in enumerate(copies):
        copy.wait()
        total = total + recv[i].astype(F32)
    o[...] = total


def small_sum(cid, T, x):
    n = x.shape[0] - 1
    return pl.pallas_call(
        functools.partial(small_body, T),
        out_shape=out(x.shape[1:]),
        in_specs=[vmem()],
        out_specs=vmem(),
        scratch_shapes=[pltpu.VMEM((n,) + x.shape[1:], x.dtype), dma(n), dma(n)],
        compiler_params=talk(cid),
        name="small_sum",
    )(x)


def conv_sum(xz, mask, taps, lo, size):
    width = taps.shape[1]
    total = jnp.broadcast_to(taps[4:5, :], (size, width))
    for j in range(4):
        rows = xz[pl.ds(lo + HALO - 3 + j, size), pl.ds(0, width)]
        total = total + taps[j : j + 1, :] * rows * mask[pl.ds(lo, size), j : j + 1]
    return total


def conv_body(xz, mask, taps, proj, u, u_low, part):
    CH = u.shape[0]
    step = min(CH, 128)
    for lo in range(0, CH, step):
        cut = pl.ds(lo, step)
        c = conv_sum(xz, mask, taps, lo, step)
        value = c / (1.0 + jnp.exp(-c))
        u[cut, :] = value
        low = value.astype(BF)
        u_low[cut, :] = low
        part[cut, :] = jnp.dot(low, proj[...], preferred_element_type=F32)


def conv_call(xz, mask, taps, proj):
    CH = mask.shape[0]
    width = taps.shape[1]
    return pl.pallas_call(
        conv_body,
        out_shape=(out((CH, width)), out((CH, width), BF), out((CH, proj.shape[1]))),
        in_specs=[vmem()] * 4,
        out_specs=(vmem(),) * 3,
        compiler_params=alone(),
        name="conv",
    )(xz, mask, taps, proj)


def conv_back_body(xz, mask, taps, du, dxs, grads):
    CH, width = du.shape
    step = min(CH, 128)
    dxs[...] = jnp.zeros_like(dxs)
    sums = [jnp.zeros((1, width), F32) for _ in range(5)]
    for lo in range(0, CH, step):
        c = conv_sum(xz, mask, taps, lo, step)
        s = 1.0 / (1.0 + jnp.exp(-c))
        dc = du[pl.ds(lo, step), :] * (s * (1.0 + c * (1.0 - s)))
        sums[4] = sums[4] + jnp.sum(dc, axis=0, keepdims=True)
        for j in range(4):
            rows = pl.ds(lo + HALO - 3 + j, step)
            live = dc * mask[pl.ds(lo, step), j : j + 1]
            sums[j] = sums[j] + jnp.sum(live * xz[rows, pl.ds(0, width)], axis=0, keepdims=True)
            dxs[rows, :] = dxs[rows, :] + live * taps[j : j + 1, :]
    grads[...] = jnp.zeros_like(grads)
    for j in range(5):
        grads[j : j + 1, :] = sums[j]


def conv_back_call(xz, mask, taps, du):
    CH, width = du.shape
    return pl.pallas_call(
        conv_back_body,
        out_shape=(out((HALO + CH, width)), out((8, width))),
        in_specs=[vmem()] * 4,
        out_specs=(vmem(),) * 2,
        compiler_params=alone(),
        name="conv_back",
    )(xz, mask, taps, du)


def wide(block, width):
    return jnp.concatenate([block] * (width // 128), axis=1) if width > 128 else block


def fold(block):
    total = block[:, 0:128]
    for lo in range(128, block.shape[1], 128):
        total = total + block[:, lo : lo + 128]
    return total


def scan_one_body(delta, u, a2, brep, first, end):
    CH, width = delta.shape
    decay = a2[...]

    def group(g, h):
        lo = pl.multiple_of(g * 8, 8)
        d8 = delta[pl.ds(lo, 8), :]
        du8 = d8 * u[pl.ds(lo, 8), :]
        for i in range(8):
            d = d8[i : i + 1, :] + first[lo + i]
            b = wide(brep[pl.ds(pl.multiple_of(g * 128 + i * 16, 16), 16), :], width)
            h = jnp.exp2(d * decay) * h + du8[i : i + 1, :] * b
        return h

    end[...] = lax.fori_loop(0, CH // 8, group, jnp.zeros(decay.shape, F32))


def scan_one(delta, u, a2, brep, first):
    return pl.pallas_call(
        scan_one_body,
        out_shape=out(a2.shape),
        in_specs=[vmem()] * 4 + [smem()],
        out_specs=vmem(),
        compiler_params=alone(),
        name="scan_one",
    )(delta, u, a2, brep, first)


def scan_two_body(delta, u, a2, brep, crep, first, h_in, y, marks):
    CH, width = delta.shape
    decay = a2[...]
    row = lax.broadcasted_iota(jnp.int32, (8, width), 0)

    def group(g, h):
        lo = pl.multiple_of(g * 8, 8)

        @pl.when(lax.rem(g, SUB // 8) == 0)
        def _():
            marks[pl.ds(pl.multiple_of(lax.div(g, SUB // 8) * 16, 16), 16), :] = h

        d8 = delta[pl.ds(lo, 8), :]
        du8 = d8 * u[pl.ds(lo, 8), :]
        y8 = jnp.zeros((8, width), F32)
        for i in range(8):
            at = pl.ds(pl.multiple_of(g * 128 + i * 16, 16), 16)
            d = d8[i : i + 1, :] + first[lo + i]
            h = jnp.exp2(d * decay) * h + du8[i : i + 1, :] * wide(brep[at, :], width)
            total = jnp.sum(h * wide(crep[at, :], width), axis=0, keepdims=True)
            y8 = jnp.where(row == i, total, y8)
        y[pl.ds(lo, 8), :] = y8
        return h

    lax.fori_loop(0, CH // 8, group, h_in[...])


def scan_two(delta, u, a2, brep, crep, first, h_in):
    CH, width = delta.shape
    return pl.pallas_call(
        scan_two_body,
        out_shape=(out((CH, width)), out((CH // SUB * 16, width))),
        in_specs=[vmem()] * 5 + [smem(), vmem()],
        out_specs=(vmem(),) * 2,
        compiler_params=alone(),
        name="scan_two",
    )(delta, u, a2, brep, crep, first, h_in)


def scan_three_body(delta, dy, a2, crep, first, start):
    CH, width = delta.shape
    decay = a2[...]

    def group(step, carry):
        g = CH // 8 - 1 - step
        lo = pl.multiple_of(g * 8, 8)
        d8 = delta[pl.ds(lo, 8), :]
        dy8 = dy[pl.ds(lo, 8), :]
        for i in range(7, -1, -1):
            at = pl.ds(pl.multiple_of(g * 128 + i * 16, 16), 16)
            d = d8[i : i + 1, :] + first[lo + i]
            lam = dy8[i : i + 1, :] * wide(crep[at, :], width) + carry
            carry = jnp.exp2(d * decay) * lam
        return carry

    start[...] = lax.fori_loop(0, CH // 8, group, jnp.zeros(decay.shape, F32))


def scan_three(delta, dy, a2, crep, first):
    return pl.pallas_call(
        scan_three_body,
        out_shape=out(a2.shape),
        in_specs=[vmem()] * 4 + [smem()],
        out_specs=vmem(),
        compiler_params=alone(),
        name="scan_three",
    )(delta, dy, a2, crep, first)


def scan_four_body(
    delta, u, dy, skip, a2, brep, crep, first, marks, g_in,
    ddelta, du_out, db, dc, ga, keep_a, keep_w,
):
    CH, width = delta.shape
    decay = a2[...]
    rate = decay * (1.0 / LOG2E)
    row = lax.broadcasted_iota(jnp.int32, (8, width), 0)
    per = SUB // 8

    def block(step, carried):
        blk = CH // SUB - 1 - step

        def forward(k, h):
            g = blk * per + k
            lo = pl.multiple_of(g * 8, 8)
            d8 = delta[pl.ds(lo, 8), :]
            du8 = d8 * u[pl.ds(lo, 8), :]
            for i in range(8):
                at = pl.ds(pl.multiple_of(g * 128 + i * 16, 16), 16)
                put = pl.ds(pl.multiple_of(k * 128 + i * 16, 16), 16)
                d = d8[i : i + 1, :] + first[lo + i]
                a = jnp.exp2(d * decay)
                keep_a[put, :] = a
                w = a * h
                keep_w[put, :] = w
                h = w + du8[i : i + 1, :] * wide(brep[at, :], width)
            return h

        lax.fori_loop(0, per, forward, marks[pl.ds(pl.multiple_of(blk * 16, 16), 16), :])

        def backward(back, state):
            carry, total_a = state
            k = per - 1 - back
            g = blk * per + k
            lo = pl.multiple_of(g * 8, 8)
            d8 = delta[pl.ds(lo, 8), :]
            u8 = u[pl.ds(lo, 8), :]
            du8 = d8 * u8
            dy8 = dy[pl.ds(lo, 8), :]
            s1 = jnp.zeros((8, width), F32)
            s2 = jnp.zeros((8, width), F32)
            for i in range(7, -1, -1):
                at = pl.ds(pl.multiple_of(g * 128 + i * 16, 16), 16)
                put = pl.ds(pl.multiple_of(k * 128 + i * 16, 16), 16)
                b = wide(brep[at, :], width)
                du = du8[i : i + 1, :]
                dyi = dy8[i : i + 1, :]
                w = keep_w[put, :]
                lam = dyi * wide(crep[at, :], width) + carry
                lw = lam * w
                s1 = jnp.where(row == i, jnp.sum(lam * b, axis=0, keepdims=True), s1)
                s2 = jnp.where(row == i, jnp.sum(lw * rate, axis=0, keepdims=True), s2)
                total_a = total_a + lw * d8[i : i + 1, :]
                dc[at, :] = fold((w + du * b) * dyi)
                db[at, :] = fold(lam * du)
                carry = keep_a[put, :] * lam
            ddelta[pl.ds(lo, 8), :] = s2 + u8 * s1
            du_out[pl.ds(lo, 8), :] = d8 * s1 + skip[0:1, :] * dy8
            return carry, total_a

        return lax.fori_loop(0, per, backward, carried)

    carry, total_a = lax.fori_loop(
        0, CH // SUB, block, (g_in[...], jnp.zeros(decay.shape, F32))
    )
    ga[...] = total_a * rate


def scan_four(delta, u, dy, skip, a2, brep, crep, first, marks, g_in):
    CH, width = delta.shape
    return pl.pallas_call(
        scan_four_body,
        out_shape=(
            out((CH, width)),
            out((CH, width)),
            out((CH * 16, 128)),
            out((CH * 16, 128)),
            out(a2.shape),
        ),
        in_specs=[vmem()] * 7 + [smem(), vmem(), vmem()],
        out_specs=(vmem(),) * 5,
        scratch_shapes=[pltpu.VMEM((SUB * 16, width), F32), pltpu.VMEM((SUB * 16, width), F32)],
        compiler_params=alone(),
        name="scan_four",
    )(delta, u, dy, skip, a2, brep, crep, first, marks, g_in)


def nt(a, b):
    return lax.dot_general(a, b, (((1,), (1,)), ((), ())), preferred_element_type=F32)


def tn(a, b):
    return lax.dot_general(a, b, (((0,), (0,)), ((), ())), preferred_element_type=F32)


def nn(a, b):
    return jnp.dot(a, b, preferred_element_type=F32)


def attend_body(q, k, v, bias, o, lse):
    s = nt(q[...], k[...]) * (HD**-0.5) + bias[...].astype(F32)
    top = jnp.max(s, axis=-1, keepdims=True)
    e = jnp.exp(s - top)
    total = jnp.sum(e, axis=-1, keepdims=True)
    o[...] = nn((e / total).astype(BF), v[...]).astype(BF)
    lse[...] = jnp.broadcast_to(top + jnp.log(total), lse.shape)


def attend(q, k, v, bias):
    CH, width = q.shape
    NK = k.shape[0]
    tq = min(CH, 256)
    return pl.pallas_call(
        attend_body,
        grid=(width // HD, CH // tq),
        out_shape=(out((CH, width), BF), out((CH, width))),
        in_specs=[
            pl.BlockSpec((tq, HD), lambda h, i: (i, h)),
            pl.BlockSpec((NK, HD), lambda h, i: (0, h)),
            pl.BlockSpec((NK, HD), lambda h, i: (0, h)),
            pl.BlockSpec((tq, NK), lambda h, i: (i, 0)),
        ],
        out_specs=(
            pl.BlockSpec((tq, HD), lambda h, i: (i, h)),
            pl.BlockSpec((tq, HD), lambda h, i: (i, h)),
        ),
        compiler_params=alone(),
        name="attend",
    )(q, k, v, bias)


def attend_back_body(q, k, v, bias, lse, do, dq, dk, dv):
    scale = HD**-0.5
    first = pl.program_id(1) == 0
    s = nt(q[...], k[...]) * scale + bias[...].astype(F32)
    prob = jnp.exp(s - lse[:, 0:1])
    dp = nt(do[...], v[...])
    rowdot = jnp.sum(prob * dp, axis=-1, keepdims=True)
    ds = (prob * (dp - rowdot)).astype(BF)
    dq[...] = nn(ds, k[...]) * scale
    add_k = tn(ds, q[...]) * scale
    add_v = tn(prob.astype(BF), do[...])

    @pl.when(first)
    def _():
        dk[...] = add_k
        dv[...] = add_v

    @pl.when(jnp.logical_not(first))
    def _():
        dk[...] += add_k
        dv[...] += add_v


def attend_back(q, k, v, bias, lse, do):
    CH, width = q.shape
    NK = k.shape[0]
    tq = min(CH, 256)
    rows = pl.BlockSpec((tq, HD), lambda h, i: (i, h))
    keys = pl.BlockSpec((NK, HD), lambda h, i: (0, h))
    return pl.pallas_call(
        attend_back_body,
        grid=(width // HD, CH // tq),
        out_shape=(out((CH, width)), out((NK, width)), out((NK, width))),
        in_specs=[rows, keys, keys, pl.BlockSpec((tq, NK), lambda h, i: (i, 0)), rows, rows],
        out_specs=(rows, keys, keys),
        compiler_params=alone(),
        name="attend_back",
    )(q, k, v, bias, lse, do)


def columns_out(weight, gain, groups, T, cols):
    rows = weight.shape[0]
    scaled = (weight.astype(F32) * gain.astype(F32)[:, None]).astype(BF)
    return scaled.reshape(rows, groups, T, W, cols).transpose(3, 0, 1, 2, 4).reshape(W, rows, -1)


def columns_back(blocks, groups, T, cols):
    rows = blocks.shape[1]
    wide_form = blocks.reshape(W, rows, groups, T, cols).transpose(1, 2, 3, 0, 4)
    return wide_form.reshape(rows, -1).astype(F32)


def gather_tc(x):
    return lax.all_gather(x.reshape(-1, x.shape[-1]), ("t", "c"), axis=0, tiled=True)


def scatter_tc(x):
    return lax.psum_scatter(x, ("t", "c"), scatter_dimension=0, tiled=True)


def swiglu(a):
    width = a.shape[1] // 2
    return jax.nn.silu(a[:, :width]) * a[:, width:]


def swiglu_back(a, dh):
    width = a.shape[1] // 2
    gate, up = a[:, :width], a[:, width:]
    s = jax.nn.sigmoid(gate)
    return jnp.concatenate([dh * up * (s * (1.0 + gate * (1.0 - s))), dh * gate * s], axis=1).astype(BF)


def local(
    inputs, segment_ids, cotangent, norm_mixer, in_proj, conv_weight, conv_bias, state_proj,
    step_proj, step_bias, decay_log, skip_gain, mixer_out, norm_ffn_one, gate_up_one, down_one,
    norm_attn, qkv_proj, attn_out, norm_ffn_two, gate_up_two, down_two,
):
    T = lax.axis_size("t")
    t, p, c = here()
    B, D = inputs.shape[1:]
    CH = W * B
    total = CH * T
    seq_len = min(SEQ_MAX, total)
    CB = conv_bias.shape[0]
    DI = CB * W * T * 2
    FB = down_one.shape[0]
    R = step_proj.shape[0]
    N = decay_log.shape[1]
    NR = state_proj.shape[1]
    width = CB * 2 * T
    heads = H // W * HD
    most = min(WIN, total // 2)
    hops = -(-(most - 1) // CH)

    par = jnp.concatenate(
        [
            state_proj, step_proj.T, decay_log, conv_weight.T,
            conv_bias[:, None], step_bias[:, None], skip_gain[:, None],
        ],
        axis=1,
    )
    used = par.shape[1]
    par = jnp.pad(par, ((0, 0), (0, 256 - used)))
    win_out = columns_out(in_proj, norm_mixer, 2, T, 2 * CB)
    seg8 = jnp.broadcast_to(segment_ids, (8, B))
    x0 = inputs[0].astype(F32)
    nh1_ext, seg_all, par_all, win_mine = start_call(T, inputs[0], seg8, par, win_out)
    w_in = gather_tc(win_mine)

    gu1_out = columns_out(gate_up_one, norm_ffn_one, 2, T, 2 * FB)
    qkv_out = columns_out(qkv_proj, norm_attn, 3, 1, heads)
    gu2_out = columns_out(gate_up_two, norm_ffn_two, 2, T, 2 * FB)
    gu1_mine, qkv_mine, gu2_mine = spread_call(1, False, (gu1_out, qkv_out, gu2_out))
    devices = 2 * W * T
    pairs = []
    for d in range(devices):
        rest = d % (2 * T)
        pairs.append((d, (rest // 2) * 2 * W + (d // (2 * T)) * 2 + rest % 2))
    ao_mine = lax.ppermute(attn_out, ("t", "p", "c"), pairs)
    w_mix = gather_tc(mixer_out)
    w_gu1 = gather_tc(gu1_mine)
    w_d1 = gather_tc(down_one)
    w_qkv = gather_tc(qkv_mine)
    w_ao = gather_tc(ao_mine)
    w_gu2 = gather_tc(gu2_mine)
    w_d2 = gather_tc(down_two)
    gl4 = plane_gather(2, cotangent[0])

    seg = seg_all[:, 0, :].reshape(total)
    pos = t * CH + jnp.arange(CH, dtype=jnp.int32)
    padded = jnp.pad(seg, (max(hops * CH, HALO), 0), constant_values=-1)
    lead = max(hops * CH, HALO)
    near = lax.dynamic_slice(padded, (t * CH + lead - HALO,), (CH + HALO,))
    own_seg = near[HALO:]
    conv_mask = jnp.stack(
        [
            (near[HALO - 3 + j : HALO - 3 + j + CH] == own_seg) & ((pos - 3 + j) // seq_len == pos // seq_len)
            & (pos - 3 + j >= 0)
            for j in range(4)
        ]
        + [jnp.zeros((CH,), jnp.bool_)] * 4,
        axis=1,
    ).astype(F32)
    starts = (pos % seq_len == 0) | (near[HALO - 1 : HALO - 1 + CH] != own_seg)
    first = jnp.where(starts, BIG, 0.0).astype(F32)
    alive = jnp.where(jnp.any(starts), 0.0, 1.0).astype(F32)
    NK = (hops + 1) * CH
    key_seg = lax.dynamic_slice(padded, (t * CH + lead - hops * CH,), (NK,))
    key_pos = t * CH - hops * CH + jnp.arange(NK, dtype=jnp.int32)
    away = pos[:, None] - key_pos[None, :]
    allowed = (
        (key_pos[None, :] >= 0) & (away >= 0) & (away < WIN) & (key_seg[None, :] == own_seg[:, None])
        & (key_pos[None, :] // seq_len == (pos // seq_len)[:, None])
    )
    bias = jnp.where(allowed, 0.0, NEG).astype(BF)
    half = HD // 2
    inverse = jnp.exp(jnp.arange(half, dtype=F32) * (-math.log(10000.0) * 2.0 / HD))
    angles = (pos % seq_len).astype(F32)[:, None] * inverse[None, :]
    cos_half, sin_half = jnp.cos(angles), jnp.sin(angles)
    cosine = jnp.concatenate([cos_half, cos_half], axis=1)
    sine = jnp.concatenate([-sin_half, sin_half], axis=1)

    par_all = par_all.reshape(width, 256)
    w_state = par_all[:, :NR]
    w_step = par_all[:, NR : NR + R].T
    side = par_all[:, NR + R : used].astype(F32).T
    a2 = -jnp.exp(side[:N]) * LOG2E
    taps = jnp.pad(side[N : N + 5], ((0, 3), (0, 0)))
    step_row = side[N + 5 : N + 6]
    skip_row = side[N + 6 : N + 7]

    xz = nn(nh1_ext, w_in)
    nh1 = nh1_ext[HALO:]
    u, u_low, part = conv_call(xz, conv_mask, taps, w_state)
    pr = plane_sum(3, part)
    dt_low = pr[:, :R].astype(BF)
    pre = nn(dt_low, w_step) + step_row
    delta = jax.nn.softplus(pre)

    def replicated(block):
        return jnp.broadcast_to(block[:, :, None], (CH, N, 128)).reshape(CH * N, 128)

    brep = replicated(pr[:, R : R + N])
    crep = replicated(pr[:, R + N :])
    sum_delta = jnp.sum(delta, axis=0, keepdims=True)

    def packed(state):
        return jnp.concatenate(
            [state, sum_delta, jnp.full((1, width), alive, F32), jnp.zeros((6, width), F32)], axis=0
        )

    end = scan_one(delta, u, a2, brep, first)
    h_in = chain(4, T, False, packed(end), a2)
    y_scan, marks = scan_two(delta, u, a2, brep, crep, first, h_in)
    y = y_scan + skip_row * u
    zg = xz[HALO:, width:]
    gate_s = jax.nn.sigmoid(zg)
    gated = (y * zg * gate_s).astype(BF)
    x1, nh2 = turn(5, nn(gated, w_mix).astype(BF), x0)

    a_one = nn(nh2, w_gu1)
    h_one = swiglu(a_one).astype(BF)
    x2, nh3 = turn(6, nn(h_one, w_d1).astype(BF), x1)

    qkv = nn(nh3, w_qkv)
    q, k_all, v_all = keys_call(7, T, hops, qkv, cosine, sine)
    o, lse = attend(q, k_all, v_all, bias)
    x3, nh4 = turn(8, nn(o, w_ao).astype(BF), x2)

    a_two = nn(nh4, w_gu2)
    h_two = swiglu(a_two).astype(BF)
    (final,) = turn(9, nn(h_two, w_d2).astype(BF), x3, gather=False, dtype=BF)

    g4 = cotangent[0].astype(F32)
    da_two = swiglu_back(a_two, nt(gl4, w_d2))
    g3, gl3 = turn(10, nt(da_two, w_gu2).astype(BF), x3, g4)
    grad_d2 = scatter_tc(tn(h_two, gl4).astype(BF))
    raw_gu2 = scatter_tc(tn(nh4, da_two).astype(BF))

    do = nt(gl3, w_ao).astype(BF)
    dq, dk, dv = attend_back(q, k_all, v_all, bias, lse, do)
    dqkv = keys_back_call(11, T, hops, dq, dk, dv, cosine, sine)
    g2, gl2 = turn(12, nt(dqkv, w_qkv).astype(BF), x2, g3)
    raw_ao = scatter_tc(tn(o, gl3).astype(BF))
    raw_qkv = scatter_tc(tn(nh3, dqkv).astype(BF))

    da_one = swiglu_back(a_one, nt(gl2, w_d1))
    g1, gl1 = turn(13, nt(da_one, w_gu1).astype(BF), x1, g2)
    grad_d1 = scatter_tc(tn(h_one, gl2).astype(BF))
    raw_gu1 = scatter_tc(tn(nh2, da_one).astype(BF))

    dgate = nt(gl1, w_mix)
    dy = dgate * zg * gate_s
    dz_low = (dgate * y * gate_s * (1.0 + zg * (1.0 - gate_s))).astype(BF)
    grad_mix = scatter_tc(tn(gated, gl1).astype(BF))
    begin = scan_three(delta, dy, a2, crep, first)
    g_in = chain(14, T, True, packed(begin), a2)
    ddelta, du_scan, db, dc_mat, ga = scan_four(
        delta, u, dy, skip_row, a2, brep, crep, first, marks, g_in
    )
    dpre = ddelta * jax.nn.sigmoid(pre)
    dpre_low = dpre.astype(BF)
    part_back = jnp.concatenate(
        [
            nt(dpre_low, w_step),
            jnp.sum(db, axis=1).reshape(CH, N),
            jnp.sum(dc_mat, axis=1).reshape(CH, N),
        ],
        axis=1,
    )
    dpr_low = plane_sum(15, part_back).astype(BF)
    du = du_scan + nt(dpr_low, w_state)
    dxs_ext, conv_grads = conv_back_call(xz, conv_mask, taps, du)
    rim = rim_back(16, T, dxs_ext[8:16])
    dxs_low = jnp.concatenate(
        [dxs_ext[HALO : HALO + CH - 8], dxs_ext[HALO + CH - 8 :] + rim], axis=0
    ).astype(BF)
    dxz = jnp.concatenate([dxs_low, dz_low], axis=1)
    raw_in = scatter_tc(tn(nh1, dxz).astype(BF))
    (grad_x,) = turn(17, nt(dxz, w_in).astype(BF), x0, g1, gather=False)

    small = jnp.concatenate(
        [
            tn(u_low, dpr_low),
            tn(dpre_low, dt_low),
            ga.T,
            conv_grads[:5].T,
            jnp.sum(dpre, axis=0)[:, None],
            jnp.sum(dy * u, axis=0)[:, None],
        ],
        axis=1,
    )
    small = jnp.pad(small, ((0, 0), (0, 256 - used))).astype(BF).reshape(2 * T, CB, 256)
    small = small_sum(18, T, small)

    def blocks(x):
        return x.reshape(W, x.shape[0] // W, x.shape[1])

    gu2_b, qkv_b, gu1_b = spread_call(19, True, (blocks(raw_gu2), blocks(raw_qkv), blocks(raw_gu1)))
    (in_b,) = spread_call(20, True, (blocks(raw_in),))
    grad_ao = lax.ppermute(raw_ao, ("t", "p", "c"), [(b, a) for a, b in pairs]).astype(F32)

    def finished(blocks_in, weight, gain, groups, groups_t, cols):
        raw = columns_back(blocks_in, groups, groups_t, cols)
        return (
            jnp.sum(weight.astype(F32) * raw, axis=1),
            raw * gain.astype(F32)[:, None],
        )

    grad_n1, grad_in = finished(in_b, in_proj, norm_mixer, 2, T, 2 * CB)
    grad_n2, grad_gu1 = finished(gu1_b, gate_up_one, norm_ffn_one, 2, T, 2 * FB)
    grad_n3, grad_qkv = finished(qkv_b, qkv_proj, norm_attn, 3, 1, heads)
    grad_n4, grad_gu2 = finished(gu2_b, gate_up_two, norm_ffn_two, 2, T, 2 * FB)
    at = NR + R + N
    return (
        final[None],
        grad_x[None],
        grad_n1,
        grad_in,
        small[:, at : at + 4].T,
        small[:, at + 4],
        small[:, :NR],
        small[:, NR : NR + R].T,
        small[:, at + 5],
        small[:, NR + R : at],
        small[:, at + 6],
        grad_mix.astype(F32),
        grad_n2,
        grad_gu1,
        grad_d1.astype(F32),
        grad_n3,
        grad_qkv,
        grad_ao,
        grad_n4,
        grad_gu2,
        grad_d2.astype(F32),
    )


def solution(mesh):
    chunks = mesh.shape["seq"] // W
    view = Mesh(mesh.devices.reshape(chunks, W, mesh.shape["fsdp"]), ("t", "p", "c"))
    every = ("t", "p", "c")
    tokens = P("c", ("t", "p"), None)
    vector, rows, cols = P(every), P(every, None), P(None, every)
    placed = (
        tokens, P("c", ("t", "p")), tokens,
        vector, rows, cols, vector, rows, cols, vector, rows, vector, rows,
        vector, rows, rows, vector, rows, rows, vector, rows, rows,
    )
    return jax.shard_map(
        local,
        mesh=view,
        in_specs=placed,
        out_specs=(tokens, tokens) + placed[3:],
        check_vma=False,
    )
```

time: 6980 us -> 1150 us (0.16)
  waiting for transfers between devices: 3480 us -> 130 us
  local copies, waits for them, and re-layouts: 1290 us -> 99 us
  other arithmetic: 990 us -> 48.3 us
  Pallas kernels: 0 us -> 715 us
  matrix products: 517 us -> 124 us
  starting transfers between devices: 344 us -> 3.92 us
  blocking collectives: 272 us -> 0 us
    reduce_scatter x9 -> x8, waiting for transfers between devices: 2460 us -> 115 us  [scatter_tc(): return lax.psum_scatter(x, ('t', 'c'), scatter_dimension=0, tiled=True)]
    pallas_call x0 -> x29, Pallas kernels: none -> 715 us  [the longest x8 259 us: turn(): pl.pallas_call(functools.partial(turn_body, back, gather, parts), out_sha...]
    dynamic_slice x1152 -> x2, local copies, waits for them, and re-layouts: 696 us -> 0.16 us  [the longest x1 0.08 us: local(): near = lax.dynamic_slice(padded, (t * CH + lead - HALO,), (CH + HALO,))]
    all_gather x11 -> x8, waiting for transfers between devices: 544 us -> 12 us  [gather_tc(): lax.all_gather(x.reshape(-1, x.shape[-1]), ('t', 'c'), axis=0, tiled=True)]
    dot_general x294 -> x29, matrix products: 515 us -> 124 us  [the longest x9 44.4 us: nn(): return jnp.dot(a, b, preferred_element_type=F32)]
    dynamic_update_slice x788 -> x0, local copies, waits for them, and re-layouts: 377 us -> none  [the longest x768 359 us: block_step(): return lax.scan(token_step, state_now, block_items)]
    ppermute x83 -> x2, waiting for transfers between devices: 373 us -> 0.01 us  [the longest x1 0.01 us: local(): ao_mine = lax.ppermute(attn_out, ('t', 'p', 'c'), pairs)]
    ppermute x83 -> x2, starting transfers between devices: 343 us -> 2.23 us  [the longest x1 1.56 us: local(): lax.ppermute(raw_ao, ('t', 'p', 'c'), [(b, a) for a, b in pairs])]
where the time goes in v1:
time: 1150 us; the launch traced here: 1140 us
  Pallas kernels  715 us (62%)
  waiting for transfers between devices  130 us (11%)
  matrix products  124 us (11%)
  local copies, waits for them, and re-layouts  99 us (9%)
  other arithmetic  48.3 us (4%)
  between operations  16.2 us (1%)
    pallas_call x8, Pallas kernels, turn(): pl.pallas_call(functools.partial(turn_body, back, gather, parts), out_sha...  259 us
    reduce_scatter x8, waiting for transfers between devices, scatter_tc(): return lax.psum_scatter(x, ('t', 'c'), scatter_dimension=0, tiled=True)  115 us
    pallas_call x1, Pallas kernels, keys_back_call(): pl.pallas_call(functools.partial(keys_back_body, T, hops), out_shape=out(...  81.2 us
    pallas_call x1, Pallas kernels, keys_call(): pl.pallas_call(functools.partial(keys_body, T, hops), out_shape=(out((CH,...  67.4 us
    pallas_call x3, Pallas kernels, spread_call(): pl.pallas_call(functools.partial(spread_body, n, back), out_shape=tuple((...  65.1 us
    dot_general x9, matrix products, nn(): return jnp.dot(a, b, preferred_element_type=F32)  44.4 us
    dot_general x10, matrix products, tn(): lax.dot_general(a, b, (((0,), (0,)), ((), ())), preferred_element_type=F32)  42.7 us
    pallas_call x1, Pallas kernels, plane_gather(): pl.pallas_call(plane_gather_body, out_shape=out((W * x.shape[0], x.shape[...  40.3 us
  transfers between devices with their start and end apart: 18, of which 3 were waited for; matrix products, arithmetic and copies ran while one was open for 17% of the time, Pallas kernels for 54%

profile of v1, /device:TPU:1, one launch (start us, length us, event | category | flops | bytes accessed | tf_op | source)
XLA Modules:
  0.0 1136.5 jit_solution(10296094792547099017)
XLA Ops:
  12.8 32.4 %start.1 = (bf16[528,1536]{1,0:T(8,128)(2,1)S(1)}, s32[16,8,128]{2,1,0:T(8,128)S(1)}, bf16[8,96,256]{2,1,0:T(8,128)(2,1)S(1)}, bf16[4,48,1536]{2,1,0:T(8,128)(2,1)}) custom-call(bf16[128,1536]{1,0:T(8,128)(2,1)S(1)} %bitcast.104, s32[8,128]{1,0:T(8,128)S(1)} %broadcast_in_dim.87.seg, bf16[96,256]{1,0:T(8,128)(2,1)S(1)} %pad.17.par, ...), custom_call_target="tpu_custom_call" | custom-call | tf_op jit(solution)/shard_map/start/pallas_call | solution.py:216
  68.7 24.7 %spread1.1 = (bf16[4,48,2048]{2,1,0:T(8,128)(2,1)S(1)}, bf16[4,48,1152]{2,1,0:T(8,128)(2,1)S(1)}, bf16[4,48,2048]{2,1,0:T(8,128)(2,1)}) custom-call(bf16[4,48,2048]{2,1,0:T(8,128)(2,1)S(1)} %reshape.286.refs_0_, bf16[4,48,1152]{2,1,0:T(8,128)(2,1)S(1)} %reshape.288.refs_1_, bf16[4,48,2048]{2,1,0:T(8,128)(2,1)S(1)} %reshape.290.refs_2_), custom_call_target="tpu_custom_call" | custom-call | tf_op jit(solution)/shard_map/spread1/pallas_call | solution.py:304
  106.1 40.3 %gather2.1 = bf16[512,1536]{1,0:T(8,128)(2,1)S(1)} custom-call(bf16[128,1536]{1,0:T(8,128)(2,1)S(1)} %bitcast.107), custom_call_target="tpu_custom_call" | custom-call | tf_op jit(solution)/shard_map/gather2/pallas_call | solution.py:331
  164.7 8.8 plane_sum3.1
  179.2 9.8 scan_one.1
  189.9 7.6 chain4.1.h_in
  200.3 16.6 %scan_two.1 = (f32[512,768]{1,0:T(8,128)}, f32[128,768]{1,0:T(8,128)}) custom-call(f32[512,768]{1,0:T(8,128)} %get-tuple-element.211.delta, f32[512,768]{1,0:T(8,128)} %get-tuple-element.68.u, f32[16,768]{1,0:T(8,128)} %fusion.26.a2, f32[8192,128]{1,0:T(8,128)} %broadcast_in_dim.92.brep, f32[8192,128]{1,0:T(8,128)} %broadcast_in_dim.94.crep, ...), custom_call_target="tpu_custom_call" | custom-call | tf_op jit(solution)/shard_map/scan_two/pallas_call | solution.py:885
  223.2 36.7 %turn5.1 = (f32[128,1536]{1,0:T(8,128)S(1)}, bf16[512,1536]{1,0:T(8,128)(2,1)S(1)}) custom-call(bf16[512,1536]{1,0:T(8,128)(2,1)S(1)} %convolution_convert_fusion.14.refs_0_, f32[128,1536]{1,0:T(8,128)S(1)} %bitcast_convert_fusion.1.refs_1_), custom_call_target="tpu_custom_call" | custom-call | tf_op jit(solution)/shard_map/turn5/pallas_call | solution.py:449
  274.9 35.5 %turn6.1 = (f32[128,1536]{1,0:T(8,128)S(1)}, bf16[512,1536]{1,0:T(8,128)(2,1)S(1)}) custom-call(bf16[512,1536]{1,0:T(8,128)(2,1)S(1)} %convolution_convert_fusion.13.refs_0_, f32[128,1536]{1,0:T(8,128)S(1)} %get-tuple-element.72.refs_1_), custom_call_target="tpu_custom_call" | custom-call | tf_op jit(solution)/shard_map/turn6/pallas_call | solution.py:449
  317.1 67.4 %keys.1 = (bf16[512,384]{1,0:T(8,128)(2,1)S(1)}, bf16[1536,384]{1,0:T(8,128)(2,1)S(1)}, bf16[1536,384]{1,0:T(8,128)(2,1)S(1)}) custom-call(f32[512,1152]{1,0:T(8,128)S(1)} %fusion.72.qkv, f32[512,128]{1,0:T(8,128)S(1)} %get-tuple-element.228.cosine, f32[512,128]{1,0:T(8,128)S(1)} %get-tuple-element.229.sine), custom_call_target="tpu_custom_call" | custom-call | tf_op jit(solution)/shard_map/keys/pallas_call | solution.py:581
  387.3 9.1 attend.1
  398.9 33.4 %turn8.1 = (f32[128,1536]{1,0:T(8,128)S(1)}, bf16[512,1536]{1,0:T(8,128)(2,1)S(1)}) custom-call(bf16[512,1536]{1,0:T(8,128)(2,1)S(1)} %convolution_convert_fusion.12.refs_0_, f32[128,1536]{1,0:T(8,128)S(1)} %copy-done.3), custom_call_target="tpu_custom_call" | custom-call | tf_op jit(solution)/shard_map/turn8/pallas_call | solution.py:449
  433.4 8.7 fusion.73
  442.2 12.0 %all-gather.23.cloned.1.call-done = bf16[1024,1536]{1,0:T(8,128)(2,1)} async-done(((bf16[128,1536]{1,0:T(8,128)(2,1)}), bf16[1024,1536]{1,0:T(8,128)(2,1)}) %all-gather.23.cloned.1.call-update) | async-done | bytes 3145744 | tf_op jit(solution)/shard_map/all_gather | solution.py:1110
  464.9 37.0 %turn10.1 = (f32[128,1536]{1,0:T(8,128)S(1)}, bf16[512,1536]{1,0:T(8,128)(2,1)S(1)}) custom-call(bf16[512,1536]{1,0:T(8,128)(2,1)S(1)} %convolution_convert_fusion.10.refs_0_, f32[128,1536]{1,0:T(8,128)S(1)} %get-tuple-element.82.refs_1_, f32[128,1536]{1,0:T(8,128)S(1)} %bitcast_convert_fusion.refs_2_), custom_call_target="tpu_custom_call" | custom-call | tf_op jit(solution)/shard_map/turn10/pallas_call | solution.py:449
  509.4 13.1 %attend_back.1 = (f32[512,384]{1,0:T(8,128)}, f32[1536,384]{1,0:T(8,128)}, f32[1536,384]{1,0:T(8,128)}) custom-call(bf16[512,384]{1,0:T(8,128)(2,1)} %copy-done.19, bf16[1536,384]{1,0:T(8,128)(2,1)} %copy-done, bf16[1536,384]{1,0:T(8,128)(2,1)} %copy-done.1, bf16[512,1536]{1,0:T(8,128)(2,1)} %select_convert_fusion.bias, f32[512,384]{1,0:T(8,128)} %get-tuple-element.83.lse, ...), custom_call_target="tpu_custom_call" | custom-call | tf_op jit(solution)/shard_map/attend_back/pallas_call | solution.py:1086
  525.3 81.2 %keys_back.1 = bf16[512,1152]{1,0:T(8,128)(2,1)S(1)} custom-call(f32[512,384]{1,0:T(8,128)S(1)} %copy-done.21, f32[1536,384]{1,0:T(8,128)S(1)} %copy-done.11, f32[1536,384]{1,0:T(8,128)} %get-tuple-element.87.dv, f32[512,128]{1,0:T(8,128)S(1)} %copy-done.8, f32[512,128]{1,0:T(8,128)S(1)} %copy-done.10), custom_call_target="tpu_custom_call" | custom-call | tf_op jit(solution)/shard_map/keys_back/pallas_call | solution.py:662
  608.9 34.7 %turn12.1 = (f32[128,1536]{1,0:T(8,128)S(1)}, bf16[512,1536]{1,0:T(8,128)(2,1)S(1)}) custom-call(bf16[512,1536]{1,0:T(8,128)(2,1)S(1)} %convolution_convert_fusion.7.refs_0_, f32[128,1536]{1,0:T(8,128)S(1)} %copy-done.4, f32[128,1536]{1,0:T(8,128)S(1)} %copy-done.26), custom_call_target="tpu_custom_call" | custom-call | tf_op jit(solution)/shard_map/turn12/pallas_call | solution.py:449
  649.5 33.4 %turn13.1 = (f32[128,1536]{1,0:T(8,128)S(1)}, bf16[512,1536]{1,0:T(8,128)(2,1)S(1)}) custom-call(bf16[512,1536]{1,0:T(8,128)(2,1)S(1)} %convolution_convert_fusion.9.refs_0_, f32[128,1536]{1,0:T(8,128)S(1)} %get-tuple-element.72.refs_1_, f32[128,1536]{1,0:T(8,128)S(1)} %get-tuple-element.90.refs_2_), custom_call_target="tpu_custom_call" | custom-call | tf_op jit(solution)/shard_map/turn13/pallas_call | solution.py:449
  705.6 9.6 scan_three.1
  716.0 11.3 chain14.1.g_in
  727.9 39.3 %scan_four.1 = (f32[512,768]{1,0:T(8,128)}, f32[512,768]{1,0:T(8,128)}, f32[8192,128]{1,0:T(8,128)}, f32[8192,128]{1,0:T(8,128)}, f32[16,768]{1,0:T(8,128)}) custom-call(f32[512,768]{1,0:T(8,128)} %get-tuple-element.211.delta, f32[512,768]{1,0:T(8,128)} %get-tuple-element.68.u, f32[512,768]{1,0:T(8,128)} %get-tuple-element.195.dy, ...), custom_call_target="tpu_custom_call" | custom-call | tf_op jit(solution)/shard_map/scan_four/pallas_call | solution.py:996
  787.0 7.9 conv_back.1
  813.0 8.1 convolution_convert_fusion
  821.6 8.2 convolution_convert_fusion.1
  831.8 19.3 %small_sum.1 = f32[96,256]{1,0:T(8,128)S(1)} custom-call(bf16[8,96,256]{2,1,0:T(8,128)(2,1)S(1)} %bitcast.105), custom_call_target="tpu_custom_call" | custom-call | tf_op jit(solution)/shard_map/small_sum/pallas_call | solution.py:739
  868.5 27.3 %turn17.1 = f32[128,1536]{1,0:T(8,128)S(1)} custom-call(bf16[512,1536]{1,0:T(8,128)(2,1)S(1)} %copy-done.16, f32[128,1536]{1,0:T(8,128)S(1)} %bitcast_convert_fusion.1.refs_1_, f32[128,1536]{1,0:T(8,128)S(1)} %copy-done.28), custom_call_target="tpu_custom_call" | custom-call | tf_op jit(solution)/shard_map/turn17/pallas_call | solution.py:449
  895.9 21.3 %turn9.1 = bf16[128,1536]{1,0:T(8,128)(2,1)S(1)} custom-call(bf16[512,1536]{1,0:T(8,128)(2,1)S(1)} %copy-done.15, f32[128,1536]{1,0:T(8,128)S(1)} %get-tuple-element.82.refs_1_), custom_call_target="tpu_custom_call" | custom-call | tf_op jit(solution)/shard_map/turn9/pallas_call | solution.py:449
  925.5 11.9 %spread20.1 = bf16[4,48,1536]{2,1,0:T(8,128)(2,1)S(1)} custom-call(bf16[4,48,1536]{2,1,0:T(8,128)(2,1)S(1)} %bitcast.111), custom_call_target="tpu_custom_call" | custom-call | tf_op jit(solution)/shard_map/spread20/pallas_call | solution.py:304
  949.8 44.3 %reduce-scatter.17.cloned.1.call-done = bf16[192,2048]{1,0:T(8,128)(2,1)} async-done(((bf16[1536,2048]{1,0:T(8,128)(2,1)}), bf16[192,2048]{1,0:T(8,128)(2,1)}) %reduce-scatter.17.cloned.1.call-update) | async-done | bytes 786448 | tf_op jit(solution)/shard_map/reduce_scatter | solution.py:1114
  994.2 70.4 %reduce-scatter.13.cloned.1.call-done = bf16[192,2048]{1,0:T(8,128)(2,1)} async-done(((bf16[1536,2048]{1,0:T(8,128)(2,1)}), bf16[192,2048]{1,0:T(8,128)(2,1)}) %reduce-scatter.13.cloned.1.call-update) | async-done | bytes 786448 | tf_op jit(solution)/shard_map/reduce_scatter | solution.py:1114
  1067.9 28.4 %spread19.1 = (bf16[4,48,2048]{2,1,0:T(8,128)(2,1)S(1)}, bf16[4,48,1152]{2,1,0:T(8,128)(2,1)S(1)}, bf16[4,48,2048]{2,1,0:T(8,128)(2,1)S(1)}) custom-call(bf16[4,48,2048]{2,1,0:T(8,128)(2,1)S(1)} %bitcast.110, bf16[4,48,1152]{2,1,0:T(8,128)(2,1)S(1)} %bitcast.113, bf16[4,48,2048]{2,1,0:T(8,128)(2,1)S(1)} %bitcast.109), custom_call_target="tpu_custom_call" | custom-call | tf_op jit(solution)/shard_map/spread19/pallas_call | solution.py:304
  (385 shorter events, 270.4 us)
Async XLA Ops:
  7.2 143.4 %all-gather.9.cloned.1.call-start = ((), (), s32[]{:S(2)}) async-start(), calls=%async_computation.8 | async-start | bytes 5308416 | tf_op jit(solution)/shard_map/all_gather | solution.py:1110
  11.0 35.0 %copy-start.82 = (bf16[48]{0:T(256)(128)(2,1)S(1)}, bf16[48]{0:T(256)(128)(2,1)}, u32[]{:S(2)}) copy-start(bf16[48]{0:T(256)(128)(2,1)} %param.35) | copy-start | bytes 292
  45.2 128.6 %copy-start.12 = (bf16[8,96,256]{2,1,0:T(8,128)(2,1)}, bf16[8,96,256]{2,1,0:T(8,128)(2,1)S(1)}, u32[]{:S(2)}) copy-start(bf16[8,96,256]{2,1,0:T(8,128)(2,1)S(1)} %get-tuple-element.66) | copy-start | bytes 1179652
  45.2 174.0 %all-gather.11.cloned.1.call-start = ((), (), s32[]{:S(2)}) async-start(), calls=%async_computation.9 | async-start | bytes 2654208 | tf_op jit(solution)/shard_map/all_gather | solution.py:1110
  46.0 215.1 %all-gather.13.cloned.1.call-start = ((), (), s32[]{:S(2)}) async-start(), calls=%async_computation.10 | async-start | bytes 7077888 | tf_op jit(solution)/shard_map/all_gather | solution.py:1110
  68.7 27.6 %copy-start.81 = (bf16[48,1536]{1,0:T(8,128)(2,1)S(1)}, bf16[48,1536]{1,0:T(8,128)(2,1)}, u32[]{:S(2)}) copy-start(bf16[48,1536]{1,0:T(8,128)(2,1)} %param.40) | copy-start | bytes 442372
  95.1 175.8 %all-gather.15.cloned.1.call-start = ((), (), s32[]{:S(2)}) async-start(), calls=%async_computation.11 | async-start | bytes 3538944 | tf_op jit(solution)/shard_map/all_gather | solution.py:1110
  95.6 216.8 %all-gather.17.cloned.1.call-start = ((), (), s32[]{:S(2)}) async-start(), calls=%async_computation.12 | async-start | bytes 3981312 | tf_op jit(solution)/shard_map/all_gather | solution.py:1110
  96.2 300.2 %all-gather.19.cloned.1.call-start = ((), (), s32[]{:S(2)}) async-start(), calls=%async_computation.13 | async-start | bytes 1327104 | tf_op jit(solution)/shard_map/all_gather | solution.py:1110
  96.3 0.7 collective-permute-start
  97.6 335.8 %all-gather.21.cloned.1.call-start = ((), (), s32[]{:S(2)}) async-start(), calls=%async_computation.14 | async-start | bytes 7077888 | tf_op jit(solution)/shard_map/all_gather | solution.py:1110
  98.4 355.8 %all-gather.23.cloned.1.call-start = ((), (), s32[]{:S(2)}) async-start(), calls=%async_computation.15 | async-start | bytes 3538944 | tf_op jit(solution)/shard_map/all_gather | solution.py:1110
  99.2 763.6 %reduce-scatter.21.cloned.1.call-start = ((), (), s32[]{:S(2)}) async-start(), calls=%async_computation.22 | async-start | bytes 1327104 | tf_op jit(solution)/shard_map/reduce_scatter | solution.py:1114
  147.8 169.3 %copy-start.7 = (f32[512,128]{1,0:T(8,128)}, f32[512,128]{1,0:T(8,128)S(1)}, u32[]{:S(2)}) copy-start(f32[512,128]{1,0:T(8,128)S(1)} %get-tuple-element.228.cosine) | copy-start | bytes 786436
  147.8 169.3 %copy-start.9 = (f32[512,128]{1,0:T(8,128)}, f32[512,128]{1,0:T(8,128)S(1)}, u32[]{:S(2)}) copy-start(f32[512,128]{1,0:T(8,128)S(1)} %get-tuple-element.229.sine) | copy-start | bytes 786436
  200.3 16.6 %copy-start.43 = (f32[512,768]{1,0:T(8,128)S(1)}, f32[512,768]{1,0:T(8,128)}, u32[]{:S(2)}) copy-start(f32[512,768]{1,0:T(8,128)} %get-tuple-element.68.u) | copy-start | bytes 4718596
  464.9 39.1 %copy-start.58 = (bf16[512,384]{1,0:T(8,128)(2,1)S(1)}, bf16[512,384]{1,0:T(8,128)(2,1)}, u32[]{:S(2)}) copy-start(bf16[512,384]{1,0:T(8,128)(2,1)} %get-tuple-element.78) | copy-start | bytes 1179652
  505.9 412.8 %reduce-scatter.11.cloned.1.call-start = ((), (), s32[]{:S(2)}) async-start(), calls=%async_computation.17 | async-start | bytes 2654208 | tf_op jit(solution)/shard_map/reduce_scatter | solution.py:1114
  525.3 81.3 %copy-start.79 = (bf16[1536,1152]{1,0:T(8,128)(2,1)S(1)}, bf16[1536,1152]{1,0:T(8,128)(2,1)}, u32[]{:S(2)}) copy-start(bf16[1536,1152]{1,0:T(8,128)(2,1)} %all-gather.17.cloned.1.call-done) | copy-start | bytes 10616836
  606.6 37.0 %copy-start.45 = (f32[512,2048]{1,0:T(8,128)S(1)}, f32[512,2048]{1,0:T(8,128)}, u32[]{:S(2)}) copy-start(f32[512,2048]{1,0:T(8,128)} %copy-done.44) | copy-start | bytes 12582916
  608.9 34.7 %copy-start.80 = (bf16[1024,1536]{1,0:T(8,128)(2,1)S(1)}, bf16[1024,1536]{1,0:T(8,128)(2,1)}, u32[]{:S(2)}) copy-start(bf16[1024,1536]{1,0:T(8,128)(2,1)} %all-gather.15.cloned.1.call-done) | copy-start | bytes 9437188
  608.9 37.1 %slice-start = ((s8[6291456]{0:T(1024)(128)(4,1)}), s8[4194304]{0:T(1024)(128)(4,1)S(1)}, s32[]{:S(2)}) async-start(s8[6291456]{0:T(1024)(128)(4,1)} %bitcast.130), calls=%async_computation.24 | async-start | bytes 8388608
  649.5 35.5 %copy-start.54 = (bf16[512,768]{1,0:T(8,128)(2,1)S(1)}, bf16[512,768]{1,0:T(8,128)(2,1)}, u32[]{:S(2)}) copy-start(bf16[512,768]{1,0:T(8,128)(2,1)} %copy-done.53) | copy-start | bytes 2359300
  687.8 232.7 %reduce-scatter.19.cloned.1.call-start = ((), (), s32[]{:S(2)}) async-start(), calls=%async_computation.21 | async-start | bytes 3538944 | tf_op jit(solution)/shard_map/reduce_scatter | solution.py:1114
  693.2 229.2 %reduce-scatter.23.cloned.1.call-start = ((), (), s32[]{:S(2)}) async-start(), calls=%async_computation.23 | async-start | bytes 3538944 | tf_op jit(solution)/shard_map/reduce_scatter | solution.py:1114
  698.7 225.8 %reduce-scatter.9.cloned.1.call-start = ((), (), s32[]{:S(2)}) async-start(), calls=%async_computation.16 | async-start | bytes 5308416 | tf_op jit(solution)/shard_map/reduce_scatter | solution.py:1114
  787.0 15.3 %copy-start.85 = (bf16[512,768]{1,0:T(8,128)(2,1)S(1)}, bf16[512,768]{1,0:T(8,128)(2,1)}, u32[]{:S(2)}) copy-start(bf16[512,768]{1,0:T(8,128)(2,1)} %get-tuple-element.200) | copy-start | bytes 2359300
  807.1 142.8 %reduce-scatter.15.cloned.1.call-start = ((), (), s32[]{:S(2)}) async-start(), calls=%async_computation.19 | async-start | bytes 3981312 | tf_op jit(solution)/shard_map/reduce_scatter | solution.py:1114
  813.0 181.2 %reduce-scatter.17.cloned.1.call-start = ((), (), s32[]{:S(2)}) async-start(), calls=%async_computation.20 | async-start | bytes 7077888 | tf_op jit(solution)/shard_map/reduce_scatter | solution.py:1114
  821.1 243.5 %reduce-scatter.13.cloned.1.call-start = ((), (), s32[]{:S(2)}) async-start(), calls=%async_computation.18 | async-start | bytes 7077888 | tf_op jit(solution)/shard_map/reduce_scatter | solution.py:1114
  862.7 55.2 %collective-permute-start.1 = (bf16[48,1536]{1,0:T(8,128)(2,1)}, bf16[48,1536]{1,0:T(8,128)(2,1)S(1)}, u32[]{:S(2)}, u32[]{:S(2)}) collective-permute-start(bf16[48,1536]{1,0:T(8,128)(2,1)} %reduce-scatter.21.cloned.1.call-done), channel_id=1, source_target_pairs={{0,0},{1,1},{8,2},{9,3},{16,4},{17,5},{24,6},{25,7},{2,8},{3,9},{1... | collective-permute-start | bytes 442376 | tf_op jit(solution)/shard_map/ppermute | solution.py:1337
  868.5 27.3 %copy-start.15 = (bf16[512,1536]{1,0:T(8,128)(2,1)S(1)}, bf16[512,1536]{1,0:T(8,128)(2,1)}, u32[]{:S(2)}) copy-start(bf16[512,1536]{1,0:T(8,128)(2,1)} %convolution_convert_fusion.11.refs_0_) | copy-start | bytes 4718596
  (79 other events, 251.6 us)
Sparse Core Ops, SparseCore 0:
  45.4 50.7 all-gather.8
  97.8 33.9 all-gather.10
  134.1 64.2 all-gather.12
  199.9 42.9 all-gather.14
  244.9 40.3 all-gather.16
  286.8 21.5 all-gather.18
  310.0 92.6 all-gather.20
  404.4 49.7 all-gather.22
  506.0 57.6 reduce-scatter.20
  687.9 36.9 reduce-scatter.10
  727.3 39.2 reduce-scatter.18
  768.7 39.9 reduce-scatter.22
  810.9 63.5 reduce-scatter.8
  876.7 46.7 reduce-scatter.14
  925.8 68.3 reduce-scatter.16
  996.4 68.1 reduce-scatter.12

commit v2 on v1

--- a/solution.py
+++ b/solution.py
@@ -96,8 +96,8 @@
 
 
 def start_body(
-    T, x, seg, par, win, nh, seg_out, par_out, win_out, nbuf, zbuf,
-    s_n, r_n, s_h, r_h, s_s, r_s, s_p, r_p, s_w, r_w, s_l,
+    T, x, seg, par, ct, nh, seg_out, par_out, ct_out, nbuf, zbuf,
+    s_n, r_n, s_h, r_h, s_s, r_s, s_p, r_p, s_c, r_c, s_l,
 ):
     t, p, c = here()
     B = x.shape[0]
@@ -109,29 +109,15 @@
             if dt or dp:
                 greet((tt, pp, c))
                 count += 1
-            if dt == 0 or dp == 0:
+            if dp == 0:
                 greet((tt, pp, 1 - c))
                 count += 1
     nbuf[...] = unit(x[...].astype(F32)).astype(BF)
     zbuf[...] = jnp.zeros_like(zbuf)
     arrive(count)
-    half = lax.div(p, 2)
-    slot = lax.rem(p, 2) * 2 + c
-    for q in range(W):
-        mine = (p == q) & (half == c)
-
-        @pl.when(jnp.logical_not(mine))
-        def _():
-            remote(win.at[q], win_out.at[slot], s_w.at[q], r_w.at[slot], (t, q, half)).start()
-
-        @pl.when(mine)
-        def _():
-            pltpu.make_async_copy(win.at[q], win_out.at[slot], s_w.at[q]).start()
-
     rows = pl.ds(pl.multiple_of(HALO + p * B, HALO), B)
+    plain = pl.ds(pl.multiple_of(p * B, B), B)
     copies = []
-    for d in range(1, W):
-        copies.append(remote(nbuf, nh.at[rows], s_n.at[d], r_n.at[d], (t, flip(p, d), c)))
     for dt in range(T):
         for dc in range(2):
             if dt or dc:
@@ -141,6 +127,8 @@
                         (lax.rem(t + dt, T), p, flip(c, dc)),
                     )
                 )
+    for d in range(1, W):
+        copies.append(remote(nbuf, nh.at[rows], s_n.at[d], r_n.at[d], (t, flip(p, d), c)))
     for dt in range(T):
         for dp in range(W):
             if dt or dp:
@@ -150,6 +138,8 @@
                         (lax.rem(t + dt, T), flip(p, dp), c),
                     )
                 )
+    for d in range(1, W):
+        copies.append(remote(ct, ct_out.at[plain], s_c.at[d], r_c.at[d], (t, flip(p, d), c)))
     for copy in copies:
         copy.start()
     last = (p == W - 1) & (t < T - 1)
@@ -168,6 +158,7 @@
         pltpu.make_async_copy(nbuf, nh.at[rows], s_l.at[0]),
         pltpu.make_async_copy(par, par_out.at[t * 2 + c], s_l.at[1]),
         pltpu.make_async_copy(seg, seg_out.at[t * W + p], s_l.at[2]),
+        pltpu.make_async_copy(ct, ct_out.at[plain], s_l.at[4]),
     ]
     for copy in local:
         copy.start()
@@ -192,26 +183,8 @@
     def _():
         rim(0).wait_recv()
 
-    for q in range(W):
-        mine = (p == q) & (half == c)
-
-        @pl.when(jnp.logical_not(mine))
-        def _():
-            remote(win.at[q], win_out.at[slot], s_w.at[q], r_w.at[slot], (t, q, half)).wait_send()
-
-        @pl.when(mine)
-        def _():
-            pltpu.make_async_copy(win.at[q], win_out.at[slot], s_w.at[q]).wait()
-
-    for j in range(W):
-        own = (half == c) & (slot == j)
-
-        @pl.when(jnp.logical_not(own))
-        def _():
-            remote(win.at[0], win_out.at[j], s_w.at[0], r_w.at[j], (t, 0, half)).wait_recv()
-
-
-def start_call(T, x, seg, par, win):
+
+def start_call(T, x, seg, par, ct):
     B, D = x.shape
     return pl.pallas_call(
         functools.partial(start_body, T),
@@ -219,7 +192,7 @@
             out((HALO + W * B, D), BF),
             out((W * T,) + seg.shape, jnp.int32),
             out((2 * T,) + par.shape, BF),
-            out(win.shape, BF),
+            out((W * B, D), BF),
         ),
         in_specs=[vmem(), hbm(), hbm(), hbm()],
         out_specs=(hbm(), hbm(), hbm(), hbm()),
@@ -227,11 +200,11 @@
             pltpu.VMEM((B, D), BF),
             pltpu.VMEM((HALO, D), BF),
             dma(W), dma(W), dma(W), pltpu.SemaphoreType.DMA,
-            dma(T, W), dma(T, W), dma(T, 2), dma(T, 2), dma(W), dma(W), dma(4),
+            dma(T, W), dma(T, W), dma(T, 2), dma(T, 2), dma(W), dma(W), dma(5),
         ],
         compiler_params=talk(0),
         name="start",
-    )(x, seg, par, win)
+    )(x, seg, par, ct)
 
 
 def spread_body(n, back, *refs):
@@ -310,33 +283,6 @@
         compiler_params=talk(cid),
         name="spread%d" % cid,
     )(*arrays)
-
-
-def plane_gather_body(x, o, ss, rs, ls):
-    t, p, c = here()
-    B = x.shape[0]
-    for d in range(1, W):
-        greet((t, flip(p, d), c))
-    arrive(W - 1)
-    rows = o.at[pl.ds(pl.multiple_of(p * B, B), B)]
-    copies = [remote(x, rows, ss.at[d], rs.at[d], (t, flip(p, d), c)) for d in range(1, W)]
-    local = pltpu.make_async_copy(x, rows, ls)
-    for copy in copies + [local]:
-        copy.start()
-    for copy in copies + [local]:
-        copy.wait()
-
-
-def plane_gather(cid, x):
-    return pl.pallas_call(
-        plane_gather_body,
-        out_shape=out((W * x.shape[0], x.shape[1]), x.dtype),
-        in_specs=[hbm()],
-        out_specs=hbm(),
-        scratch_shapes=[dma(W), dma(W), pltpu.SemaphoreType.DMA],
-        compiler_params=talk(cid),
-        name="gather%d" % cid,
-    )(x)
 
 
 def plane_sum_body(x, o, sb, recv, ss, rs):
@@ -524,40 +470,45 @@
     t, p, c = here()
     CH = q.shape[0]
     width = q.shape[1]
-    for d in range(1, hops + 1):
-
-        @pl.when(t >= d)
-        def _():
-            greet((lax.rem(t - d + T, T), p, c))
+
+    @pl.when(t > 0)
+    def _():
+        greet((lax.rem(t - 1 + T, T), p, c))
 
     mine = pl.ds(hops * CH, CH)
     for h in range(width // HD):
         cols = pl.ds(h * HD, HD)
-        q[:, cols] = rope(qkv[:, cols], cosine[...], sine[...]).astype(BF)
         k_all[mine, cols] = rope(
             qkv[:, pl.ds(width + h * HD, HD)], cosine[...], sine[...]
         ).astype(BF)
     v_all[mine, :] = qkv[:, pl.ds(2 * width, width)].astype(BF)
-    arrive_some(jnp.minimum(hops, T - 1 - t))
+
+    @pl.when(t < T - 1)
+    def _():
+        arrive(1)
 
     def send(a, d):
         ref = (k_all, v_all)[a]
         return remote(
-            ref.at[mine],
+            ref.at[pl.ds((hops - d + 1) * CH, CH)],
             ref.at[pl.ds((hops - d) * CH, CH)],
             ss.at[a, d - 1],
             rs.at[a, d - 1],
-            (lax.rem(t + d, T), p, c),
+            (lax.rem(t + 1, T), p, c),
         )
 
     for d in range(1, hops + 1):
-
-        @pl.when(t + d < T)
+        goes = (t < T - 1) & (t >= d - 1)
+
+        @pl.when(goes)
         def _():
             send(0, d).start()
             send(1, d).start()
 
-    for d in range(1, hops + 1):
+        if d == 1:
+            for h in range(width // HD):
+                cols = pl.ds(h * HD, HD)
+                q[:, cols] = rope(qkv[:, cols], cosine[...], sine[...]).astype(BF)
 
         @pl.when(t < d)
         def _():
@@ -569,7 +520,10 @@
             send(0, d).wait_recv()
             send(1, d).wait_recv()
 
-        @pl.when(t + d < T)
+    for d in range(1, hops + 1):
+        goes = (t < T - 1) & (t >= d - 1)
+
+        @pl.when(goes)
         def _():
             send(0, d).wait_send()
             send(1, d).wait_send()
@@ -597,17 +551,10 @@
     t, p, c = here()
     CH = dq.shape[0]
     width = dq.shape[1]
-    for d in range(1, hops + 1):
-
-        @pl.when(t + d < T)
-        def _():
-            greet((lax.rem(t + d, T), p, c))
-
-    for d in range(1, hops + 1):
-        rows = pl.ds((hops - d) * CH, CH)
-        sb[0, d - 1] = dk[rows, :].astype(BF)
-        sb[1, d - 1] = dv[rows, :].astype(BF)
-    arrive_some(jnp.minimum(hops, t))
+
+    @pl.when(t < T - 1)
+    def _():
+        greet((lax.rem(t + 1, T), p, c))
 
     def send(a, d):
         return remote(
@@ -615,46 +562,68 @@
             recv.at[a, d - 1],
             ss.at[a, d - 1],
             rs.at[a, d - 1],
-            (lax.rem(t - d + T, T), p, c),
+            (lax.rem(t - 1 + T, T), p, c),
         )
 
-    for d in range(1, hops + 1):
+    for d in range(hops, 0, -1):
+        rows = pl.ds((hops - d) * CH, CH)
+        k_sum = dk[rows, :]
+        v_sum = dv[rows, :]
+        if d == hops:
+            sb[0, d - 1] = k_sum.astype(BF)
+            sb[1, d - 1] = v_sum.astype(BF)
+
+            @pl.when(t > 0)
+            def _():
+                arrive(1)
+        else:
+
+            @pl.when((t < T - 1) & (t >= d))
+            def _():
+                send(0, d + 1).wait_recv()
+                send(1, d + 1).wait_recv()
+
+            @pl.when((t == T - 1) | (t < d))
+            def _():
+                recv[0, d] = jnp.zeros((CH, width), BF)
+                recv[1, d] = jnp.zeros((CH, width), BF)
+
+            sb[0, d - 1] = (k_sum + recv[0, d].astype(F32)).astype(BF)
+            sb[1, d - 1] = (v_sum + recv[1, d].astype(F32)).astype(BF)
 
         @pl.when(t >= d)
         def _():
             send(0, d).start()
             send(1, d).start()
 
+        if d == hops:
+            for h in range(width // HD):
+                cols = pl.ds(h * HD, HD)
+                dqkv[:, cols] = rope(dq[:, cols], cosine[...], -sine[...]).astype(BF)
+
+    @pl.when(t < T - 1)
+    def _():
+        send(0, 1).wait_recv()
+        send(1, 1).wait_recv()
+
+    @pl.when(t == T - 1)
+    def _():
+        recv[0, 0] = jnp.zeros((CH, width), BF)
+        recv[1, 0] = jnp.zeros((CH, width), BF)
+
     mine = pl.ds(hops * CH, CH)
     for h in range(width // HD):
         cols = pl.ds(h * HD, HD)
-        dqkv[:, cols] = rope(dq[:, cols], cosine[...], -sine[...]).astype(BF)
-    for d in range(1, hops + 1):
-
-        @pl.when(t + d < T)
-        def _():
-            send(0, d).wait_recv()
-            send(1, d).wait_recv()
-
-        @pl.when(t + d >= T)
-        def _():
-            recv[0, d - 1] = jnp.zeros((CH, width), BF)
-            recv[1, d - 1] = jnp.zeros((CH, width), BF)
+        k_sum = dk[mine, cols] + recv[0, 0, :, cols].astype(F32)
+        v_sum = dv[mine, cols] + recv[1, 0, :, cols].astype(F32)
+        dqkv[:, pl.ds(width + h * HD, HD)] = rope(k_sum, cosine[...], -sine[...]).astype(BF)
+        dqkv[:, pl.ds(2 * width + h * HD, HD)] = v_sum.astype(BF)
+    for d in range(hops, 0, -1):
 
         @pl.when(t >= d)
         def _():
             send(0, d).wait_send()
             send(1, d).wait_send()
-
-    for h in range(width // HD):
-        cols = pl.ds(h * HD, HD)
-        k_sum = dk[mine, cols]
-        v_sum = dv[mine, cols]
-        for d in range(hops):
-            k_sum = k_sum + recv[0, d, :, cols].astype(F32)
-            v_sum = v_sum + recv[1, d, :, cols].astype(F32)
-        dqkv[:, pl.ds(width + h * HD, HD)] = rope(k_sum, cosine[...], -sine[...]).astype(BF)
-        dqkv[:, pl.ds(2 * width + h * HD, HD)] = v_sum.astype(BF)
 
 
 def keys_back_call(cid, T, hops, dq, dk, dv, cosine, sine):
@@ -1110,6 +1079,10 @@
     return lax.all_gather(x.reshape(-1, x.shape[-1]), ("t", "c"), axis=0, tiled=True)
 
 
+def together(*values):
+    return lax.optimization_barrier(values)
+
+
 def scatter_tc(x):
     return lax.psum_scatter(x, ("t", "c"), scatter_dimension=0, tiled=True)
 
@@ -1160,8 +1133,9 @@
     win_out = columns_out(in_proj, norm_mixer, 2, T, 2 * CB)
     seg8 = jnp.broadcast_to(segment_ids, (8, B))
     x0 = inputs[0].astype(F32)
-    nh1_ext, seg_all, par_all, win_mine = start_call(T, inputs[0], seg8, par, win_out)
+    (win_mine,) = spread_call(21, False, (win_out,))
     w_in = gather_tc(win_mine)
+    nh1_ext, seg_all, par_all, gl4 = start_call(T, inputs[0], seg8, par, cotangent[0])
 
     gu1_out = columns_out(gate_up_one, norm_ffn_one, 2, T, 2 * FB)
     qkv_out = columns_out(qkv_proj, norm_attn, 3, 1, heads)
@@ -1180,7 +1154,6 @@
     w_ao = gather_tc(ao_mine)
     w_gu2 = gather_tc(gu2_mine)
     w_d2 = gather_tc(down_two)
-    gl4 = plane_gather(2, cotangent[0])
 
     seg = seg_all[:, 0, :].reshape(total)
     pos = t * CH + jnp.arange(CH, dtype=jnp.int32)
@@ -1268,29 +1241,41 @@
     (final,) = turn(9, nn(h_two, w_d2).astype(BF), x3, gather=False, dtype=BF)
 
     g4 = cotangent[0].astype(F32)
+    dw_d2 = tn(h_two, gl4).astype(BF)
     da_two = swiglu_back(a_two, nt(gl4, w_d2))
-    g3, gl3 = turn(10, nt(da_two, w_gu2).astype(BF), x3, g4)
-    grad_d2 = scatter_tc(tn(h_two, gl4).astype(BF))
-    raw_gu2 = scatter_tc(tn(nh4, da_two).astype(BF))
-
-    do = nt(gl3, w_ao).astype(BF)
+    da_two, dw_d2 = together(da_two, dw_d2)
+    grad_d2 = scatter_tc(dw_d2)
+    part, dw_gu2 = together(nt(da_two, w_gu2).astype(BF), tn(nh4, da_two).astype(BF))
+    g3, gl3 = turn(10, part, x3, g4)
+    raw_gu2 = scatter_tc(dw_gu2)
+
+    do, dw_ao = together(nt(gl3, w_ao).astype(BF), tn(o, gl3).astype(BF))
+    raw_ao = scatter_tc(dw_ao)
     dq, dk, dv = attend_back(q, k_all, v_all, bias, lse, do)
+    dq, grad_d2 = together(dq, grad_d2)
     dqkv = keys_back_call(11, T, hops, dq, dk, dv, cosine, sine)
-    g2, gl2 = turn(12, nt(dqkv, w_qkv).astype(BF), x2, g3)
-    raw_ao = scatter_tc(tn(o, gl3).astype(BF))
-    raw_qkv = scatter_tc(tn(nh3, dqkv).astype(BF))
-
-    da_one = swiglu_back(a_one, nt(gl2, w_d1))
-    g1, gl1 = turn(13, nt(da_one, w_gu1).astype(BF), x1, g2)
-    grad_d1 = scatter_tc(tn(h_one, gl2).astype(BF))
-    raw_gu1 = scatter_tc(tn(nh2, da_one).astype(BF))
+    part, dw_qkv = together(nt(dqkv, w_qkv).astype(BF), tn(nh3, dqkv).astype(BF))
+    raw_qkv = scatter_tc(dw_qkv)
+    part, raw_gu2 = together(part, raw_gu2)
+    g2, gl2 = turn(12, part, x2, g3)
+    gl2, raw_ao = together(gl2, raw_ao)
+
+    da_one, dw_d1 = together(swiglu_back(a_one, nt(gl2, w_d1)), tn(h_one, gl2).astype(BF))
+    grad_d1 = scatter_tc(dw_d1)
+    part, dw_gu1 = together(nt(da_one, w_gu1).astype(BF), tn(nh2, da_one).astype(BF))
+    raw_gu1 = scatter_tc(dw_gu1)
+    g1, gl1 = turn(13, part, x1, g2)
+    gl1, raw_qkv = together(gl1, raw_qkv)
 
     dgate = nt(gl1, w_mix)
     dy = dgate * zg * gate_s
     dz_low = (dgate * y * gate_s * (1.0 + zg * (1.0 - gate_s))).astype(BF)
-    grad_mix = scatter_tc(tn(gated, gl1).astype(BF))
+    dy, dw_mix, dw_z = together(dy, tn(gated, gl1).astype(BF), tn(nh1, dz_low).astype(BF))
+    grad_mix = scatter_tc(dw_mix)
+    raw_z = scatter_tc(dw_z)
     begin = scan_three(delta, dy, a2, crep, first)
     g_in = chain(14, T, True, packed(begin), a2)
+    g_in, grad_d1 = together(g_in, grad_d1)
     ddelta, du_scan, db, dc_mat, ga = scan_four(
         delta, u, dy, skip_row, a2, brep, crep, first, marks, g_in
     )
@@ -1304,6 +1289,7 @@
         ],
         axis=1,
     )
+    part_back, raw_gu1 = together(part_back, raw_gu1)
     dpr_low = plane_sum(15, part_back).astype(BF)
     du = du_scan + nt(dpr_low, w_state)
     dxs_ext, conv_grads = conv_back_call(xz, conv_mask, taps, du)
@@ -1312,7 +1298,8 @@
         [dxs_ext[HALO : HALO + CH - 8], dxs_ext[HALO + CH - 8 :] + rim], axis=0
     ).astype(BF)
     dxz = jnp.concatenate([dxs_low, dz_low], axis=1)
-    raw_in = scatter_tc(tn(nh1, dxz).astype(BF))
+    dxz, dw_x, grad_mix = together(dxz, tn(nh1, dxs_low).astype(BF), grad_mix)
+    raw_x = scatter_tc(dw_x)
     (grad_x,) = turn(17, nt(dxz, w_in).astype(BF), x0, g1, gather=False)
 
     small = jnp.concatenate(
@@ -1327,13 +1314,17 @@
         axis=1,
     )
     small = jnp.pad(small, ((0, 0), (0, 256 - used))).astype(BF).reshape(2 * T, CB, 256)
+    small, raw_z = together(small, raw_z)
     small = small_sum(18, T, small)
 
     def blocks(x):
         return x.reshape(W, x.shape[0] // W, x.shape[1])
 
-    gu2_b, qkv_b, gu1_b = spread_call(19, True, (blocks(raw_gu2), blocks(raw_qkv), blocks(raw_gu1)))
-    (in_b,) = spread_call(20, True, (blocks(raw_in),))
+    gu2_b, qkv_b, gu1_b, z_b = spread_call(
+        19, True, (blocks(raw_gu2), blocks(raw_qkv), blocks(raw_gu1), blocks(raw_z))
+    )
+    (x_b,) = spread_call(20, True, (blocks(raw_x),))
+    in_b = jnp.concatenate([x_b, z_b], axis=2)
     grad_ao = lax.ppermute(raw_ao, ("t", "p", "c"), [(b, a) for a, b in pairs]).astype(F32)
 
     def finished(blocks_in, weight, gain, groups, groups_t, cols):

time: 1150 us -> 1040 us (0.904)
  waiting for transfers between devices: 130 us -> 53.9 us
  Pallas kernels: 715 us -> 663 us
  matrix products: 124 us -> 139 us
    reduce_scatter x8 -> x9, waiting for transfers between devices: 115 us -> 5.12 us  [scatter_tc(): return lax.psum_scatter(x, ('t', 'c'), scatter_dimension=0, tiled=True)]
    pallas_call x1 -> x0, Pallas kernels: 40.3 us -> none  [plane_gather(): pl.pallas_call(plane_gather_body, out_shape=out((W * x.shape[0], x.shape[...]
    pallas_call x1, Pallas kernels: 67.4 us -> 27.6 us  [keys_call(): pl.pallas_call(functools.partial(keys_body, T, hops), out_shape=(out((CH,...]
    all_gather x8, waiting for transfers between devices: 12 us -> 44.9 us  [gather_tc(): lax.all_gather(x.reshape(-1, x.shape[-1]), ('t', 'c'), axis=0, tiled=True)]
    pallas_call x1, Pallas kernels: 32.4 us -> 64.9 us  [start_call(): pl.pallas_call(functools.partial(start_body, T), out_shape=(out((HALO + W...]
    pallas_call x8, Pallas kernels: 259 us -> 239 us  [turn(): pl.pallas_call(functools.partial(turn_body, back, gather, parts), out_sha...]
    dot_general x10, matrix products: 37.1 us -> 54 us  [nt(): lax.dot_general(a, b, (((1,), (1,)), ((), ())), preferred_element_type=F32)]
    pallas_call x2, Pallas kernels: 18.9 us -> 35.4 us  [chain(): pl.pallas_call(functools.partial(chain_body, T, back), out_shape=out(a2.s...]
  transfers between devices with their start and end apart: 18 -> 19, of which waited for: 3 -> 2; matrix products, arithmetic and copies ran while one was open for 17% -> 21% of each run, Pallas kernels for 54% -> 63%
where the time goes in v2:
time: 1040 us; the launch traced here: 1030 us
  Pallas kernels  663 us (64%)
  matrix products  139 us (13%)
  local copies, waits for them, and re-layouts  103 us (10%)
  waiting for transfers between devices  53.9 us (5%)
  other arithmetic  46.8 us (4%)
  between operations  16.4 us (2%)
    pallas_call x8, Pallas kernels, turn(): pl.pallas_call(functools.partial(turn_body, back, gather, parts), out_sha...  239 us
    pallas_call x1, Pallas kernels, keys_back_call(): pl.pallas_call(functools.partial(keys_back_body, T, hops), out_shape=out(...  79.9 us
    pallas_call x4, Pallas kernels, spread_call(): pl.pallas_call(functools.partial(spread_body, n, back), out_shape=tuple((...  73.5 us
    pallas_call x1, Pallas kernels, start_call(): pl.pallas_call(functools.partial(start_body, T), out_shape=(out((HALO + W...  64.9 us
    dot_general x10, matrix products, nt(): lax.dot_general(a, b, (((1,), (1,)), ((), ())), preferred_element_type=F32)  54 us
    unnamed x210, local copies, waits for them, and re-layouts  47.1 us
    all_gather x8, waiting for transfers between devices, gather_tc(): lax.all_gather(x.reshape(-1, x.shape[-1]), ('t', 'c'), axis=0, tiled=True)  44.9 us
    dot_general x9, matrix products, nn(): return jnp.dot(a, b, preferred_element_type=F32)  42.9 us
  transfers between devices with their start and end apart: 19, of which 2 were waited for; matrix products, arithmetic and copies ran while one was open for 21% of the time, Pallas kernels for 63%

profile of v2, /device:TPU:1, one launch (start us, length us, event | category | flops | bytes accessed | tf_op | source)
XLA Modules:
  0.0 1025.2 jit_solution(5405002687525122855)
XLA Ops:
  11.8 10.8 %spread21.1 = bf16[4,48,1536]{2,1,0:T(8,128)(2,1)} custom-call(bf16[4,48,1536]{2,1,0:T(8,128)(2,1)S(1)} %reshape.285.refs_0_), custom_call_target="tpu_custom_call" | custom-call | tf_op jit(solution)/shard_map/spread21/pallas_call | solution.py:277
  29.3 25.1 %spread1.1 = (bf16[4,48,2048]{2,1,0:T(8,128)(2,1)}, bf16[4,48,1152]{2,1,0:T(8,128)(2,1)}, bf16[4,48,2048]{2,1,0:T(8,128)(2,1)}) custom-call(bf16[4,48,2048]{2,1,0:T(8,128)(2,1)S(1)} %reshape.289.refs_0_, bf16[4,48,1152]{2,1,0:T(8,128)(2,1)S(1)} %reshape.291.refs_1_, bf16[4,48,2048]{2,1,0:T(8,128)(2,1)S(1)} %reshape.293.refs_2_), custom_call_target="tpu_custom_call" | custom-call | tf_op jit(solution)/shard_map/spread1/pallas_call | solution.py:277
  59.7 64.9 %start.1 = (bf16[528,1536]{1,0:T(8,128)(2,1)S(1)}, s32[16,8,128]{2,1,0:T(8,128)S(1)}, bf16[8,96,256]{2,1,0:T(8,128)(2,1)S(1)}, bf16[512,1536]{1,0:T(8,128)(2,1)S(1)}) custom-call(bf16[128,1536]{1,0:T(8,128)(2,1)S(1)} %bitcast.111, s32[8,128]{1,0:T(8,128)S(1)} %broadcast_in_dim.87.seg, bf16[96,256]{1,0:T(8,128)(2,1)S(1)} %pad.17.par, ...), custom_call_target="tpu_custom_call" | custom-call | tf_op jit(solution)/shard_map/start/pallas_call | solution.py:189
  151.3 8.1 plane_sum3.1
  165.2 9.8 scan_one.1
  175.9 10.2 chain4.1.h_in
  188.7 16.6 %scan_two.1 = (f32[512,768]{1,0:T(8,128)}, f32[128,768]{1,0:T(8,128)}) custom-call(f32[512,768]{1,0:T(8,128)} %get-tuple-element.276.delta, f32[512,768]{1,0:T(8,128)} %get-tuple-element.100.u, f32[16,768]{1,0:T(8,128)} %fusion.30.a2, f32[8192,128]{1,0:T(8,128)} %broadcast_in_dim.92.brep, f32[8192,128]{1,0:T(8,128)} %broadcast_in_dim.94.crep, ...), custom_call_target="tpu_custom_call" | custom-call | tf_op jit(solution)/shard_map/scan_two/pallas_call | solution.py:854
  211.6 35.7 %turn5.1 = (f32[128,1536]{1,0:T(8,128)S(1)}, bf16[512,1536]{1,0:T(8,128)(2,1)S(1)}) custom-call(bf16[512,1536]{1,0:T(8,128)(2,1)S(1)} %convolution_convert_fusion.15.refs_0_, f32[128,1536]{1,0:T(8,128)S(1)} %bitcast_convert_fusion.1.refs_1_), custom_call_target="tpu_custom_call" | custom-call | tf_op jit(solution)/shard_map/turn5/pallas_call | solution.py:395
  262.3 34.7 %turn6.1 = (f32[128,1536]{1,0:T(8,128)S(1)}, bf16[512,1536]{1,0:T(8,128)(2,1)S(1)}) custom-call(bf16[512,1536]{1,0:T(8,128)(2,1)S(1)} %convolution_convert_fusion.14.refs_0_, f32[128,1536]{1,0:T(8,128)S(1)} %get-tuple-element.104.refs_1_), custom_call_target="tpu_custom_call" | custom-call | tf_op jit(solution)/shard_map/turn6/pallas_call | solution.py:395
  302.9 27.6 %keys.1 = (bf16[512,384]{1,0:T(8,128)(2,1)S(1)}, bf16[1536,384]{1,0:T(8,128)(2,1)S(1)}, bf16[1536,384]{1,0:T(8,128)(2,1)S(1)}) custom-call(f32[512,1152]{1,0:T(8,128)S(1)} %fusion.71.qkv, f32[512,128]{1,0:T(8,128)S(1)} %get-tuple-element.293.cosine, f32[512,128]{1,0:T(8,128)S(1)} %get-tuple-element.294.sine), custom_call_target="tpu_custom_call" | custom-call | tf_op jit(solution)/shard_map/keys/pallas_call | solution.py:535
  333.3 9.2 attend.1
  344.9 27.4 %turn8.1 = (f32[128,1536]{1,0:T(8,128)S(1)}, bf16[512,1536]{1,0:T(8,128)(2,1)S(1)}) custom-call(bf16[512,1536]{1,0:T(8,128)(2,1)S(1)} %convolution_convert_fusion.13.refs_0_, f32[128,1536]{1,0:T(8,128)S(1)} %get-tuple-element.111.refs_1_), custom_call_target="tpu_custom_call" | custom-call | tf_op jit(solution)/shard_map/turn8/pallas_call | solution.py:395
  373.5 8.7 fusion.72
  382.2 44.9 %all-gather.23.cloned.1.call-done = bf16[1024,1536]{1,0:T(8,128)(2,1)} async-done(((bf16[128,1536]{1,0:T(8,128)(2,1)}), bf16[1024,1536]{1,0:T(8,128)(2,1)}) %all-gather.23.cloned.1.call-update) | async-done | bytes 3145744 | tf_op jit(solution)/shard_map/all_gather | solution.py:1079
  427.0 7.6 multiply_convert_fusion.3
  442.5 8.1 convolution_convert_fusion.1
  450.6 8.0 convolution_convert_fusion.11.refs_0_
  461.2 37.1 %turn10.1 = (f32[128,1536]{1,0:T(8,128)S(1)}, bf16[512,1536]{1,0:T(8,128)(2,1)S(1)}) custom-call(bf16[512,1536]{1,0:T(8,128)(2,1)S(1)} %copy-done.13, f32[128,1536]{1,0:T(8,128)S(1)} %get-tuple-element.114.refs_1_, f32[128,1536]{1,0:T(8,128)S(1)} %bitcast_convert_fusion.refs_2_), custom_call_target="tpu_custom_call" | custom-call | tf_op jit(solution)/shard_map/turn10/pallas_call | solution.py:395
  505.9 13.2 %attend_back.1 = (f32[512,384]{1,0:T(8,128)}, f32[1536,384]{1,0:T(8,128)}, f32[1536,384]{1,0:T(8,128)}) custom-call(bf16[512,384]{1,0:T(8,128)(2,1)} %copy-done.16, bf16[1536,384]{1,0:T(8,128)(2,1)} %copy-done, bf16[1536,384]{1,0:T(8,128)(2,1)} %copy-done.1, bf16[512,1536]{1,0:T(8,128)(2,1)} %select_convert_fusion.bias, f32[512,384]{1,0:T(8,128)} %get-tuple-element.115.lse, ...), custom_call_target="tpu_custom_call" | custom-call | tf_op jit(solution)/shard_map/attend_back/pallas_call | solution.py:1055
  523.8 79.9 %keys_back.1 = bf16[512,1152]{1,0:T(8,128)(2,1)} custom-call(f32[512,384]{1,0:T(8,128)S(1)} %copy-done.17, f32[1536,384]{1,0:T(8,128)S(1)} %copy-done.8, f32[1536,384]{1,0:T(8,128)} %get-tuple-element.125.dv, f32[512,128]{1,0:T(8,128)S(1)} %copy-done.5, f32[512,128]{1,0:T(8,128)S(1)} %copy-done.7), custom_call_target="tpu_custom_call" | custom-call | tf_op jit(solution)/shard_map/keys_back/pallas_call | solution.py:631
  617.3 32.7 %turn12.1 = (f32[128,1536]{1,0:T(8,128)S(1)}, bf16[512,1536]{1,0:T(8,128)(2,1)S(1)}) custom-call(bf16[512,1536]{1,0:T(8,128)(2,1)S(1)} %copy-done.11, f32[128,1536]{1,0:T(8,128)S(1)} %get-tuple-element.111.refs_1_, f32[128,1536]{1,0:T(8,128)S(1)} %copy-done.21), custom_call_target="tpu_custom_call" | custom-call | tf_op jit(solution)/shard_map/turn12/pallas_call | solution.py:395
  664.5 8.3 convolution_convert_fusion
  672.8 8.1 convolution_convert_fusion.10.refs_0_
  683.5 31.8 %turn13.1 = (f32[128,1536]{1,0:T(8,128)S(1)}, bf16[512,1536]{1,0:T(8,128)(2,1)S(1)}) custom-call(bf16[512,1536]{1,0:T(8,128)(2,1)S(1)} %copy-done.12, f32[128,1536]{1,0:T(8,128)S(1)} %get-tuple-element.104.refs_1_, f32[128,1536]{1,0:T(8,128)S(1)} %copy-done.23), custom_call_target="tpu_custom_call" | custom-call | tf_op jit(solution)/shard_map/turn13/pallas_call | solution.py:395
  732.5 10.1 scan_three.1
  743.5 25.1 %chain14.1.g_in = f32[16,768]{1,0:T(8,128)S(1)} custom-call(f32[24,768]{1,0:T(8,128)S(1)} %fusion.26.v, f32[16,768]{1,0:T(8,128)S(1)} %copy-done.3), custom_call_target="tpu_custom_call" | custom-call | tf_op jit(solution)/shard_map/chain14/pallas_call | solution.py:454
  769.2 39.3 %scan_four.1 = (f32[512,768]{1,0:T(8,128)}, f32[512,768]{1,0:T(8,128)}, f32[8192,128]{1,0:T(8,128)}, f32[8192,128]{1,0:T(8,128)}, f32[16,768]{1,0:T(8,128)}) custom-call(f32[512,768]{1,0:T(8,128)} %get-tuple-element.276.delta, f32[512,768]{1,0:T(8,128)} %get-tuple-element.100.u, f32[512,768]{1,0:T(8,128)} %get-tuple-element.139.dy, ...), custom_call_target="tpu_custom_call" | custom-call | tf_op jit(solution)/shard_map/scan_four/pallas_call | solution.py:965
  829.8 7.8 conv_back.1
  854.1 20.1 %turn9.1 = bf16[128,1536]{1,0:T(8,128)(2,1)S(1)} custom-call(bf16[512,1536]{1,0:T(8,128)(2,1)S(1)} %convolution_convert_fusion.12.refs_0_, f32[128,1536]{1,0:T(8,128)S(1)} %get-tuple-element.114.refs_1_), custom_call_target="tpu_custom_call" | custom-call | tf_op jit(solution)/shard_map/turn9/pallas_call | solution.py:395
  885.6 13.5 %small_sum.1 = f32[96,256]{1,0:T(8,128)S(1)} custom-call(bf16[8,96,256]{2,1,0:T(8,128)(2,1)S(1)} %bitcast.113), custom_call_target="tpu_custom_call" | custom-call | tf_op jit(solution)/shard_map/small_sum/pallas_call | solution.py:708
  905.4 19.1 %turn17.1 = f32[128,1536]{1,0:T(8,128)S(1)} custom-call(bf16[512,1536]{1,0:T(8,128)(2,1)S(1)} %convolution_convert_fusion.9.refs_0_, f32[128,1536]{1,0:T(8,128)S(1)} %bitcast_convert_fusion.1.refs_1_, f32[128,1536]{1,0:T(8,128)S(1)} %copy-done.28), custom_call_target="tpu_custom_call" | custom-call | tf_op jit(solution)/shard_map/turn17/pallas_call | solution.py:395
  929.5 30.7 %spread19.1 = (bf16[4,48,2048]{2,1,0:T(8,128)(2,1)S(1)}, bf16[4,48,1152]{2,1,0:T(8,128)(2,1)S(1)}, bf16[4,48,2048]{2,1,0:T(8,128)(2,1)S(1)}, bf16[4,48,768]{2,1,0:T(8,128)(2,1)S(1)}) custom-call(bf16[4,48,2048]{2,1,0:T(8,128)(2,1)S(1)} %bitcast.115, bf16[4,48,1152]{2,1,0:T(8,128)(2,1)S(1)} %bitcast.117, bf16[4,48,2048]{2,1,0:T(8,128)(2,1)S(1)} %bitcast.116, ...), custom_call_target="tpu_custom_call" | custom-call | tf_op jit(solution)/shard_map/spread19/pallas_call | solution.py:277
  (407 shorter events, 274.4 us)
Async XLA Ops:
  7.2 130.1 %all-gather.9.cloned.1.call-start = ((), (), s32[]{:S(2)}) async-start(), calls=%async_computation.9 | async-start | bytes 5308416 | tf_op jit(solution)/shard_map/all_gather | solution.py:1079
  10.9 13.0 %copy-start.59 = (bf16[48,8192]{1,0:T(8,128)(2,1)S(1)}, bf16[48,8192]{1,0:T(8,128)(2,1)}, u32[]{:S(2)}) copy-start(bf16[48,8192]{1,0:T(8,128)(2,1)} %param.36) | copy-start | bytes 2359300
  22.6 185.1 %all-gather.11.cloned.1.call-start = ((), (), s32[]{:S(2)}) async-start(), calls=%async_computation.10 | async-start | bytes 2654208 | tf_op jit(solution)/shard_map/all_gather | solution.py:1079
  23.3 225.2 %all-gather.13.cloned.1.call-start = ((), (), s32[]{:S(2)}) async-start(), calls=%async_computation.11 | async-start | bytes 7077888 | tf_op jit(solution)/shard_map/all_gather | solution.py:1079
  29.3 26.5 %copy-start.95 = (bf16[48,1536]{1,0:T(8,128)(2,1)S(1)}, bf16[48,1536]{1,0:T(8,128)(2,1)}, u32[]{:S(2)}) copy-start(bf16[48,1536]{1,0:T(8,128)(2,1)} %param.40) | copy-start | bytes 442372
  54.6 203.7 %all-gather.15.cloned.1.call-start = ((), (), s32[]{:S(2)}) async-start(), calls=%async_computation.12 | async-start | bytes 3538944 | tf_op jit(solution)/shard_map/all_gather | solution.py:1079
  55.1 243.0 %all-gather.17.cloned.1.call-start = ((), (), s32[]{:S(2)}) async-start(), calls=%async_computation.13 | async-start | bytes 3981312 | tf_op jit(solution)/shard_map/all_gather | solution.py:1079
  55.7 286.8 %all-gather.19.cloned.1.call-start = ((), (), s32[]{:S(2)}) async-start(), calls=%async_computation.14 | async-start | bytes 1327104 | tf_op jit(solution)/shard_map/all_gather | solution.py:1079
  55.8 0.7 collective-permute-start
  57.2 316.3 %all-gather.21.cloned.1.call-start = ((), (), s32[]{:S(2)}) async-start(), calls=%async_computation.15 | async-start | bytes 7077888 | tf_op jit(solution)/shard_map/all_gather | solution.py:1079
  57.9 369.1 %all-gather.23.cloned.1.call-start = ((), (), s32[]{:S(2)}) async-start(), calls=%async_computation.16 | async-start | bytes 3538944 | tf_op jit(solution)/shard_map/all_gather | solution.py:1079
  58.7 460.4 %reduce-scatter.10.cloned.1.call-start = ((), (), s32[]{:S(2)}) async-start(), calls=%async_computation.17 | async-start | bytes 3538944 | tf_op jit(solution)/shard_map/reduce_scatter | solution.py:1087
  126.9 33.0 %copy-start.9 = (bf16[8,96,256]{2,1,0:T(8,128)(2,1)}, bf16[8,96,256]{2,1,0:T(8,128)(2,1)S(1)}, u32[]{:S(2)}) copy-start(bf16[8,96,256]{2,1,0:T(8,128)(2,1)S(1)} %get-tuple-element.98) | copy-start | bytes 1179652
  134.4 168.4 %copy-start.4 = (f32[512,128]{1,0:T(8,128)}, f32[512,128]{1,0:T(8,128)S(1)}, u32[]{:S(2)}) copy-start(f32[512,128]{1,0:T(8,128)S(1)} %get-tuple-element.293.cosine) | copy-start | bytes 786436
  134.4 168.4 %copy-start.6 = (f32[512,128]{1,0:T(8,128)}, f32[512,128]{1,0:T(8,128)S(1)}, u32[]{:S(2)}) copy-start(f32[512,128]{1,0:T(8,128)S(1)} %get-tuple-element.294.sine) | copy-start | bytes 786436
  188.7 16.6 %copy-start.53 = (f32[512,768]{1,0:T(8,128)S(1)}, f32[512,768]{1,0:T(8,128)}, u32[]{:S(2)}) copy-start(f32[512,768]{1,0:T(8,128)} %get-tuple-element.100.u) | copy-start | bytes 4718596
  442.3 172.5 %reduce-scatter.12.cloned.1.call-start = ((), (), s32[]{:S(2)}) async-start(), calls=%async_computation.18 | async-start | bytes 7077888 | tf_op jit(solution)/shard_map/reduce_scatter | solution.py:1087
  458.7 193.4 %reduce-scatter.14.cloned.1.call-start = ((), (), s32[]{:S(2)}) async-start(), calls=%async_computation.19 | async-start | bytes 1327104 | tf_op jit(solution)/shard_map/reduce_scatter | solution.py:1087
  461.2 39.2 %copy-start.73 = (bf16[512,384]{1,0:T(8,128)(2,1)S(1)}, bf16[512,384]{1,0:T(8,128)(2,1)}, u32[]{:S(2)}) copy-start(bf16[512,384]{1,0:T(8,128)(2,1)} %get-tuple-element.110) | copy-start | bytes 1179652
  505.8 211.5 %reduce-scatter.16.cloned.1.call-start = ((), (), s32[]{:S(2)}) async-start(), calls=%async_computation.20 | async-start | bytes 3981312 | tf_op jit(solution)/shard_map/reduce_scatter | solution.py:1087
  523.8 79.9 %copy-start.46 = (bf16[512,1536]{1,0:T(8,128)(2,1)S(1)}, bf16[512,1536]{1,0:T(8,128)(2,1)}, u32[]{:S(2)}) copy-start(bf16[512,1536]{1,0:T(8,128)(2,1)} %copy-done.45) | copy-start | bytes 4718596
  614.7 154.5 %reduce-scatter.18.cloned.1.call-start = ((), (), s32[]{:S(2)}) async-start(), calls=%async_computation.21 | async-start | bytes 3538944 | tf_op jit(solution)/shard_map/reduce_scatter | solution.py:1087
  664.1 156.1 %reduce-scatter.20.cloned.1.call-start = ((), (), s32[]{:S(2)}) async-start(), calls=%async_computation.22 | async-start | bytes 7077888 | tf_op jit(solution)/shard_map/reduce_scatter | solution.py:1087
  681.0 167.3 %reduce-scatter.22.cloned.1.call-start = ((), (), s32[]{:S(2)}) async-start(), calls=%async_computation.23 | async-start | bytes 2654208 | tf_op jit(solution)/shard_map/reduce_scatter | solution.py:1087
  731.9 153.8 %reduce-scatter.26.cloned.1.call-start = ((), (), s32[]{:S(2)}) async-start(), calls=%async_computation.25 | async-start | bytes 2654208 | tf_op jit(solution)/shard_map/reduce_scatter | solution.py:1087
  732.5 261.8 %reduce-scatter.24.cloned.1.call-start = ((), (), s32[]{:S(2)}) async-start(), calls=%async_computation.24 | async-start | bytes 2654208 | tf_op jit(solution)/shard_map/reduce_scatter | solution.py:1087
  848.3 27.0 %collective-permute-start.1 = (bf16[48,1536]{1,0:T(8,128)(2,1)}, bf16[48,1536]{1,0:T(8,128)(2,1)S(1)}, u32[]{:S(2)}, u32[]{:S(2)}) collective-permute-start(bf16[48,1536]{1,0:T(8,128)(2,1)} %reduce-scatter.14.cloned.1.call-done), channel_id=1, source_target_pairs={{0,0},{1,1},{8,2},{9,3},{16,4},{17,5},{24,6},{25,7},{2,8},{3,9},{1... | collective-permute-start | bytes 442376 | tf_op jit(solution)/shard_map/ppermute | solution.py:1328
  850.0 24.2 %copy-start.74 = (bf16[128,1536]{1,0:T(8,128)(2,1)S(1)}, bf16[128,1536]{1,0:T(8,128)(2,1)}, u32[]{:S(2)}) copy-start(bf16[128,1536]{1,0:T(8,128)(2,1)} %reduce-scatter.10.cloned.1.call-done) | copy-start | bytes 1179652
  854.1 21.9 %copy-start.54 = (f32[512,768]{1,0:T(8,128)S(1)}, f32[512,768]{1,0:T(8,128)}, u32[]{:S(2)}) copy-start(f32[512,768]{1,0:T(8,128)} %get-tuple-element.100.u) | copy-start | bytes 4718596
  854.1 21.8 %copy-start.55 = (f32[512,768]{1,0:T(8,128)S(1)}, f32[512,768]{1,0:T(8,128)}, u32[]{:S(2)}) copy-start(f32[512,768]{1,0:T(8,128)} %get-tuple-element.139.dy) | copy-start | bytes 4718596
  905.4 23.0 %copy-start.19 = (bf16[192,2048]{1,0:T(8,128)(2,1)S(1)}, bf16[192,2048]{1,0:T(8,128)(2,1)}, u32[]{:S(2)}) copy-start(bf16[192,2048]{1,0:T(8,128)(2,1)} %reduce-scatter.20.cloned.1.call-done) | copy-start | bytes 2359300
  905.4 23.0 %copy-start.32 = (bf16[192,768]{1,0:T(8,128)(2,1)S(1)}, bf16[192,768]{1,0:T(8,128)(2,1)}, u32[]{:S(2)}) copy-start(bf16[192,768]{1,0:T(8,128)(2,1)} %reduce-scatter.26.cloned.1.call-done) | copy-start | bytes 884740
  (87 other events, 232.7 us)
Sparse Core Ops, SparseCore 0:
  22.7 61.7 all-gather.8
  86.1 31.5 all-gather.10
  119.4 67.9 all-gather.12
  188.9 43.0 all-gather.14
  233.5 40.3 all-gather.16
  276.0 21.5 all-gather.18
  299.2 73.5 all-gather.20
  374.4 52.5 all-gather.22
  442.4 64.2 reduce-scatter.9
  508.8 82.9 reduce-scatter.11
  594.1 43.8 reduce-scatter.13
  640.2 43.2 reduce-scatter.15
  685.9 38.4 reduce-scatter.17
  726.6 73.9 reduce-scatter.19
  802.9 34.9 reduce-scatter.21
  840.2 45.3 reduce-scatter.25
  887.9 34.5 reduce-scatter.23

commit v3 on v2

--- a/solution.py
+++ b/solution.py
@@ -95,10 +95,13 @@
     return x * lax.rsqrt(jnp.mean(x * x, axis=-1, keepdims=True) + EPS)
 
 
-def start_body(
-    T, x, seg, par, ct, nh, seg_out, par_out, ct_out, nbuf, zbuf,
-    s_n, r_n, s_h, r_h, s_s, r_s, s_p, r_p, s_c, r_c, s_l,
+def first_body(
+    T, n, x, seg, par, win, *refs
 ):
+    srcs, refs = refs[:n], refs[n:]
+    nh, seg_out, par_out, w_in = refs[:4]
+    dsts, refs = refs[4 : 4 + n], refs[4 + n :]
+    (nbuf, zbuf, s_n, r_n, s_h, r_h, s_s, r_s, s_p, r_p, s_w, r_w, s_z, r_z, s_c, r_c, s_l, s_o, r_o) = refs
     t, p, c = here()
     B = x.shape[0]
     count = 0
@@ -109,21 +112,59 @@
             if dt or dp:
                 greet((tt, pp, c))
                 count += 1
-            if dp == 0:
+            if dt == 0 or dp == 0:
                 greet((tt, pp, 1 - c))
                 count += 1
     nbuf[...] = unit(x[...].astype(F32)).astype(BF)
     zbuf[...] = jnp.zeros_like(zbuf)
     arrive(count)
+    half = lax.div(p, 2)
+    slot = lax.rem(p, 2) * 2 + c
+    me = t * 2 + c
+
+    def block(src, dst, send, recv, q):
+        return remote(src.at[q], dst.at[slot], send.at[q], recv.at[slot], (t, q, half))
+
+    def kept(src, dst, send, q):
+        return pltpu.make_async_copy(src.at[q], dst.at[slot], send.at[q])
+
+    def exchange(src, dst, send, recv):
+        for q in range(W):
+            mine = (p == q) & (half == c)
+
+            @pl.when(jnp.logical_not(mine))
+            def _():
+                block(src, dst, send, recv, q).start()
+
+            @pl.when(mine)
+            def _():
+                kept(src, dst, send, q).start()
+
+    def exchanged(src, dst, send, recv, j):
+        own = (half == c) & (slot == j)
+
+        @pl.when(jnp.logical_not(own))
+        def _():
+            remote(src.at[0], dst.at[j], send.at[0], recv.at[j], (t, 0, half)).wait_recv()
+
+    def sent(src, dst, send, recv):
+        for q in range(W):
+            mine = (p == q) & (half == c)
+
+            @pl.when(jnp.logical_not(mine))
+            def _():
+                block(src, dst, send, recv, q).wait_send()
+
+    landing = w_in.at[t * 2 + half]
+    exchange(win, landing, s_w, r_w)
     rows = pl.ds(pl.multiple_of(HALO + p * B, HALO), B)
-    plain = pl.ds(pl.multiple_of(p * B, B), B)
     copies = []
     for dt in range(T):
         for dc in range(2):
             if dt or dc:
                 copies.append(
                     remote(
-                        par, par_out.at[t * 2 + c], s_p.at[dt, dc], r_p.at[dt, dc],
+                        par, par_out.at[me], s_p.at[dt, dc], r_p.at[dt, dc],
                         (lax.rem(t + dt, T), p, flip(c, dc)),
                     )
                 )
@@ -138,8 +179,11 @@
                         (lax.rem(t + dt, T), flip(p, dp), c),
                     )
                 )
-    for d in range(1, W):
-        copies.append(remote(ct, ct_out.at[plain], s_c.at[d], r_c.at[d], (t, flip(p, d), c)))
+    copies += [
+        pltpu.make_async_copy(nbuf, nh.at[rows], s_l.at[0]),
+        pltpu.make_async_copy(par, par_out.at[me], s_l.at[1]),
+        pltpu.make_async_copy(seg, seg_out.at[t * W + p], s_l.at[2]),
+    ]
     for copy in copies:
         copy.start()
     last = (p == W - 1) & (t < T - 1)
@@ -154,23 +198,78 @@
         for q in range(W):
             rim(q).start()
 
-    local = [
-        pltpu.make_async_copy(nbuf, nh.at[rows], s_l.at[0]),
-        pltpu.make_async_copy(par, par_out.at[t * 2 + c], s_l.at[1]),
-        pltpu.make_async_copy(seg, seg_out.at[t * W + p], s_l.at[2]),
-        pltpu.make_async_copy(ct, ct_out.at[plain], s_l.at[4]),
-    ]
-    for copy in local:
-        copy.start()
-
     @pl.when(t == 0)
     def _():
         clear = pltpu.make_async_copy(zbuf, head, s_l.at[3])
         clear.start()
         clear.wait()
 
-    for copy in local:
-        copy.wait()
+    for i in range(n):
+        exchange(srcs[i], dsts[i], s_o.at[i], r_o.at[i])
+
+    def on(way, d, j):
+        step = 1 - 2 * way
+        source = lax.rem(t - step * d + T, T) * 2 + c
+        part = w_in.at[source, j]
+        return remote(
+            part, part, s_z.at[way, d, j], r_z.at[way, d + 1, j], (lax.rem(t + step + T, T), p, c)
+        )
+
+    def came(way, d, j):
+        step = 1 - 2 * way
+        part = w_in.at[lax.rem(t - step * d + T, T) * 2 + c, j]
+        return remote(part, part, s_z.at[way, d, j], r_z.at[way, d, j], (lax.rem(t + step + T, T), p, c))
+
+    def across(way, d, j):
+        step = 1 - 2 * way
+        part = w_in.at[lax.rem(t - step * d + T, T) * 2 + c, j]
+        return remote(part, part, s_c.at[way, d, j], r_c.at[way, d, j], (t, p, 1 - c))
+
+    def crossed(way, d, j):
+        step = 1 - 2 * way
+        part = w_in.at[lax.rem(t - step * d + T, T) * 2 + 1 - c, j]
+        return remote(part, part, s_c.at[way, d, j], r_c.at[way, d, j], (t, p, 1 - c))
+
+    def goes(way, d):
+        if way == 0:
+            return (t >= d) & (t < T - 1)
+        return (t + d < T) & (t > 0)
+
+    def arrives(way, d):
+        return (t >= d) if way == 0 else (t + d < T)
+
+    for j in range(W):
+        mine = (half == c) & (slot == j)
+
+        @pl.when(mine)
+        def _():
+            for q in range(W):
+
+                @pl.when(p == q)
+                def _():
+                    kept(win, landing, s_w, q).wait()
+
+        exchanged(win, w_in.at[me], s_w, r_w, j)
+        across(0, 0, j).start()
+        for way in range(2):
+
+            @pl.when(goes(way, 0))
+            def _():
+                on(way, 0, j).start()
+
+    for d in range(1, T):
+        for j in range(W):
+            for way in range(2):
+
+                @pl.when(arrives(way, d))
+                def _():
+                    came(way, d, j).wait_recv()
+                    across(way, d, j).start()
+
+                @pl.when(goes(way, d))
+                def _():
+                    on(way, d, j).start()
+
     for copy in copies:
         copy.wait()
 
@@ -183,28 +282,58 @@
     def _():
         rim(0).wait_recv()
 
-
-def start_call(T, x, seg, par, ct):
+    sent(win, landing, s_w, r_w)
+    for i in range(n):
+        sent(srcs[i], dsts[i], s_o.at[i], r_o.at[i])
+        for q in range(W):
+            mine = (p == q) & (half == c)
+
+            @pl.when(mine)
+            def _():
+                kept(srcs[i], dsts[i], s_o.at[i], q).wait()
+
+        for j in range(W):
+            exchanged(srcs[i], dsts[i], s_o.at[i], r_o.at[i], j)
+    for d in range(T):
+        for j in range(W):
+            for way in range(2):
+                if d or way == 0:
+
+                    @pl.when(arrives(way, d))
+                    def _():
+                        across(way, d, j).wait_send()
+                        crossed(way, d, j).wait_recv()
+
+                @pl.when(goes(way, d))
+                def _():
+                    on(way, d, j).wait_send()
+
+
+def first_call(T, x, seg, par, win, others):
     B, D = x.shape
+    n = len(others)
     return pl.pallas_call(
-        functools.partial(start_body, T),
+        functools.partial(first_body, T, n),
         out_shape=(
             out((HALO + W * B, D), BF),
             out((W * T,) + seg.shape, jnp.int32),
             out((2 * T,) + par.shape, BF),
-            out((W * B, D), BF),
-        ),
-        in_specs=[vmem(), hbm(), hbm(), hbm()],
-        out_specs=(hbm(), hbm(), hbm(), hbm()),
+            out((2 * T,) + win.shape, BF),
+        )
+        + tuple(out(a.shape, BF) for a in others),
+        in_specs=[vmem()] + [hbm()] * (3 + n),
+        out_specs=(hbm(),) * (4 + n),
         scratch_shapes=[
             pltpu.VMEM((B, D), BF),
             pltpu.VMEM((HALO, D), BF),
             dma(W), dma(W), dma(W), pltpu.SemaphoreType.DMA,
-            dma(T, W), dma(T, W), dma(T, 2), dma(T, 2), dma(W), dma(W), dma(5),
+            dma(T, W), dma(T, W), dma(T, 2), dma(T, 2), dma(W), dma(W),
+            dma(2, T, W), dma(2, T + 1, W), dma(2, T, W), dma(2, T, W), dma(4),
+            dma(n, W), dma(n, W),
         ],
         compiler_params=talk(0),
-        name="start",
-    )(x, seg, par, ct)
+        name="first",
+    )(x, seg, par, win, *others)
 
 
 def spread_body(n, back, *refs):
@@ -322,22 +451,111 @@
     )(x)
 
 
-def turn_body(back, gather, parts, *refs):
+def gather_job(T, src, dst, s_z, r_z, s_c, r_c, s_l):
+    t, p, c = here()
+
+    def part(dt, core):
+        return dst.at[lax.rem(t - dt + T, T) * 2 + core]
+
+    def out_to(dt):
+        return remote(src, part(0, c), s_z.at[dt], r_z.at[dt], (lax.rem(t + dt, T), p, c))
+
+    def across(dt):
+        return remote(src if dt == 0 else part(dt, c), part(dt, c), s_c.at[dt], r_c.at[dt], (t, p, 1 - c))
+
+    keep = pltpu.make_async_copy(src, part(0, c), s_l)
+
+    def begin():
+        for dt in range(1, T):
+            out_to(dt).start()
+        across(0).start()
+        keep.start()
+
+    def end():
+        for dt in range(1, T):
+            out_to(dt).wait_recv()
+            across(dt).start()
+        keep.wait()
+        for dt in range(T):
+            across(dt).wait_send()
+            remote(part(dt, 1 - c), part(dt, 1 - c), s_c.at[dt], r_c.at[dt], (t, p, 1 - c)).wait_recv()
+        for dt in range(1, T):
+            out_to(dt).wait_send()
+
+    return begin, end
+
+
+def scatter_job(T, src, dst, mine, other, recv, s_z, r_z, s_c, r_c, s_l):
+    t, p, c = here()
+
+    def at(dt):
+        return lax.rem(t + dt, T)
+
+    def across(dt):
+        return remote(
+            src.at[at(dt) * 2 + 1 - c], other.at[dt], s_c.at[dt], r_c.at[dt], (t, p, 1 - c)
+        )
+
+    def load(dt):
+        return pltpu.make_async_copy(src.at[at(dt) * 2 + c], mine.at[dt], s_l.at[dt])
+
+    def out_to(dt):
+        return remote(mine.at[dt], recv.at[dt - 1], s_z.at[dt], r_z.at[dt], (at(dt), p, c))
+
+    order = list(range(1, T)) + [0]
+
+    def begin():
+        for dt in order:
+            across(dt).start()
+            load(dt).start()
+        for dt in order[:-1]:
+            across(dt).wait_recv()
+            load(dt).wait()
+            mine[dt] = (mine[dt].astype(F32) + other[dt].astype(F32)).astype(BF)
+            out_to(dt).start()
+
+    def end():
+        across(0).wait_recv()
+        load(0).wait()
+        total = mine[0].astype(F32) + other[0].astype(F32)
+        for dt in range(1, T):
+            out_to(dt).wait_recv()
+            total = total + recv[dt - 1].astype(F32)
+        dst[...] = total
+        for dt in range(T):
+            across(dt).wait_send()
+        for dt in range(1, T):
+            out_to(dt).wait_send()
+
+    return begin, end
+
+
+def turn_body(T, back, gather, parts, job, *refs):
     refs = list(refs)
     part = refs.pop(0)
     x = refs.pop(0)
     g = refs.pop(0) if back else None
+    job_src = refs.pop(0) if job else None
     o = refs.pop(0)
     gath = refs.pop(0) if gather else None
-    own, recv, sbuf, ss, rs, ls, ss2, rs2, ls2 = refs
+    job_dst = refs.pop(0) if job else None
+    own, recv, sbuf, ss, rs, ls, ss2, rs2, ls2 = refs[:9]
     t, p, c = here()
     B = x.shape[0]
     rows = B // parts
     for d in range(1, W):
         greet((t, flip(p, d), c))
+    count = W - 1
+    if job:
+        for dt in range(1, T):
+            greet((lax.rem(t + dt, T), p, c))
+        greet((t, p, 1 - c))
+        count += T
+        build = gather_job if job == "gather" else scatter_job
+        begin, end = build(T, job_src, job_dst, *refs[9:])
     local = pltpu.make_async_copy(part.at[pl.ds(pl.multiple_of(p * B, B), B)], own, ls)
     local.start()
-    arrive(W - 1)
+    arrive(count)
     first = {}
     for k in range(parts):
         for d in range(1, W):
@@ -350,6 +568,8 @@
                 (t, q, c),
             )
             first[k, d].start()
+    if job:
+        begin()
     local.wait()
     later = []
     for k in range(parts):
@@ -377,33 +597,58 @@
             later.append(pltpu.make_async_copy(sbuf.at[cut], place, ls2.at[k]))
             for copy in later[-W:]:
                 copy.start()
+    if job:
+        end()
     for copy in first.values():
         copy.wait_send()
     for copy in later:
         copy.wait()
 
 
-def turn(cid, part, x, g=None, gather=True, dtype=F32, parts=2):
+def turn(cid, part, x, g=None, gather=True, dtype=F32, parts=2, T=1, fetch=None, give=None):
     B, D = x.shape
     back = g is not None
     shapes = [out((B, D), dtype)]
     specs = [vmem()]
+    args = (part, x) + ((g,) if back else ())
+    in_specs = [hbm()] + [vmem()] * (len(args) - 1)
+    scratch = [
+        pltpu.VMEM((B, D), BF),
+        pltpu.VMEM((W - 1, B, D), BF),
+        pltpu.VMEM((B, D), BF),
+        dma(W - 1, parts), dma(W - 1, parts), pltpu.SemaphoreType.DMA,
+        dma(W - 1, parts), dma(W - 1, parts), dma(parts),
+    ]
     if gather:
         shapes.append(out((W * B, D), BF))
         specs.append(hbm())
-    args = (part, x) + ((g,) if back else ())
+    job = None
+    if fetch is not None:
+        job = "gather"
+        args += (fetch,)
+        in_specs.append(hbm())
+        shapes.append(out((2 * T,) + fetch.shape, BF))
+        specs.append(hbm())
+        scratch += [dma(T), dma(T), dma(T), dma(T), pltpu.SemaphoreType.DMA]
+    if give is not None:
+        job = "scatter"
+        give = give.reshape(2 * T, -1, give.shape[-1])
+        args += (give,)
+        in_specs.append(hbm())
+        shapes.append(out(give.shape[1:]))
+        specs.append(vmem())
+        scratch += [
+            pltpu.VMEM((T,) + give.shape[1:], BF),
+            pltpu.VMEM((T,) + give.shape[1:], BF),
+            pltpu.VMEM((T - 1,) + give.shape[1:], BF),
+            dma(T), dma(T), dma(T), dma(T), dma(T),
+        ]
     return pl.pallas_call(
-        functools.partial(turn_body, back, gather, parts),
+        functools.partial(turn_body, T, back, gather, parts, job),
         out_shape=tuple(shapes),
-        in_specs=[hbm()] + [vmem()] * (len(args) - 1),
+        in_specs=in_specs,
         out_specs=tuple(specs),
-        scratch_shapes=[
-            pltpu.VMEM((B, D), BF),
-            pltpu.VMEM((W - 1, B, D), BF),
-            pltpu.VMEM((B, D), BF),
-            dma(W - 1, parts), dma(W - 1, parts), pltpu.SemaphoreType.DMA,
-            dma(W - 1, parts), dma(W - 1, parts), dma(parts),
-        ],
+        scratch_shapes=scratch,
         compiler_params=talk(cid),
         name="turn%d" % cid,
     )(*args)
@@ -466,14 +711,18 @@
     return w * cosine + pltpu.roll(w, HD // 2, 1) * sine
 
 
-def keys_body(T, hops, qkv, cosine, sine, q, k_all, v_all, ss, rs):
+def keys_body(T, hops, qkv, cosine, sine, ct, q, k_all, v_all, ct_out, ss, rs, s_g, r_g, s_l):
     t, p, c = here()
     CH = q.shape[0]
     width = q.shape[1]
+    B = ct.shape[0]
 
     @pl.when(t > 0)
     def _():
         greet((lax.rem(t - 1 + T, T), p, c))
+
+    for d in range(1, W):
+        greet((t, flip(p, d), c))
 
     mine = pl.ds(hops * CH, CH)
     for h in range(width // HD):
@@ -485,7 +734,11 @@
 
     @pl.when(t < T - 1)
     def _():
-        arrive(1)
+        arrive(W)
+
+    @pl.when(t == T - 1)
+    def _():
+        arrive(W - 1)
 
     def send(a, d):
         ref = (k_all, v_all)[a]
@@ -506,6 +759,12 @@
             send(1, d).start()
 
         if d == 1:
+            rows = ct_out.at[pl.ds(pl.multiple_of(p * B, B), B)]
+            copies = [
+                remote(ct, rows, s_g.at[e], r_g.at[e], (t, flip(p, e), c)) for e in range(1, W)
+            ] + [pltpu.make_async_copy(ct, rows, s_l)]
+            for copy in copies:
+                copy.start()
             for h in range(width // HD):
                 cols = pl.ds(h * HD, HD)
                 q[:, cols] = rope(qkv[:, cols], cosine[...], sine[...]).astype(BF)
@@ -528,8 +787,11 @@
             send(0, d).wait_send()
             send(1, d).wait_send()
 
-
-def keys_call(cid, T, hops, qkv, cosine, sine):
+    for copy in copies:
+        copy.wait()
+
+
+def keys_call(cid, T, hops, qkv, cosine, sine, ct):
     CH = qkv.shape[0]
     width = qkv.shape[1] // 3
     return pl.pallas_call(
@@ -538,13 +800,16 @@
             out((CH, width), BF),
             out(((hops + 1) * CH, width), BF),
             out(((hops + 1) * CH, width), BF),
+            out((W * ct.shape[0], ct.shape[1]), BF),
         ),
-        in_specs=[vmem()] * 3,
-        out_specs=(vmem(),) * 3,
-        scratch_shapes=[dma(2, hops), dma(2, hops)],
+        in_specs=[vmem()] * 3 + [hbm()],
+        out_specs=(vmem(),) * 3 + (hbm(),),
+        scratch_shapes=[
+            dma(2, hops), dma(2, hops), dma(W), dma(W), pltpu.SemaphoreType.DMA,
+        ],
         compiler_params=talk(cid),
         name="keys",
-    )(qkv, cosine, sine)
+    )(qkv, cosine, sine, ct)
 
 
 def keys_back_body(T, hops, dq, dk, dv, cosine, sine, dqkv, sb, recv, ss, rs):
@@ -1133,14 +1398,14 @@
     win_out = columns_out(in_proj, norm_mixer, 2, T, 2 * CB)
     seg8 = jnp.broadcast_to(segment_ids, (8, B))
     x0 = inputs[0].astype(F32)
-    (win_mine,) = spread_call(21, False, (win_out,))
-    w_in = gather_tc(win_mine)
-    nh1_ext, seg_all, par_all, gl4 = start_call(T, inputs[0], seg8, par, cotangent[0])
 
     gu1_out = columns_out(gate_up_one, norm_ffn_one, 2, T, 2 * FB)
     qkv_out = columns_out(qkv_proj, norm_attn, 3, 1, heads)
     gu2_out = columns_out(gate_up_two, norm_ffn_two, 2, T, 2 * FB)
-    gu1_mine, qkv_mine, gu2_mine = spread_call(1, False, (gu1_out, qkv_out, gu2_out))
+    nh1_ext, seg_all, par_all, w_in, gu1_mine, qkv_mine, gu2_mine = first_call(
+        T, inputs[0], seg8, par, win_out, (gu1_out, qkv_out, gu2_out)
+    )
+    w_in = w_in.reshape(D, -1)
     devices = 2 * W * T
     pairs = []
     for d in range(devices):
@@ -1149,11 +1414,8 @@
     ao_mine = lax.ppermute(attn_out, ("t", "p", "c"), pairs)
     w_mix = gather_tc(mixer_out)
     w_gu1 = gather_tc(gu1_mine)
-    w_d1 = gather_tc(down_one)
     w_qkv = gather_tc(qkv_mine)
-    w_ao = gather_tc(ao_mine)
     w_gu2 = gather_tc(gu2_mine)
-    w_d2 = gather_tc(down_two)
 
     seg = seg_all[:, 0, :].reshape(total)
     pos = t * CH + jnp.arange(CH, dtype=jnp.int32)
@@ -1225,16 +1487,19 @@
     zg = xz[HALO:, width:]
     gate_s = jax.nn.sigmoid(zg)
     gated = (y * zg * gate_s).astype(BF)
-    x1, nh2 = turn(5, nn(gated, w_mix).astype(BF), x0)
+    x1, nh2, w_d1 = turn(5, nn(gated, w_mix).astype(BF), x0, T=T, fetch=down_one)
+    w_d1 = w_d1.reshape(-1, D)
 
     a_one = nn(nh2, w_gu1)
     h_one = swiglu(a_one).astype(BF)
-    x2, nh3 = turn(6, nn(h_one, w_d1).astype(BF), x1)
+    x2, nh3, w_ao = turn(6, nn(h_one, w_d1).astype(BF), x1, T=T, fetch=ao_mine)
+    w_ao = w_ao.reshape(-1, D)
 
     qkv = nn(nh3, w_qkv)
-    q, k_all, v_all = keys_call(7, T, hops, qkv, cosine, sine)
+    q, k_all, v_all, gl4 = keys_call(7, T, hops, qkv, cosine, sine, cotangent[0])
     o, lse = attend(q, k_all, v_all, bias)
-    x3, nh4 = turn(8, nn(o, w_ao).astype(BF), x2)
+    x3, nh4, w_d2 = turn(8, nn(o, w_ao).astype(BF), x2, T=T, fetch=down_two)
+    w_d2 = w_d2.reshape(-1, D)
 
     a_two = nn(nh4, w_gu2)
     h_two = swiglu(a_two).astype(BF)
@@ -1243,28 +1508,23 @@
     g4 = cotangent[0].astype(F32)
     dw_d2 = tn(h_two, gl4).astype(BF)
     da_two = swiglu_back(a_two, nt(gl4, w_d2))
-    da_two, dw_d2 = together(da_two, dw_d2)
-    grad_d2 = scatter_tc(dw_d2)
     part, dw_gu2 = together(nt(da_two, w_gu2).astype(BF), tn(nh4, da_two).astype(BF))
-    g3, gl3 = turn(10, part, x3, g4)
+    g3, gl3, grad_d2 = turn(10, part, x3, g4, T=T, give=dw_d2)
     raw_gu2 = scatter_tc(dw_gu2)
 
     do, dw_ao = together(nt(gl3, w_ao).astype(BF), tn(o, gl3).astype(BF))
-    raw_ao = scatter_tc(dw_ao)
     dq, dk, dv = attend_back(q, k_all, v_all, bias, lse, do)
-    dq, grad_d2 = together(dq, grad_d2)
+    dq, final = together(dq, final)
     dqkv = keys_back_call(11, T, hops, dq, dk, dv, cosine, sine)
     part, dw_qkv = together(nt(dqkv, w_qkv).astype(BF), tn(nh3, dqkv).astype(BF))
     raw_qkv = scatter_tc(dw_qkv)
     part, raw_gu2 = together(part, raw_gu2)
-    g2, gl2 = turn(12, part, x2, g3)
-    gl2, raw_ao = together(gl2, raw_ao)
+    g2, gl2, raw_ao = turn(12, part, x2, g3, T=T, give=dw_ao)
 
     da_one, dw_d1 = together(swiglu_back(a_one, nt(gl2, w_d1)), tn(h_one, gl2).astype(BF))
-    grad_d1 = scatter_tc(dw_d1)
     part, dw_gu1 = together(nt(da_one, w_gu1).astype(BF), tn(nh2, da_one).astype(BF))
     raw_gu1 = scatter_tc(dw_gu1)
-    g1, gl1 = turn(13, part, x1, g2)
+    g1, gl1, grad_d1 = turn(13, part, x1, g2, T=T, give=dw_d1)
     gl1, raw_qkv = together(gl1, raw_qkv)
 
     dgate = nt(gl1, w_mix)
@@ -1275,7 +1535,6 @@
     raw_z = scatter_tc(dw_z)
     begin = scan_three(delta, dy, a2, crep, first)
     g_in = chain(14, T, True, packed(begin), a2)
-    g_in, grad_d1 = together(g_in, grad_d1)
     ddelta, du_scan, db, dc_mat, ga = scan_four(
         delta, u, dy, skip_row, a2, brep, crep, first, marks, g_in
     )
@@ -1325,7 +1584,7 @@
     )
     (x_b,) = spread_call(20, True, (blocks(raw_x),))
     in_b = jnp.concatenate([x_b, z_b], axis=2)
-    grad_ao = lax.ppermute(raw_ao, ("t", "p", "c"), [(b, a) for a, b in pairs]).astype(F32)
+    grad_ao = lax.ppermute(raw_ao.astype(BF), ("t", "p", "c"), [(b, a) for a, b in pairs]).astype(F32)
 
     def finished(blocks_in, weight, gain, groups, groups_t, cols):
         raw = columns_back(blocks_in, groups, groups_t, cols)
@@ -1354,13 +1613,13 @@
         grad_mix.astype(F32),
         grad_n2,
         grad_gu1,
-        grad_d1.astype(F32),
+        grad_d1,
         grad_n3,
         grad_qkv,
         grad_ao,
         grad_n4,
         grad_gu2,
-        grad_d2.astype(F32),
+        grad_d2,
     )
 
 

time: 1040 us -> 1010 us (0.971)
  waiting for transfers between devices: 53.9 us -> 2.74 us
  Pallas kernels: 663 us -> 711 us
  matrix products: 139 us -> 116 us
    pallas_call x9, Pallas kernels: 304 us -> 402 us  [the longest x8 338 us: turn(): pl.pallas_call(functools.partial(turn_body, T, back, gather, parts, job),...]
    all_gather x8 -> x4, waiting for transfers between devices: 44.9 us -> 0.01 us  [gather_tc(): lax.all_gather(x.reshape(-1, x.shape[-1]), ('t', 'c'), axis=0, tiled=True)]
    pallas_call x4 -> x2, Pallas kernels: 73.5 us -> 35.8 us  [spread_call(): pl.pallas_call(functools.partial(spread_body, n, back), out_shape=tuple((...]
    pallas_call x1, Pallas kernels: 79.9 us -> 50.1 us  [keys_back_call(): pl.pallas_call(functools.partial(keys_back_body, T, hops), out_shape=out(...]
    pallas_call x1, Pallas kernels: 13.5 us -> 34.5 us  [small_sum(): pl.pallas_call(functools.partial(small_body, T), out_shape=out(x.shape[1:...]
    unnamed x210 -> x252, local copies, waits for them, and re-layouts: 47.1 us -> 55.2 us
  transfers between devices with their start and end apart: 19 -> 12, of which waited for: 2 -> 0; matrix products, arithmetic and copies ran while one was open for 21% -> 18% of each run, Pallas kernels for 63% -> 70%
where the time goes in v3:
time: 1010 us; the launch traced here: 1000 us
  Pallas kernels  711 us (70%)
  matrix products  116 us (11%)
  local copies, waits for them, and re-layouts  113 us (11%)
  other arithmetic  39.5 us (4%)
  between operations  16.8 us (2%)
    pallas_call x8, Pallas kernels, turn(): pl.pallas_call(functools.partial(turn_body, T, back, gather, parts, job),...  338 us
    pallas_call x1, Pallas kernels, first_call(): pl.pallas_call(functools.partial(first_body, T, n), out_shape=(out((HALO...  63.6 us
    unnamed x252, local copies, waits for them, and re-layouts  55.2 us
    pallas_call x1, Pallas kernels, keys_back_call(): pl.pallas_call(functools.partial(keys_back_body, T, hops), out_shape=out(...  50.1 us
    dot_general x10, matrix products, nt(): lax.dot_general(a, b, (((1,), (1,)), ((), ())), preferred_element_type=F32)  44.1 us
    pallas_call x1, Pallas kernels, scan_four(): pl.pallas_call(scan_four_body, out_shape=(out((CH, width)), out((CH, widt...  39.4 us
    pallas_call x2, Pallas kernels, chain(): pl.pallas_call(functools.partial(chain_body, T, back), out_shape=out(a2.s...  37.9 us
    dot_general x11, matrix products, tn(): lax.dot_general(a, b, (((0,), (0,)), ((), ())), preferred_element_type=F32)  36.1 us
  transfers between devices with their start and end apart: 12, of which 0 were waited for; matrix products, arithmetic and copies ran while one was open for 18% of the time, Pallas kernels for 70%

profile of v3, /device:TPU:1, one launch (start us, length us, event | category | flops | bytes accessed | tf_op | source)
XLA Modules:
  0.0 1004.8 jit_solution(10675908344216404631)
XLA Ops:
  26.3 63.6 %first.1 = (bf16[528,1536]{1,0:T(8,128)(2,1)S(1)}, s32[16,8,128]{2,1,0:T(8,128)S(1)}, bf16[8,96,256]{2,1,0:T(8,128)(2,1)S(1)}, bf16[8,4,48,1536]{3,2,1,0:T(8,128...) custom-call(bf16[128,1536]{1,0:T(8,128)(2,1)S(1)} %bitcast.117, ...), custom_call_target="tpu_custom_call" | custom-call | tf_op jit(solution)/shard_map/first/pallas_call | solution.py:315
  102.8 6.7 fusion.71.xz
  116.2 9.9 plane_sum3.1
  134.6 9.7 scan_one.1
  145.2 15.4 %chain4.1.h_in = f32[16,768]{1,0:T(8,128)S(1)} custom-call(f32[24,768]{1,0:T(8,128)S(1)} %fusion.24.v, f32[16,768]{1,0:T(8,128)S(1)} %copy-done.3), custom_call_target="tpu_custom_call" | custom-call | tf_op jit(solution)/shard_map/chain4/pallas_call | solution.py:699
  163.2 16.5 %scan_two.1 = (f32[512,768]{1,0:T(8,128)}, f32[128,768]{1,0:T(8,128)}) custom-call(f32[512,768]{1,0:T(8,128)} %get-tuple-element.278.delta, f32[512,768]{1,0:T(8,128)} %get-tuple-element.102.u, f32[16,768]{1,0:T(8,128)} %fusion.30.a2, f32[8192,128]{1,0:T(8,128)} %broadcast_in_dim.92.brep, f32[8192,128]{1,0:T(8,128)} %broadcast_in_dim.94.crep, ...), custom_call_target="tpu_custom_call" | custom-call | tf_op jit(solution)/shard_map/scan_two/pallas_call | solution.py:1119
  189.8 49.1 %turn5.1 = (f32[128,1536]{1,0:T(8,128)S(1)}, bf16[512,1536]{1,0:T(8,128)(2,1)S(1)}, bf16[8,128,1536]{2,1,0:T(8,128)(2,1)S(1)}) custom-call(bf16[512,1536]{1,0:T(8,128)(2,1)S(1)} %convolution_convert_fusion.15.refs_0_, f32[128,1536]{1,0:T(8,128)S(1)} %bitcast_convert_fusion.1.refs_1_, bf16[128,1536]{1,0:T(8,128)(2,1)S(1)} %copy-done.42), custom_call_target="tpu_custom_call" | custom-call | tf_op jit(solution)/shard_map/turn5/pallas_call | solution.py:646
  241.7 6.5 fusion.72
  253.9 45.7 %turn6.1 = (f32[128,1536]{1,0:T(8,128)S(1)}, bf16[512,1536]{1,0:T(8,128)(2,1)S(1)}, bf16[8,48,1536]{2,1,0:T(8,128)(2,1)S(1)}) custom-call(bf16[512,1536]{1,0:T(8,128)(2,1)S(1)} %convolution_convert_fusion.14.refs_0_, f32[128,1536]{1,0:T(8,128)S(1)} %get-tuple-element.107.refs_1_, bf16[48,1536]{1,0:T(8,128)(2,1)} %collective-permute-done.refs_2_), custom_call_target="tpu_custom_call" | custom-call | tf_op jit(solution)/shard_map/turn6/pallas_call | solution.py:646
  306.5 19.2 %keys.1 = (bf16[512,384]{1,0:T(8,128)(2,1)S(1)}, bf16[1536,384]{1,0:T(8,128)(2,1)S(1)}, bf16[1536,384]{1,0:T(8,128)(2,1)S(1)}, bf16[512,1536]{1,0:T(8,128)(2,1)S(1)}) custom-call(f32[512,1152]{1,0:T(8,128)S(1)} %fusion.73.qkv, f32[512,128]{1,0:T(8,128)S(1)} %get-tuple-element.295.cosine, f32[512,128]{1,0:T(8,128)S(1)} %get-tuple-element.296.sine, ...), custom_call_target="tpu_custom_call" | custom-call | tf_op jit(solution)/shard_map/keys/pallas_call | solution.py:797
  329.8 9.2 attend.1
  341.1 52.5 %turn8.1 = (f32[128,1536]{1,0:T(8,128)S(1)}, bf16[512,1536]{1,0:T(8,128)(2,1)S(1)}, bf16[8,128,1536]{2,1,0:T(8,128)(2,1)S(1)}) custom-call(bf16[512,1536]{1,0:T(8,128)(2,1)S(1)} %convolution_convert_fusion.13.refs_0_, f32[128,1536]{1,0:T(8,128)S(1)} %get-tuple-element.117.refs_1_, bf16[128,1536]{1,0:T(8,128)(2,1)S(1)} %copy-done.43), custom_call_target="tpu_custom_call" | custom-call | tf_op jit(solution)/shard_map/turn8/pallas_call | solution.py:646
  396.5 6.1 fusion.74
  413.0 8.0 convolution_convert_fusion.12.refs_0_
  426.1 55.1 %turn10.1 = (f32[128,1536]{1,0:T(8,128)S(1)}, bf16[512,1536]{1,0:T(8,128)(2,1)S(1)}, f32[128,1536]{1,0:T(8,128)S(1)}) custom-call(bf16[512,1536]{1,0:T(8,128)(2,1)S(1)} %copy-done.15, f32[128,1536]{1,0:T(8,128)S(1)} %get-tuple-element.122.refs_1_, f32[128,1536]{1,0:T(8,128)S(1)} %bitcast_convert_fusion.refs_2_, bf16[8,128,1536]{2,1,0:T(8,128)(2,1)S(1)} %bitcast.110), custom_call_target="tpu_custom_call" | custom-call | tf_op jit(solution)/shard_map/turn10/pallas_call | solution.py:646
  487.5 20.1 %turn9.1 = bf16[128,1536]{1,0:T(8,128)(2,1)S(1)} custom-call(bf16[512,1536]{1,0:T(8,128)(2,1)S(1)} %convolution_convert_fusion.11.refs_0_, f32[128,1536]{1,0:T(8,128)S(1)} %get-tuple-element.122.refs_1_), custom_call_target="tpu_custom_call" | custom-call | tf_op jit(solution)/shard_map/turn9/pallas_call | solution.py:646
  508.3 13.1 %attend_back.1 = (f32[512,384]{1,0:T(8,128)}, f32[1536,384]{1,0:T(8,128)}, f32[1536,384]{1,0:T(8,128)}) custom-call(bf16[512,384]{1,0:T(8,128)(2,1)} %copy-done.18, bf16[1536,384]{1,0:T(8,128)(2,1)} %copy-done, bf16[1536,384]{1,0:T(8,128)(2,1)} %copy-done.1, bf16[512,1536]{1,0:T(8,128)(2,1)} %select_convert_fusion.bias, f32[512,384]{1,0:T(8,128)} %get-tuple-element.113.lse, ...), custom_call_target="tpu_custom_call" | custom-call | tf_op jit(solution)/shard_map/attend_back/pallas_call | solution.py:1320
  524.4 50.1 %keys_back.1 = bf16[512,1152]{1,0:T(8,128)(2,1)} custom-call(f32[512,384]{1,0:T(8,128)S(1)} %copy-done.25, f32[1536,384]{1,0:T(8,128)S(1)} %copy-done.9, f32[1536,384]{1,0:T(8,128)} %get-tuple-element.129.dv, f32[512,128]{1,0:T(8,128)S(1)} %copy-done.6, f32[512,128]{1,0:T(8,128)S(1)} %copy-done.8), custom_call_target="tpu_custom_call" | custom-call | tf_op jit(solution)/shard_map/keys_back/pallas_call | solution.py:896
  579.8 5.9 convolution_convert_fusion.8.refs_0_
  589.4 38.7 %turn12.1 = (f32[128,1536]{1,0:T(8,128)S(1)}, bf16[512,1536]{1,0:T(8,128)(2,1)S(1)}, f32[48,1536]{1,0:T(8,128)S(1)}) custom-call(bf16[512,1536]{1,0:T(8,128)(2,1)S(1)} %copy-done.12, f32[128,1536]{1,0:T(8,128)S(1)} %get-tuple-element.117.refs_1_, f32[128,1536]{1,0:T(8,128)S(1)} %copy-done.37, bf16[8,48,1536]{2,1,0:T(8,128)(2,1)S(1)} %bitcast.123), custom_call_target="tpu_custom_call" | custom-call | tf_op jit(solution)/shard_map/turn12/pallas_call | solution.py:646
  643.3 6.9 convolution_convert_fusion.10.refs_0_
  653.4 53.8 %turn13.1 = (f32[128,1536]{1,0:T(8,128)S(1)}, bf16[512,1536]{1,0:T(8,128)(2,1)S(1)}, f32[128,1536]{1,0:T(8,128)S(1)}) custom-call(bf16[512,1536]{1,0:T(8,128)(2,1)S(1)} %convolution_convert_fusion.10.refs_0_, f32[128,1536]{1,0:T(8,128)S(1)} %get-tuple-element.107.refs_1_, f32[128,1536]{1,0:T(8,128)S(1)} %copy-done.24, bf16[8,128,1536]{2,1,0:T(8,128)(2,1)S(1)} %bitcast.109), custom_call_target="tpu_custom_call" | custom-call | tf_op jit(solution)/shard_map/turn13/pallas_call | solution.py:646
  714.8 6.2 multiply_multiply_fusion
  725.5 9.6 scan_three.1
  736.0 22.5 %chain14.1.g_in = f32[16,768]{1,0:T(8,128)S(1)} custom-call(f32[24,768]{1,0:T(8,128)S(1)} %fusion.26.v, f32[16,768]{1,0:T(8,128)S(1)} %copy-done.4), custom_call_target="tpu_custom_call" | custom-call | tf_op jit(solution)/shard_map/chain14/pallas_call | solution.py:699
  759.1 39.4 %scan_four.1 = (f32[512,768]{1,0:T(8,128)}, f32[512,768]{1,0:T(8,128)}, f32[8192,128]{1,0:T(8,128)}, f32[8192,128]{1,0:T(8,128)}, f32[16,768]{1,0:T(8,128)}) custom-call(f32[512,768]{1,0:T(8,128)} %get-tuple-element.278.delta, f32[512,768]{1,0:T(8,128)} %get-tuple-element.102.u, f32[512,768]{1,0:T(8,128)} %get-tuple-element.143.dy, ...), custom_call_target="tpu_custom_call" | custom-call | tf_op jit(solution)/shard_map/scan_four/pallas_call | solution.py:1230
  810.5 8.0 plane_sum15.1
  820.1 7.8 conv_back.1
  844.7 34.5 %small_sum.1 = f32[96,256]{1,0:T(8,128)S(1)} custom-call(bf16[8,96,256]{2,1,0:T(8,128)(2,1)S(1)} %bitcast.119), custom_call_target="tpu_custom_call" | custom-call | tf_op jit(solution)/shard_map/small_sum/pallas_call | solution.py:973
  885.7 23.1 %turn17.1 = f32[128,1536]{1,0:T(8,128)S(1)} custom-call(bf16[512,1536]{1,0:T(8,128)(2,1)S(1)} %convolution_convert_fusion.9.refs_0_, f32[128,1536]{1,0:T(8,128)S(1)} %bitcast_convert_fusion.1.refs_1_, f32[128,1536]{1,0:T(8,128)S(1)} %copy-done.35), custom_call_target="tpu_custom_call" | custom-call | tf_op jit(solution)/shard_map/turn17/pallas_call | solution.py:646
  912.8 29.4 %spread19.1 = (bf16[4,48,2048]{2,1,0:T(8,128)(2,1)S(1)}, bf16[4,48,1152]{2,1,0:T(8,128)(2,1)S(1)}, bf16[4,48,2048]{2,1,0:T(8,128)(2,1)S(1)}, bf16[4,48,768]{2,1,0:T(8,128)(2,1)S(1)}) custom-call(bf16[4,48,2048]{2,1,0:T(8,128)(2,1)S(1)} %bitcast.125, bf16[4,48,1152]{2,1,0:T(8,128)(2,1)S(1)} %bitcast.128, bf16[4,48,2048]{2,1,0:T(8,128)(2,1)S(1)} %bitcast.126, ...), custom_call_target="tpu_custom_call" | custom-call | tf_op jit(solution)/shard_map/spread19/pallas_call | solution.py:406
  977.4 6.4 spread20.1
  (424 shorter events, 239.0 us)
Async XLA Ops:
  7.2 179.4 %all-gather.5.cloned.1.call-start = ((), (), s32[]{:S(2)}) async-start(), calls=%async_computation.6 | async-start | bytes 2654208 | tf_op jit(solution)/shard_map/all_gather | solution.py:1344
  7.9 233.8 %all-gather.7.cloned.1.call-start = ((), (), s32[]{:S(2)}) async-start(), calls=%async_computation.7 | async-start | bytes 7077888 | tf_op jit(solution)/shard_map/all_gather | solution.py:1344
  94.9 32.3 %copy-start.10 = (bf16[8,96,256]{2,1,0:T(8,128)(2,1)}, bf16[8,96,256]{2,1,0:T(8,128)(2,1)S(1)}, u32[]{:S(2)}) copy-start(bf16[8,96,256]{2,1,0:T(8,128)(2,1)S(1)} %get-tuple-element.100) | copy-start | bytes 1179652
  94.9 7.9 copy-start.61
  94.9 206.9 %all-gather.9.cloned.1.call-start = ((), (), s32[]{:S(2)}) async-start(), calls=%async_computation.8 | async-start | bytes 3981312 | tf_op jit(solution)/shard_map/all_gather | solution.py:1344
  95.7 300.8 %all-gather.11.cloned.1.call-start = ((), (), s32[]{:S(2)}) async-start(), calls=%async_computation.9 | async-start | bytes 7077888 | tf_op jit(solution)/shard_map/all_gather | solution.py:1344
  96.2 489.9 %reduce-scatter.7.cloned.1.call-start = ((), (), s32[]{:S(2)}) async-start(), calls=%async_computation.10 | async-start | bytes 7077888 | tf_op jit(solution)/shard_map/reduce_scatter | solution.py:1352
  96.3 157.6 %collective-permute-start = (bf16[48,1536]{1,0:T(8,128)(2,1)}, bf16[48,1536]{1,0:T(8,128)(2,1)}, u32[]{:S(2)}, u32[]{:S(2)}) collective-permute-start(bf16[48,1536]{1,0:T(8,128)(2,1)} %param.40), channel_id=1, source_target_pairs={{0,0},{1,1},{2,8},{3,9},{4,16},{5,17},{6,24},{7,25},{8,2},{9,3},{1... | collective-permute-start | bytes 442376 | tf_op jit(solution)/shard_map/ppermute | solution.py:1414
  134.6 10.6 %copy-start.3 = (f32[16,768]{1,0:T(8,128)S(1)}, f32[16,768]{1,0:T(8,128)}, u32[]{:S(2)}) copy-start(f32[16,768]{1,0:T(8,128)} %fusion.30.a2) | copy-start | bytes 147460
  181.1 125.4 %copy-start.5 = (f32[512,128]{1,0:T(8,128)}, f32[512,128]{1,0:T(8,128)S(1)}, u32[]{:S(2)}) copy-start(f32[512,128]{1,0:T(8,128)S(1)} %get-tuple-element.295.cosine) | copy-start | bytes 786436
  181.1 125.4 %copy-start.7 = (f32[512,128]{1,0:T(8,128)}, f32[512,128]{1,0:T(8,128)S(1)}, u32[]{:S(2)}) copy-start(f32[512,128]{1,0:T(8,128)S(1)} %get-tuple-element.296.sine) | copy-start | bytes 786436
  329.8 9.2 copy-start.20
  421.1 289.1 %reduce-scatter.9.cloned.1.call-start = ((), (), s32[]{:S(2)}) async-start(), calls=%async_computation.11 | async-start | bytes 3981312 | tf_op jit(solution)/shard_map/reduce_scatter | solution.py:1352
  426.1 55.2 %copy-start.21 = (bf16[8,48,1536]{2,1,0:T(8,128)(2,1)S(1)}, bf16[8,48,1536]{2,1,0:T(8,128)(2,1)}, u32[]{:S(2)}) copy-start(bf16[8,48,1536]{2,1,0:T(8,128)(2,1)} %copy-done.19) | copy-start | bytes 3538948
  508.3 13.1 %copy-start.6 = (f32[512,128]{1,0:T(8,128)S(1)}, f32[512,128]{1,0:T(8,128)}, u32[]{:S(2)}) copy-start(f32[512,128]{1,0:T(8,128)} %copy-done.5) | copy-start | bytes 786436
  508.3 13.1 %copy-start.8 = (f32[512,128]{1,0:T(8,128)S(1)}, f32[512,128]{1,0:T(8,128)}, u32[]{:S(2)}) copy-start(f32[512,128]{1,0:T(8,128)} %copy-done.7) | copy-start | bytes 786436
  524.4 50.1 %copy-start.67 = (bf16[512,1536]{1,0:T(8,128)(2,1)S(1)}, bf16[512,1536]{1,0:T(8,128)(2,1)}, u32[]{:S(2)}) copy-start(bf16[512,1536]{1,0:T(8,128)(2,1)} %copy-done.66) | copy-start | bytes 4718596
  585.7 224.8 %reduce-scatter.11.cloned.1.call-start = ((), (), s32[]{:S(2)}) async-start(), calls=%async_computation.12 | async-start | bytes 7077888 | tf_op jit(solution)/shard_map/reduce_scatter | solution.py:1352
  589.4 38.8 %copy-start.56 = (bf16[8,128,1536]{2,1,0:T(8,128)(2,1)S(1)}, bf16[8,128,1536]{2,1,0:T(8,128)(2,1)}, u32[]{:S(2)}) copy-start(bf16[8,128,1536]{2,1,0:T(8,128)(2,1)} %copy-done.54) | copy-start | bytes 9437188
  650.2 188.4 %reduce-scatter.13.cloned.1.call-start = ((), (), s32[]{:S(2)}) async-start(), calls=%async_computation.13 | async-start | bytes 2654208 | tf_op jit(solution)/shard_map/reduce_scatter | solution.py:1352
  714.8 7.0 copy-start.62
  724.7 120.0 %reduce-scatter.17.cloned.1.call-start = ((), (), s32[]{:S(2)}) async-start(), calls=%async_computation.15 | async-start | bytes 2654208 | tf_op jit(solution)/shard_map/reduce_scatter | solution.py:1352
  725.5 10.5 %copy-start.4 = (f32[16,768]{1,0:T(8,128)S(1)}, f32[16,768]{1,0:T(8,128)}, u32[]{:S(2)}) copy-start(f32[16,768]{1,0:T(8,128)} %fusion.30.a2) | copy-start | bytes 147460
  725.5 251.0 %reduce-scatter.15.cloned.1.call-start = ((), (), s32[]{:S(2)}) async-start(), calls=%async_computation.14 | async-start | bytes 2654208 | tf_op jit(solution)/shard_map/reduce_scatter | solution.py:1352
  809.0 9.6 copy-start.89
  841.7 1.4 collective-permute-start.1
  844.2 36.4 %copy-start.90 = (bf16[512,1536]{1,0:T(8,128)(2,1)S(1)}, bf16[512,1536]{1,0:T(8,128)(2,1)}, u32[]{:S(2)}) copy-start(bf16[512,1536]{1,0:T(8,128)(2,1)} %pad_maximum_fusion.2) | copy-start | bytes 4718596
  885.7 24.6 %copy-start.101 = (f32[96,16]{1,0:T(8,128)S(1)}, f32[96,16]{1,0:T(8,128)}, u32[]{:S(2)}) copy-start(f32[96,16]{1,0:T(8,128)} %slice.135) | copy-start | bytes 18436
  885.7 25.3 %copy-start.100 = (bf16[96,1536]{1,0:T(8,128)(2,1)S(1)}, bf16[96,1536]{1,0:T(8,128)(2,1)}, u32[]{:S(2)}) copy-start(bf16[96,1536]{1,0:T(8,128)(2,1)} %reduce-scatter.13.cloned.1.call-done) | copy-start | bytes 884740
  885.7 26.1 %copy-start.32 = (bf16[192,2048]{1,0:T(8,128)(2,1)S(1)}, bf16[192,2048]{1,0:T(8,128)(2,1)}, u32[]{:S(2)}) copy-start(bf16[192,2048]{1,0:T(8,128)(2,1)} %reduce-scatter.11.cloned.1.call-done) | copy-start | bytes 2359300
  885.7 26.1 %copy-start.44 = (bf16[192,768]{1,0:T(8,128)(2,1)S(1)}, bf16[192,768]{1,0:T(8,128)(2,1)}, u32[]{:S(2)}) copy-start(bf16[192,768]{1,0:T(8,128)(2,1)} %reduce-scatter.17.cloned.1.call-done) | copy-start | bytes 884740
  974.4 9.4 copy-start.46
  (100 other events, 218.3 us)
Sparse Core Ops, SparseCore 0:
  9.7 43.1 all-gather.4
  95.0 68.8 all-gather.6
  166.1 68.9 all-gather.8
  236.6 75.1 all-gather.10
  421.2 102.1 reduce-scatter.6
  585.8 56.6 reduce-scatter.8
  650.3 99.0 reduce-scatter.10
  751.8 36.5 reduce-scatter.12
  790.8 35.4 reduce-scatter.16
  838.7 50.5 reduce-scatter.14

commit v4 on v3

--- a/solution.py
+++ b/solution.py
@@ -95,12 +95,20 @@
     return x * lax.rsqrt(jnp.mean(x * x, axis=-1, keepdims=True) + EPS)
 
 
-def first_body(
-    T, n, x, seg, par, win, *refs
-):
-    srcs, refs = refs[:n], refs[n:]
+def column_blocks(w, gain, chunk, blocks):
+    groups = w.shape[1] // (W * chunk)
+    for q in range(W):
+        pieces = [w[:, (k * W + q) * chunk : (k * W + q + 1) * chunk] for k in range(groups)]
+        value = jnp.concatenate(pieces, axis=1) if groups > 1 else pieces[0]
+        blocks[q] = (value.astype(F32) * gain).astype(BF)
+
+
+def first_body(T, chunks, x, seg, state, rows_in, log_in, gains, *refs):
+    n = len(chunks) - 1
+    weights, refs = refs[: n + 1], refs[n + 1 :]
     nh, seg_out, par_out, w_in = refs[:4]
     dsts, refs = refs[4 : 4 + n], refs[4 + n :]
+    win, srcs, par, refs = refs[0], refs[1 : n + 1], refs[n + 1], refs[n + 2 :]
     (nbuf, zbuf, s_n, r_n, s_h, r_h, s_s, r_s, s_p, r_p, s_w, r_w, s_z, r_z, s_c, r_c, s_l, s_o, r_o) = refs
     t, p, c = here()
     B = x.shape[0]
@@ -115,8 +123,7 @@
             if dt == 0 or dp == 0:
                 greet((tt, pp, 1 - c))
                 count += 1
-    nbuf[...] = unit(x[...].astype(F32)).astype(BF)
-    zbuf[...] = jnp.zeros_like(zbuf)
+    column_blocks(weights[0], gains[:, 0:1], chunks[0], win)
     arrive(count)
     half = lax.div(p, 2)
     slot = lax.rem(p, 2) * 2 + c
@@ -157,6 +164,20 @@
 
     landing = w_in.at[t * 2 + half]
     exchange(win, landing, s_w, r_w)
+    nbuf[...] = unit(x[...].astype(F32)).astype(BF)
+    zbuf[...] = jnp.zeros_like(zbuf)
+    size = rows_in.shape[1]
+    eye = (
+        lax.broadcasted_iota(jnp.int32, (size, size), 0)
+        == lax.broadcasted_iota(jnp.int32, (size, size), 1)
+    ).astype(BF)
+    lines = nt(eye, rows_in[...]).astype(BF)
+    wide_at = state.shape[1]
+    par[:, 0:wide_at] = state[...]
+    par[:, wide_at:] = jnp.concatenate(
+        [lines, log_in[...], jnp.zeros((size, 256 - wide_at - lines.shape[1] - log_in.shape[1]), BF)],
+        axis=1,
+    )
     rows = pl.ds(pl.multiple_of(HALO + p * B, HALO), B)
     copies = []
     for dt in range(T):
@@ -205,6 +226,7 @@
         clear.wait()
 
     for i in range(n):
+        column_blocks(weights[i + 1], gains[:, i + 1 : i + 2], chunks[i + 1], srcs[i])
         exchange(srcs[i], dsts[i], s_o.at[i], r_o.at[i])
 
     def on(way, d, j):
@@ -309,21 +331,24 @@
                     on(way, d, j).wait_send()
 
 
-def first_call(T, x, seg, par, win, others):
+def first_call(T, x, seg, state, rows_in, log_in, gains, weights, chunks):
     B, D = x.shape
-    n = len(others)
+    n = len(weights) - 1
+    blocks = [(W, w.shape[0], w.shape[1] // W) for w in weights]
     return pl.pallas_call(
-        functools.partial(first_body, T, n),
+        functools.partial(first_body, T, chunks),
         out_shape=(
             out((HALO + W * B, D), BF),
             out((W * T,) + seg.shape, jnp.int32),
-            out((2 * T,) + par.shape, BF),
-            out((2 * T,) + win.shape, BF),
+            out((2 * T, state.shape[0], 256), BF),
+            out((2 * T,) + blocks[0], BF),
         )
-        + tuple(out(a.shape, BF) for a in others),
-        in_specs=[vmem()] + [hbm()] * (3 + n),
+        + tuple(out(b, BF) for b in blocks[1:]),
+        in_specs=[vmem(), hbm()] + [vmem()] * (5 + n),
         out_specs=(hbm(),) * (4 + n),
-        scratch_shapes=[
+        scratch_shapes=[pltpu.VMEM(b, BF) for b in blocks]
+        + [
+            pltpu.VMEM((state.shape[0], 256), BF),
             pltpu.VMEM((B, D), BF),
             pltpu.VMEM((HALO, D), BF),
             dma(W), dma(W), dma(W), pltpu.SemaphoreType.DMA,
@@ -333,85 +358,139 @@
         ],
         compiler_params=talk(0),
         name="first",
-    )(x, seg, par, win, *others)
-
-
-def spread_body(n, back, *refs):
-    srcs, dsts = refs[:n], refs[n : 2 * n]
-    s_w, r_w = refs[2 * n :]
-    t, p, c = here()
-    half = lax.div(p, 2)
-    pair = lax.rem(p, 2) * 2 + c
-    both = half == c
-
-    def there(q):
-        if back:
-            return (t, c * 2 + q // 2, jnp.int32(q % 2))
-        return (t, jnp.int32(q), half)
-
-    def comes(j):
-        if back:
-            return (t, jnp.int32(j), half)
-        return (t, c * 2 + j // 2, jnp.int32(j % 2))
-
-    slot = p if back else pair
-    for q in range(W):
-        to, source = there(q), comes(q)
-        own = both & ((pair == q) if back else (p == q))
-        from_me = both & ((p == q) if back else (pair == q))
-
-        @pl.when(jnp.logical_not(from_me))
-        def _():
-            greet(source)
-
-    arrive(W - both.astype(jnp.int32))
-    for q in range(W):
-        own = both & ((pair == q) if back else (p == q))
-        for a in range(n):
-
-            @pl.when(jnp.logical_not(own))
+    )(x, seg, state, rows_in, log_in, gains, *weights)
+
+
+class Job:
+    def __init__(self, build, inputs, in_specs, shapes, specs, scratch):
+        self.build, self.inputs, self.in_specs = build, tuple(inputs), list(in_specs)
+        self.shapes, self.specs, self.scratch = tuple(shapes), tuple(specs), list(scratch)
+
+
+def take(refs, count):
+    head = refs[:count]
+    del refs[:count]
+    return head
+
+
+def started(jobs, ins, outs, scratch):
+    made = []
+    for job in jobs:
+        made.append(
+            job.build(
+                take(ins, len(job.inputs)), take(outs, len(job.shapes)), take(scratch, len(job.scratch))
+            )
+        )
+    return made
+
+
+def spread_build(n, back):
+    def build(srcs, dsts, sems):
+        s_w, r_w = sems
+        t, p, c = here()
+        half = lax.div(p, 2)
+        pair = lax.rem(p, 2) * 2 + c
+        both = half == c
+
+        def there(q):
+            if back:
+                return (t, c * 2 + q // 2, jnp.int32(q % 2))
+            return (t, jnp.int32(q), half)
+
+        def comes(j):
+            if back:
+                return (t, jnp.int32(j), half)
+            return (t, c * 2 + j // 2, jnp.int32(j % 2))
+
+        slot = p if back else pair
+
+        def own(q):
+            return both & ((pair == q) if back else (p == q))
+
+        def from_me(q):
+            return both & ((p == q) if back else (pair == q))
+
+        def away(a, q):
+            return remote(
+                srcs[a].at[q], dsts[a].at[slot], s_w.at[a, q], r_w.at[a, slot], there(q)
+            )
+
+        def kept(a, q):
+            return pltpu.make_async_copy(srcs[a].at[q], dsts[a].at[slot], s_w.at[a, q])
+
+        for q in range(W):
+            source = comes(q)
+
+            @pl.when(jnp.logical_not(from_me(q)))
             def _():
-                remote(
-                    srcs[a].at[q], dsts[a].at[slot], s_w.at[a, q], r_w.at[a, slot], there(q)
-                ).start()
-
-            @pl.when(own)
-            def _():
-                pltpu.make_async_copy(srcs[a].at[q], dsts[a].at[slot], s_w.at[a, q]).start()
-
-    for q in range(W):
-        own = both & ((pair == q) if back else (p == q))
-        from_me = both & ((p == q) if back else (pair == q))
-        for a in range(n):
-
-            @pl.when(jnp.logical_not(own))
-            def _():
-                remote(
-                    srcs[a].at[q], dsts[a].at[slot], s_w.at[a, q], r_w.at[a, slot], there(q)
-                ).wait_send()
-
-            @pl.when(own)
-            def _():
-                pltpu.make_async_copy(srcs[a].at[q], dsts[a].at[slot], s_w.at[a, q]).wait()
-
-            @pl.when(jnp.logical_not(from_me))
-            def _():
-                remote(
-                    srcs[a].at[q], dsts[a].at[q], s_w.at[a, q], r_w.at[a, q], there(q)
-                ).wait_recv()
-
-
-def spread_call(cid, back, arrays):
+                greet(source)
+
+        def begin():
+            for a in range(n):
+                for q in range(W):
+
+                    @pl.when(jnp.logical_not(own(q)))
+                    def _():
+                        away(a, q).start()
+
+                    @pl.when(own(q))
+                    def _():
+                        kept(a, q).start()
+
+        def end():
+            for a in range(n):
+                for q in range(W):
+
+                    @pl.when(jnp.logical_not(own(q)))
+                    def _():
+                        away(a, q).wait_send()
+
+                    @pl.when(own(q))
+                    def _():
+                        kept(a, q).wait()
+
+                    @pl.when(jnp.logical_not(from_me(q)))
+                    def _():
+                        remote(
+                            srcs[a].at[q], dsts[a].at[q], s_w.at[a, q], r_w.at[a, q], there(q)
+                        ).wait_recv()
+
+        return W - both.astype(jnp.int32), begin, end
+
+    return build
+
+
+def spread_job(back, arrays):
     n = len(arrays)
+    return Job(
+        spread_build(n, back), arrays, [hbm()] * n,
+        [out(a.shape, a.dtype) for a in arrays], [hbm()] * n, [dma(n, W), dma(n, W)],
+    )
+
+
+def jobs_body(counts, jobs, *refs):
+    refs = list(refs)
+    ins, outs = take(refs, counts[0]), take(refs, counts[1])
+    made = started(jobs, ins, outs, refs)
+    arrive(sum(m[0] for m in made))
+    for m in made:
+        m[1]()
+    for m in made:
+        m[2]()
+
+
+def run_jobs(cid, *jobs):
+    inputs = sum((j.inputs for j in jobs), ())
+    shapes = sum((j.shapes for j in jobs), ())
     return pl.pallas_call(
-        functools.partial(spread_body, n, back),
-        out_shape=tuple(out(a.shape, a.dtype) for a in arrays),
-        in_specs=[hbm()] * n,
-        out_specs=(hbm(),) * n,
-        scratch_shapes=[dma(n, W), dma(n, W)],
+        functools.partial(jobs_body, (len(inputs), len(shapes)), jobs),
+        out_shape=shapes,
+        in_specs=sum((j.in_specs for j in jobs), []),
+        out_specs=sum((j.specs for j in jobs), ()),
+        scratch_shapes=sum((j.scratch for j in jobs), []),
         compiler_params=talk(cid),
-        name="spread%d" % cid,
-    )(*arrays)
+        name="jobs%d" % cid,
+    )(*inputs)
 
 
 def plane_sum_body(x, o, sb, recv, ss, rs):
@@ -451,111 +530,215 @@
     )(x)
 
 
-def gather_job(T, src, dst, s_z, r_z, s_c, r_c, s_l):
-    t, p, c = here()
-
-    def part(dt, core):
-        return dst.at[lax.rem(t - dt + T, T) * 2 + core]
-
-    def out_to(dt):
-        return remote(src, part(0, c), s_z.at[dt], r_z.at[dt], (lax.rem(t + dt, T), p, c))
-
-    def across(dt):
-        return remote(src if dt == 0 else part(dt, c), part(dt, c), s_c.at[dt], r_c.at[dt], (t, p, 1 - c))
-
-    keep = pltpu.make_async_copy(src, part(0, c), s_l)
-
-    def begin():
+def gather_job(T, piece):
+    def build(ins, outs, sems):
+        (src,), (dst,) = ins, outs
+        s_z, r_z, s_c, r_c, s_l = sems
+        t, p, c = here()
+
+        def part(dt, core):
+            return dst.at[lax.rem(t - dt + T, T) * 2 + core]
+
+        def out_to(dt):
+            return remote(src, part(0, c), s_z.at[dt], r_z.at[dt], (lax.rem(t + dt, T), p, c))
+
+        def across(dt):
+            return remote(
+                src if dt == 0 else part(dt, c), part(dt, c), s_c.at[dt], r_c.at[dt], (t, p, 1 - c)
+            )
+
+        keep = pltpu.make_async_copy(src, part(0, c), s_l)
         for dt in range(1, T):
-            out_to(dt).start()
-        across(0).start()
-        keep.start()
-
-    def end():
+            greet((lax.rem(t + dt, T), p, c))
+        greet((t, p, 1 - c))
+
+        def begin():
+            for dt in range(1, T):
+                out_to(dt).start()
+            across(0).start()
+            keep.start()
+
+        def end():
+            for dt in range(1, T):
+                out_to(dt).wait_recv()
+                across(dt).start()
+            keep.wait()
+            for dt in range(T):
+                across(dt).wait_send()
+                other = part(dt, 1 - c)
+                remote(other, other, s_c.at[dt], r_c.at[dt], (t, p, 1 - c)).wait_recv()
+            for dt in range(1, T):
+                out_to(dt).wait_send()
+
+        return T, begin, end
+
+    return Job(
+        build, [piece], [hbm()], [out((2 * T,) + piece.shape, BF)], [hbm()],
+        [dma(T), dma(T), dma(T), dma(T), pltpu.SemaphoreType.DMA],
+    )
+
+
+def scatter_job(T, grad):
+    grad = grad.reshape(2 * T, -1, grad.shape[-1])
+
+    def build(ins, outs, scratch):
+        (src,), (dst,) = ins, outs
+        mine, other, recv, s_z, r_z, s_c, r_c, s_l = scratch
+        t, p, c = here()
+
+        def at(dt):
+            return lax.rem(t + dt, T)
+
+        def across(dt):
+            return remote(
+                src.at[at(dt) * 2 + 1 - c], other.at[dt], s_c.at[dt], r_c.at[dt], (t, p, 1 - c)
+            )
+
+        def load(dt):
+            return pltpu.make_async_copy(src.at[at(dt) * 2 + c], mine.at[dt], s_l.at[dt])
+
+        def out_to(dt):
+            return remote(mine.at[dt], recv.at[dt - 1], s_z.at[dt], r_z.at[dt], (at(dt), p, c))
+
+        order = list(range(1, T)) + [0]
         for dt in range(1, T):
-            out_to(dt).wait_recv()
-            across(dt).start()
-        keep.wait()
-        for dt in range(T):
-            across(dt).wait_send()
-            remote(part(dt, 1 - c), part(dt, 1 - c), s_c.at[dt], r_c.at[dt], (t, p, 1 - c)).wait_recv()
-        for dt in range(1, T):
-            out_to(dt).wait_send()
-
-    return begin, end
-
-
-def scatter_job(T, src, dst, mine, other, recv, s_z, r_z, s_c, r_c, s_l):
-    t, p, c = here()
-
-    def at(dt):
-        return lax.rem(t + dt, T)
-
-    def across(dt):
-        return remote(
-            src.at[at(dt) * 2 + 1 - c], other.at[dt], s_c.at[dt], r_c.at[dt], (t, p, 1 - c)
-        )
-
-    def load(dt):
-        return pltpu.make_async_copy(src.at[at(dt) * 2 + c], mine.at[dt], s_l.at[dt])
-
-    def out_to(dt):
-        return remote(mine.at[dt], recv.at[dt - 1], s_z.at[dt], r_z.at[dt], (at(dt), p, c))
-
-    order = list(range(1, T)) + [0]
-
-    def begin():
-        for dt in order:
-            across(dt).start()
-            load(dt).start()
-        for dt in order[:-1]:
-            across(dt).wait_recv()
-            load(dt).wait()
-            mine[dt] = (mine[dt].astype(F32) + other[dt].astype(F32)).astype(BF)
-            out_to(dt).start()
-
-    def end():
-        across(0).wait_recv()
-        load(0).wait()
-        total = mine[0].astype(F32) + other[0].astype(F32)
-        for dt in range(1, T):
-            out_to(dt).wait_recv()
-            total = total + recv[dt - 1].astype(F32)
-        dst[...] = total
-        for dt in range(T):
-            across(dt).wait_send()
-        for dt in range(1, T):
-            out_to(dt).wait_send()
-
-    return begin, end
-
-
-def turn_body(T, back, gather, parts, job, *refs):
+            greet((at(dt), p, c))
+        greet((t, p, 1 - c))
+
+        def begin():
+            for dt in order:
+                across(dt).start()
+                load(dt).start()
+            for dt in order[:-1]:
+                across(dt).wait_recv()
+                load(dt).wait()
+                mine[dt] = (mine[dt].astype(F32) + other[dt].astype(F32)).astype(BF)
+                out_to(dt).start()
+
+        def end():
+            across(0).wait_recv()
+            load(0).wait()
+            total = mine[0].astype(F32) + other[0].astype(F32)
+            for dt in range(1, T):
+                out_to(dt).wait_recv()
+                total = total + recv[dt - 1].astype(F32)
+            dst[...] = total
+            for dt in range(T):
+                across(dt).wait_send()
+            for dt in range(1, T):
+                out_to(dt).wait_send()
+
+        return T, begin, end
+
+    shape = grad.shape[1:]
+    return Job(
+        build, [grad], [hbm()], [out(shape)], [vmem()],
+        [
+            pltpu.VMEM((T,) + shape, BF),
+            pltpu.VMEM((T,) + shape, BF),
+            pltpu.VMEM((T - 1,) + shape, BF),
+            dma(T), dma(T), dma(T), dma(T), dma(T),
+        ],
+    )
+
+
+def small_job(T, x):
+    peers = [(dt, dc) for dt in range(T) for dc in range(2) if dt or dc]
+    n = len(peers)
+
+    def build(ins, outs, scratch):
+        (src,), (dst,) = ins, outs
+        recv, ss, rs = scratch
+        t, p, c = here()
+
+        def copy(i):
+            dt, dc = peers[i]
+            tt, cc = lax.rem(t + dt, T), flip(c, dc)
+            return remote(src.at[tt * 2 + cc], recv.at[i], ss.at[i], rs.at[i], (tt, p, cc))
+
+        for dt, dc in peers:
+            greet((lax.rem(t + dt, T), p, flip(c, dc)))
+
+        def begin():
+            for i in range(n):
+                copy(i).start()
+
+        def end():
+            total = src[t * 2 + c].astype(F32)
+            for i in range(n):
+                copy(i).wait()
+                total = total + recv[i].astype(F32)
+            dst[...] = total
+
+        return n, begin, end
+
+    return Job(
+        build, [x], [vmem()], [out(x.shape[1:])], [vmem()],
+        [pltpu.VMEM((n,) + x.shape[1:], x.dtype), dma(n), dma(n)],
+    )
+
+
+def sum_job(part, x, dtype):
+    B, D = x.shape
+
+    def build(ins, outs, scratch):
+        src, base = ins
+        (o,) = outs
+        own, recv, ss, rs, ls = scratch
+        t, p, c = here()
+
+        def copy(d):
+            q = flip(p, d)
+            return remote(
+                src.at[pl.ds(pl.multiple_of(q * B, B), B)], recv.at[d - 1],
+                ss.at[d - 1], rs.at[d - 1], (t, q, c),
+            )
+
+        local = pltpu.make_async_copy(src.at[pl.ds(pl.multiple_of(p * B, B), B)], own, ls)
+        for d in range(1, W):
+            greet((t, flip(p, d), c))
+
+        def begin():
+            for d in range(1, W):
+                copy(d).start()
+            local.start()
+
+        def end():
+            local.wait()
+            total = base[...] + own[...].astype(F32)
+            for d in range(1, W):
+                copy(d).wait()
+                total = total + recv[d - 1].astype(F32)
+            o[...] = total.astype(o.dtype)
+
+        return W - 1, begin, end
+
+    return Job(
+        build, [part, x], [hbm(), vmem()], [out((B, D), dtype)], [vmem()],
+        [
+            pltpu.VMEM((B, D), BF), pltpu.VMEM((W - 1, B, D), BF),
+            dma(W - 1), dma(W - 1), pltpu.SemaphoreType.DMA,
+        ],
+    )
+
+
+def turn_body(back, gather, parts, jobs, counts, *refs):
     refs = list(refs)
-    part = refs.pop(0)
-    x = refs.pop(0)
-    g = refs.pop(0) if back else None
-    job_src = refs.pop(0) if job else None
-    o = refs.pop(0)
-    gath = refs.pop(0) if gather else None
-    job_dst = refs.pop(0) if job else None
-    own, recv, sbuf, ss, rs, ls, ss2, rs2, ls2 = refs[:9]
+    ins, outs = take(refs, counts[0]), take(refs, counts[1])
+    part, x = take(ins, 2)
+    g = take(ins, 1)[0] if back else None
+    o = take(outs, 1)[0]
+    gath = take(outs, 1)[0] if gather else None
+    own, recv, sbuf, ss, rs, ls, ss2, rs2, ls2 = take(refs, 9)
     t, p, c = here()
     B = x.shape[0]
     rows = B // parts
     for d in range(1, W):
         greet((t, flip(p, d), c))
-    count = W - 1
-    if job:
-        for dt in range(1, T):
-            greet((lax.rem(t + dt, T), p, c))
-        greet((t, p, 1 - c))
-        count += T
-        build = gather_job if job == "gather" else scatter_job
-        begin, end = build(T, job_src, job_dst, *refs[9:])
+    made = started(jobs, ins, outs, refs)
     local = pltpu.make_async_copy(part.at[pl.ds(pl.multiple_of(p * B, B), B)], own, ls)
     local.start()
-    arrive(count)
+    arrive(sum((m[0] for m in made), W - 1))
     first = {}
     for k in range(parts):
         for d in range(1, W):
@@ -568,8 +751,8 @@
                 (t, q, c),
             )
             first[k, d].start()
-    if job:
-        begin()
+    for m in made:
+        m[1]()
     local.wait()
     later = []
     for k in range(parts):
@@ -597,21 +780,23 @@
             later.append(pltpu.make_async_copy(sbuf.at[cut], place, ls2.at[k]))
             for copy in later[-W:]:
                 copy.start()
-    if job:
-        end()
+    for m in made:
+        m[2]()
     for copy in first.values():
         copy.wait_send()
     for copy in later:
         copy.wait()
 
 
-def turn(cid, part, x, g=None, gather=True, dtype=F32, parts=2, T=1, fetch=None, give=None):
+def turn(cid, part, x, g=None, gather=True, dtype=F32, parts=2, jobs=()):
     B, D = x.shape
     back = g is not None
-    shapes = [out((B, D), dtype)]
-    specs = [vmem()]
     args = (part, x) + ((g,) if back else ())
     in_specs = [hbm()] + [vmem()] * (len(args) - 1)
+    shapes, specs = (out((B, D), dtype),), (vmem(),)
+    if gather:
+        shapes += (out((W * B, D), BF),)
+        specs += (hbm(),)
     scratch = [
         pltpu.VMEM((B, D), BF),
         pltpu.VMEM((W - 1, B, D), BF),
@@ -619,42 +804,29 @@
         dma(W - 1, parts), dma(W - 1, parts), pltpu.SemaphoreType.DMA,
         dma(W - 1, parts), dma(W - 1, parts), dma(parts),
     ]
-    if gather:
-        shapes.append(out((W * B, D), BF))
-        specs.append(hbm())
-    job = None
-    if fetch is not None:
-        job = "gather"
-        args += (fetch,)
-        in_specs.append(hbm())
-        shapes.append(out((2 * T,) + fetch.shape, BF))
-        specs.append(hbm())
-        scratch += [dma(T), dma(T), dma(T), dma(T), pltpu.SemaphoreType.DMA]
-    if give is not None:
-        job = "scatter"
-        give = give.reshape(2 * T, -1, give.shape[-1])
-        args += (give,)
-        in_specs.append(hbm())
-        shapes.append(out(give.shape[1:]))
-        specs.append(vmem())
-        scratch += [
-            pltpu.VMEM((T,) + give.shape[1:], BF),
-            pltpu.VMEM((T,) + give.shape[1:], BF),
-            pltpu.VMEM((T - 1,) + give.shape[1:], BF),
-            dma(T), dma(T), dma(T), dma(T), dma(T),
-        ]
+    for job in jobs:
+        args += job.inputs
+        in_specs += job.in_specs
+        shapes += job.shapes
+        specs += job.specs
+        scratch += job.scratch
     return pl.pallas_call(
-        functools.partial(turn_body, T, back, gather, parts, job),
-        out_shape=tuple(shapes),
+        functools.partial(turn_body, back, gather, parts, jobs, (len(args), len(shapes))),
+        out_shape=shapes,
         in_specs=in_specs,
-        out_specs=tuple(specs),
+        out_specs=specs,
         scratch_shapes=scratch,
         compiler_params=talk(cid),
         name="turn%d" % cid,
     )(*args)
 
 
-def chain_body(T, back, v, a2, h, recv, ss, rs):
+def chain_body(T, back, jobs, counts, *refs):
+    refs = list(refs)
+    ins, outs = take(refs, counts[0]), take(refs, counts[1])
+    v, a2 = take(ins, 2)
+    (h,) = take(outs, 1)
+    recv, ss, rs = take(refs, 3)
     t, p, c = here()
     sign = -1 if back else 1
     for k in range(1, T):
@@ -664,7 +836,8 @@
         def _():
             greet((lax.rem(source + T, T), p, c))
 
-    arrive_some(t if back else T - 1 - t)
+    made = started(jobs, ins, outs, refs)
+    arrive_some(sum((m[0] for m in made), t if back else T - 1 - t))
 
     def send(k):
         to = lax.rem(t + sign * k + T, T)
@@ -677,6 +850,8 @@
         def _():
             send(k).start()
 
+    for m in made:
+        m[1]()
     h[...] = jnp.zeros_like(h)
     for k in range(T - 1, 0, -1):
         source = t - sign * k
@@ -694,17 +869,29 @@
         def _():
             send(k).wait_send()
 
-
-def chain(cid, T, back, v, a2):
+    for m in made:
+        m[2]()
+
+
+def chain(cid, T, back, v, a2, jobs=()):
+    args, in_specs = (v, a2), [vmem(), vmem()]
+    shapes, specs = (out(a2.shape),), (vmem(),)
+    scratch = [pltpu.VMEM((T - 1,) + v.shape, F32), dma(T - 1), dma(T - 1)]
+    for job in jobs:
+        args += job.inputs
+        in_specs += job.in_specs
+        shapes += job.shapes
+        specs += job.specs
+        scratch += job.scratch
     return pl.pallas_call(
-        functools.partial(chain_body, T, back),
-        out_shape=out(a2.shape),
-        in_specs=[vmem(), vmem()],
-        out_specs=vmem(),
-        scratch_shapes=[pltpu.VMEM((T - 1,) + v.shape, F32), dma(T - 1), dma(T - 1)],
+        functools.partial(chain_body, T, back, jobs, (len(args), len(shapes))),
+        out_shape=shapes,
+        in_specs=in_specs,
+        out_specs=specs,
+        scratch_shapes=scratch,
         compiler_params=talk(cid),
         name="chain%d" % cid,
-    )(v, a2)
+    )(*args)
 
 
 def rope(w, cosine, sine):
@@ -812,7 +999,12 @@
     )(qkv, cosine, sine, ct)
 
 
-def keys_back_body(T, hops, dq, dk, dv, cosine, sine, dqkv, sb, recv, ss, rs):
+def keys_back_body(T, hops, jobs, counts, *refs):
+    refs = list(refs)
+    ins, outs = take(refs, counts[0]), take(refs, counts[1])
+    dq, dk, dv, cosine, sine = take(ins, 5)
+    (dqkv,) = take(outs, 1)
+    sb, recv, ss, rs = take(refs, 4)
     t, p, c = here()
     CH = dq.shape[0]
     width = dq.shape[1]
@@ -820,6 +1012,9 @@
     @pl.when(t < T - 1)
     def _():
         greet((lax.rem(t + 1, T), p, c))
+
+    made = started(jobs, ins, outs, refs)
+    extra = sum(m[0] for m in made)
 
     def send(a, d):
         return remote(
@@ -840,7 +1035,14 @@
 
             @pl.when(t > 0)
             def _():
-                arrive(1)
+                arrive(1 + extra)
+
+            if extra:
+
+                @pl.when(t == 0)
+                def _():
+                    arrive(extra)
+
         else:
 
             @pl.when((t < T - 1) & (t >= d))
@@ -862,6 +1064,8 @@
             send(1, d).start()
 
         if d == hops:
+            for m in made:
+                m[1]()
             for h in range(width // HD):
                 cols = pl.ds(h * HD, HD)
                 dqkv[:, cols] = rope(dq[:, cols], cosine[...], -sine[...]).astype(BF)
@@ -883,6 +1087,8 @@
         v_sum = dv[mine, cols] + recv[1, 0, :, cols].astype(F32)
         dqkv[:, pl.ds(width + h * HD, HD)] = rope(k_sum, cosine[...], -sine[...]).astype(BF)
         dqkv[:, pl.ds(2 * width + h * HD, HD)] = v_sum.astype(BF)
+    for m in made:
+        m[2]()
     for d in range(hops, 0, -1):
 
         @pl.when(t >= d)
@@ -891,22 +1097,29 @@
             send(1, d).wait_send()
 
 
-def keys_back_call(cid, T, hops, dq, dk, dv, cosine, sine):
+def keys_back_call(cid, T, hops, dq, dk, dv, cosine, sine, jobs=()):
     CH, width = dq.shape
+    args, in_specs = (dq, dk, dv, cosine, sine), [vmem()] * 5
+    shapes, specs = (out((CH, 3 * width), BF),), (vmem(),)
+    scratch = [
+        pltpu.VMEM((2, hops, CH, width), BF), pltpu.VMEM((2, hops, CH, width), BF),
+        dma(2, hops), dma(2, hops),
+    ]
+    for job in jobs:
+        args += job.inputs
+        in_specs += job.in_specs
+        shapes += job.shapes
+        specs += job.specs
+        scratch += job.scratch
     return pl.pallas_call(
-        functools.partial(keys_back_body, T, hops),
-        out_shape=out((CH, 3 * width), BF),
-        in_specs=[vmem()] * 5,
-        out_specs=vmem(),
-        scratch_shapes=[
-            pltpu.VMEM((2, hops, CH, width), BF),
-            pltpu.VMEM((2, hops, CH, width), BF),
-            dma(2, hops),
-            dma(2, hops),
-        ],
+        functools.partial(keys_back_body, T, hops, jobs, (len(args), len(shapes))),
+        out_shape=shapes,
+        in_specs=in_specs,
+        out_specs=specs,
+        scratch_shapes=scratch,
         compiler_params=talk(cid, 48),
         name="keys_back",
-    )(dq, dk, dv, cosine, sine)
+    )(*args)
 
 
 def rim_body(T, x, o, recv, ss, rs):
@@ -942,42 +1155,6 @@
         scratch_shapes=[pltpu.VMEM(x.shape, F32), pltpu.SemaphoreType.DMA, pltpu.SemaphoreType.DMA],
         compiler_params=talk(cid),
         name="rim_back",
-    )(x)
-
-
-def small_body(T, x, o, recv, ss, rs):
-    t, p, c = here()
-    peers = [(dt, dc) for dt in range(T) for dc in range(2) if dt or dc]
-
-    def device(dt, dc):
-        return lax.rem(t + dt, T), flip(c, dc)
-
-    for dt, dc in peers:
-        tt, cc = device(dt, dc)
-        greet((tt, p, cc))
-    arrive(len(peers))
-    copies = []
-    for i, (dt, dc) in enumerate(peers):
-        tt, cc = device(dt, dc)
-        copies.append(remote(x.at[tt * 2 + cc], recv.at[i], ss.at[i], rs.at[i], (tt, p, cc)))
-        copies[-1].start()
-    total = x[t * 2 + c].astype(F32)
-    for i, copy in enumerate(copies):
-        copy.wait()
-        total = total + recv[i].astype(F32)
-    o[...] = total
-
-
-def small_sum(cid, T, x):
-    n = x.shape[0] - 1
-    return pl.pallas_call(
-        functools.partial(small_body, T),
-        out_shape=out(x.shape[1:]),
-        in_specs=[vmem()],
-        out_specs=vmem(),
-        scratch_shapes=[pltpu.VMEM((n,) + x.shape[1:], x.dtype), dma(n), dma(n)],
-        compiler_params=talk(cid),
-        name="small_sum",
     )(x)
 
 
@@ -1328,20 +1505,40 @@
     )(q, k, v, bias, lse, do)
 
 
-def columns_out(weight, gain, groups, T, cols):
-    rows = weight.shape[0]
-    scaled = (weight.astype(F32) * gain.astype(F32)[:, None]).astype(BF)
-    return scaled.reshape(rows, groups, T, W, cols).transpose(3, 0, 1, 2, 4).reshape(W, rows, -1)
-
-
-def columns_back(blocks, groups, T, cols):
-    rows = blocks.shape[1]
-    wide_form = blocks.reshape(W, rows, groups, T, cols).transpose(1, 2, 3, 0, 4)
-    return wide_form.reshape(rows, -1).astype(F32)
+def finish_body(n, chunk, *refs):
+    blocks, (w, gain, o, total) = refs[:n], refs[n:]
+    acc = jnp.zeros((w.shape[0], 1), F32)
+    at = 0
+    for b in blocks:
+        for k in range(b.shape[2] // chunk):
+            pieces = [b[q, :, k * chunk : (k + 1) * chunk] for q in range(W)]
+            value = jnp.concatenate(pieces, axis=1).astype(F32)
+            cut = pl.ds(at, W * chunk)
+            acc = acc + jnp.sum(w[:, cut].astype(F32) * value, axis=1, keepdims=True)
+            o[:, cut] = value * gain[...]
+            at += W * chunk
+    total[...] = jnp.broadcast_to(acc, total.shape)
+
+
+def finish(blocks, w, gain, chunk):
+    rows = w.shape[0]
+    grad, total = pl.pallas_call(
+        functools.partial(finish_body, len(blocks), chunk),
+        out_shape=(out(w.shape), out((rows, 128))),
+        in_specs=[vmem()] * (len(blocks) + 2),
+        out_specs=(vmem(), vmem()),
+        compiler_params=alone(),
+        name="finish",
+    )(*blocks, w, gain.astype(F32).reshape(rows, 1))
+    return total[:, 0], grad
 
 
 def gather_tc(x):
     return lax.all_gather(x.reshape(-1, x.shape[-1]), ("t", "c"), axis=0, tiled=True)
+
+
+def blocks(x):
+    return x.reshape(W, x.shape[0] // W, x.shape[1])
 
 
 def together(*values):
@@ -1386,36 +1583,34 @@
     most = min(WIN, total // 2)
     hops = -(-(most - 1) // CH)
 
-    par = jnp.concatenate(
-        [
-            state_proj, step_proj.T, decay_log, conv_weight.T,
-            conv_bias[:, None], step_bias[:, None], skip_gain[:, None],
-        ],
-        axis=1,
-    )
-    used = par.shape[1]
-    par = jnp.pad(par, ((0, 0), (0, 256 - used)))
-    win_out = columns_out(in_proj, norm_mixer, 2, T, 2 * CB)
+    used = NR + R + N + 7
+    rows_in = jnp.concatenate(
+        [step_proj, conv_weight, conv_bias[None], step_bias[None], skip_gain[None]]
+        + [jnp.zeros((1, CB), BF)],
+        axis=0,
+    )
+    gains = jnp.stack([norm_mixer, norm_ffn_one, norm_attn, norm_ffn_two], axis=1).astype(F32)
+    chunks = (2 * CB, 2 * FB, heads, 2 * FB)
     seg8 = jnp.broadcast_to(segment_ids, (8, B))
     x0 = inputs[0].astype(F32)
-
-    gu1_out = columns_out(gate_up_one, norm_ffn_one, 2, T, 2 * FB)
-    qkv_out = columns_out(qkv_proj, norm_attn, 3, 1, heads)
-    gu2_out = columns_out(gate_up_two, norm_ffn_two, 2, T, 2 * FB)
     nh1_ext, seg_all, par_all, w_in, gu1_mine, qkv_mine, gu2_mine = first_call(
-        T, inputs[0], seg8, par, win_out, (gu1_out, qkv_out, gu2_out)
+        T, inputs[0], seg8, state_proj, rows_in, decay_log, gains,
+        (in_proj, gate_up_one, qkv_proj, gate_up_two), chunks,
     )
     w_in = w_in.reshape(D, -1)
+    nh1_ext, attn_late = together(nh1_ext, attn_out)
     devices = 2 * W * T
     pairs = []
     for d in range(devices):
         rest = d % (2 * T)
         pairs.append((d, (rest // 2) * 2 * W + (d // (2 * T)) * 2 + rest % 2))
-    ao_mine = lax.ppermute(attn_out, ("t", "p", "c"), pairs)
+    ao_mine = lax.ppermute(attn_late, ("t", "p", "c"), pairs)
     w_mix = gather_tc(mixer_out)
     w_gu1 = gather_tc(gu1_mine)
+    w_d1 = gather_tc(down_one)
     w_qkv = gather_tc(qkv_mine)
     w_gu2 = gather_tc(gu2_mine)
+    w_d2 = gather_tc(down_two)
 
     seg = seg_all[:, 0, :].reshape(total)
     pos = t * CH + jnp.arange(CH, dtype=jnp.int32)
@@ -1454,11 +1649,11 @@
     par_all = par_all.reshape(width, 256)
     w_state = par_all[:, :NR]
     w_step = par_all[:, NR : NR + R].T
-    side = par_all[:, NR + R : used].astype(F32).T
-    a2 = -jnp.exp(side[:N]) * LOG2E
-    taps = jnp.pad(side[N : N + 5], ((0, 3), (0, 0)))
-    step_row = side[N + 5 : N + 6]
-    skip_row = side[N + 6 : N + 7]
+    side = par_all[:, NR + R : NR + R + 8 + N].astype(F32).T
+    a2 = -jnp.exp(side[8:]) * LOG2E
+    taps = side[:8]
+    step_row = side[5:6]
+    skip_row = side[6:7]
 
     xz = nn(nh1_ext, w_in)
     nh1 = nh1_ext[HALO:]
@@ -1481,50 +1676,52 @@
         )
 
     end = scan_one(delta, u, a2, brep, first)
-    h_in = chain(4, T, False, packed(end), a2)
+    (h_in,) = chain(4, T, False, packed(end), a2)
     y_scan, marks = scan_two(delta, u, a2, brep, crep, first, h_in)
     y = y_scan + skip_row * u
     zg = xz[HALO:, width:]
     gate_s = jax.nn.sigmoid(zg)
     gated = (y * zg * gate_s).astype(BF)
-    x1, nh2, w_d1 = turn(5, nn(gated, w_mix).astype(BF), x0, T=T, fetch=down_one)
-    w_d1 = w_d1.reshape(-1, D)
+    x1, nh2 = turn(5, nn(gated, w_mix).astype(BF), x0)
 
     a_one = nn(nh2, w_gu1)
     h_one = swiglu(a_one).astype(BF)
-    x2, nh3, w_ao = turn(6, nn(h_one, w_d1).astype(BF), x1, T=T, fetch=ao_mine)
+    x2, nh3, w_ao = turn(6, nn(h_one, w_d1).astype(BF), x1, jobs=(gather_job(T, ao_mine),))
     w_ao = w_ao.reshape(-1, D)
 
     qkv = nn(nh3, w_qkv)
     q, k_all, v_all, gl4 = keys_call(7, T, hops, qkv, cosine, sine, cotangent[0])
     o, lse = attend(q, k_all, v_all, bias)
-    x3, nh4, w_d2 = turn(8, nn(o, w_ao).astype(BF), x2, T=T, fetch=down_two)
-    w_d2 = w_d2.reshape(-1, D)
+    x3, nh4 = turn(8, nn(o, w_ao).astype(BF), x2)
 
     a_two = nn(nh4, w_gu2)
     h_two = swiglu(a_two).astype(BF)
-    (final,) = turn(9, nn(h_two, w_d2).astype(BF), x3, gather=False, dtype=BF)
+    last_part = nn(h_two, w_d2).astype(BF)
 
     g4 = cotangent[0].astype(F32)
     dw_d2 = tn(h_two, gl4).astype(BF)
     da_two = swiglu_back(a_two, nt(gl4, w_d2))
     part, dw_gu2 = together(nt(da_two, w_gu2).astype(BF), tn(nh4, da_two).astype(BF))
-    g3, gl3, grad_d2 = turn(10, part, x3, g4, T=T, give=dw_d2)
     raw_gu2 = scatter_tc(dw_gu2)
+    g3, gl3 = turn(10, part, x3, g4)
 
     do, dw_ao = together(nt(gl3, w_ao).astype(BF), tn(o, gl3).astype(BF))
     dq, dk, dv = attend_back(q, k_all, v_all, bias, lse, do)
-    dq, final = together(dq, final)
-    dqkv = keys_back_call(11, T, hops, dq, dk, dv, cosine, sine)
+    dq, last_part, raw_gu2 = together(dq, last_part, raw_gu2)
+    dqkv, final = keys_back_call(
+        11, T, hops, dq, dk, dv, cosine, sine, jobs=(sum_job(last_part, x3, BF),)
+    )
+    dqkv, dw_d2 = together(dqkv, dw_d2)
+    grad_d2 = scatter_tc(dw_d2)
     part, dw_qkv = together(nt(dqkv, w_qkv).astype(BF), tn(nh3, dqkv).astype(BF))
     raw_qkv = scatter_tc(dw_qkv)
-    part, raw_gu2 = together(part, raw_gu2)
-    g2, gl2, raw_ao = turn(12, part, x2, g3, T=T, give=dw_ao)
+    g2, gl2, raw_ao = turn(12, part, x2, g3, jobs=(scatter_job(T, dw_ao),))
 
     da_one, dw_d1 = together(swiglu_back(a_one, nt(gl2, w_d1)), tn(h_one, gl2).astype(BF))
-    part, dw_gu1 = together(nt(da_one, w_gu1).astype(BF), tn(nh2, da_one).astype(BF))
+    part, dw_gu1, grad_d2 = together(nt(da_one, w_gu1).astype(BF), tn(nh2, da_one).astype(BF), grad_d2)
     raw_gu1 = scatter_tc(dw_gu1)
-    g1, gl1, grad_d1 = turn(13, part, x1, g2, T=T, give=dw_d1)
+    grad_d1 = scatter_tc(dw_d1)
+    g1, gl1 = turn(13, part, x1, g2)
     gl1, raw_qkv = together(gl1, raw_qkv)
 
     dgate = nt(gl1, w_mix)
@@ -1534,7 +1731,10 @@
     grad_mix = scatter_tc(dw_mix)
     raw_z = scatter_tc(dw_z)
     begin = scan_three(delta, dy, a2, crep, first)
-    g_in = chain(14, T, True, packed(begin), a2)
+    g_in, gu2_b, qkv_b = chain(
+        14, T, True, packed(begin), a2, jobs=(spread_job(True, (blocks(raw_gu2), blocks(raw_qkv))),)
+    )
+    g_in, grad_d1 = together(g_in, grad_d1)
     ddelta, du_scan, db, dc_mat, ga = scan_four(
         delta, u, dy, skip_row, a2, brep, crep, first, marks, g_in
     )
@@ -1559,8 +1759,6 @@
     dxz = jnp.concatenate([dxs_low, dz_low], axis=1)
     dxz, dw_x, grad_mix = together(dxz, tn(nh1, dxs_low).astype(BF), grad_mix)
     raw_x = scatter_tc(dw_x)
-    (grad_x,) = turn(17, nt(dxz, w_in).astype(BF), x0, g1, gather=False)
-
     small = jnp.concatenate(
         [
             tn(u_low, dpr_low),
@@ -1574,29 +1772,17 @@
     )
     small = jnp.pad(small, ((0, 0), (0, 256 - used))).astype(BF).reshape(2 * T, CB, 256)
     small, raw_z = together(small, raw_z)
-    small = small_sum(18, T, small)
-
-    def blocks(x):
-        return x.reshape(W, x.shape[0] // W, x.shape[1])
-
-    gu2_b, qkv_b, gu1_b, z_b = spread_call(
-        19, True, (blocks(raw_gu2), blocks(raw_qkv), blocks(raw_gu1), blocks(raw_z))
-    )
-    (x_b,) = spread_call(20, True, (blocks(raw_x),))
-    in_b = jnp.concatenate([x_b, z_b], axis=2)
+    grad_x, small, gu1_b = turn(
+        17, nt(dxz, w_in).astype(BF), x0, g1, gather=False,
+        jobs=(small_job(T, small), spread_job(True, (blocks(raw_gu1),))),
+    )
+    x_b, z_b = run_jobs(20, spread_job(True, (blocks(raw_x), blocks(raw_z))))
     grad_ao = lax.ppermute(raw_ao.astype(BF), ("t", "p", "c"), [(b, a) for a, b in pairs]).astype(F32)
 
-    def finished(blocks_in, weight, gain, groups, groups_t, cols):
-        raw = columns_back(blocks_in, groups, groups_t, cols)
-        return (
-            jnp.sum(weight.astype(F32) * raw, axis=1),
-            raw * gain.astype(F32)[:, None],
-        )
-
-    grad_n1, grad_in = finished(in_b, in_proj, norm_mixer, 2, T, 2 * CB)
-    grad_n2, grad_gu1 = finished(gu1_b, gate_up_one, norm_ffn_one, 2, T, 2 * FB)
-    grad_n3, grad_qkv = finished(qkv_b, qkv_proj, norm_attn, 3, 1, heads)
-    grad_n4, grad_gu2 = finished(gu2_b, gate_up_two, norm_ffn_two, 2, T, 2 * FB)
+    grad_n1, grad_in = finish((x_b, z_b), in_proj, norm_mixer, chunks[0])
+    grad_n2, grad_gu1 = finish((gu1_b,), gate_up_one, norm_ffn_one, chunks[1])
+    grad_n3, grad_qkv = finish((qkv_b,), qkv_proj, norm_attn, chunks[2])
+    grad_n4, grad_gu2 = finish((gu2_b,), gate_up_two, norm_ffn_two, chunks[3])
     at = NR + R + N
     return (
         final[None],
@@ -1613,13 +1799,13 @@
         grad_mix.astype(F32),
         grad_n2,
         grad_gu1,
-        grad_d1,
+        grad_d1.astype(F32),
         grad_n3,
         grad_qkv,
         grad_ao,
         grad_n4,
         grad_gu2,
-        grad_d2,
+        grad_d2.astype(F32),
     )
 
 

time: 1010 us -> 931 us (0.922)
  Pallas kernels: 711 us -> 594 us
  waiting for transfers between devices: 2.74 us -> 73.6 us
  local copies, waits for them, and re-layouts: 113 us -> 73.7 us
  matrix products: 116 us -> 130 us
    pallas_call x15 -> x16, Pallas kernels: 560 us -> 422 us  [the longest x7 253 us: turn(): pl.pallas_call(functools.partial(turn_body, back, gather, parts, jobs, (l...]
    reduce_scatter x6 -> x8, waiting for transfers between devices: 0.07 us -> 70.3 us  [scatter_tc(): return lax.psum_scatter(x, ('t', 'c'), scatter_dimension=0, tiled=True)]
    convert_element_type x12 -> x1, local copies, waits for them, and re-layouts: 31.4 us -> 0.09 us  [local(): jnp.stack([norm_mixer, norm_ffn_one, norm_attn, norm_ffn_two], axis=1)]
    pallas_call x1, Pallas kernels: 19.2 us -> 34.2 us  [keys_call(): pl.pallas_call(functools.partial(keys_body, T, hops), out_shape=(out((CH,...]
    unnamed x252 -> x208, local copies, waits for them, and re-layouts: 55.2 us -> 49.8 us
  transfers between devices with their start and end apart: 12 -> 16, of which waited for: 0 -> 3; matrix products, arithmetic and copies ran while one was open for 18% -> 18% of each run, Pallas kernels for 70% -> 58%
where the time goes in v4:
time: 931 us; the launch traced here: 921 us
  Pallas kernels  594 us (64%)
  matrix products  130 us (14%)
  local copies, waits for them, and re-layouts  73.7 us (8%)
  waiting for transfers between devices  73.6 us (8%)
  other arithmetic  31.9 us (3%)
  between operations  15.9 us (2%)
    pallas_call x7, Pallas kernels, turn(): pl.pallas_call(functools.partial(turn_body, back, gather, parts, jobs, (l...  253 us
    pallas_call x1, Pallas kernels, first_call(): pl.pallas_call(functools.partial(first_body, T, chunks), out_shape=(out((...  72.1 us
    reduce_scatter x8, waiting for transfers between devices, scatter_tc(): return lax.psum_scatter(x, ('t', 'c'), scatter_dimension=0, tiled=True)  70.3 us
    unnamed x208, local copies, waits for them, and re-layouts  49.8 us
    dot_general x10, matrix products, nt(): lax.dot_general(a, b, (((1,), (1,)), ((), ())), preferred_element_type=F32)  47.9 us
    pallas_call x1, Pallas kernels, keys_back_call(): pl.pallas_call(functools.partial(keys_back_body, T, hops, jobs, (len(args...  43.7 us
    dot_general x9, matrix products, nn(): return jnp.dot(a, b, preferred_element_type=F32)  43.7 us
    pallas_call x1, Pallas kernels, scan_four(): pl.pallas_call(scan_four_body, out_shape=(out((CH, width)), out((CH, widt...  39.3 us
  transfers between devices with their start and end apart: 16, of which 3 were waited for; matrix products, arithmetic and copies ran while one was open for 18% of the time, Pallas kernels for 58%

profile of v4, /device:TPU:1, one launch (start us, length us, event | category | flops | bytes accessed | tf_op | source)
XLA Modules:
  0.0 921.2 jit_solution(16677338023557591789)
XLA Ops:
  17.8 72.1 %first.1 = (bf16[528,1536]{1,0:T(8,128)(2,1)S(1)}, s32[16,8,128]{2,1,0:T(8,128)S(1)}, bf16[8,96,256]{2,1,0:T(8,128)(2,1)S(1)}, bf16[8,4,48,1536]{3,2,1,0:T(8,128...) custom-call(bf16[128,1536]{1,0:T(8,128)(2,1)S(1)} %bitcast.98, ...), custom_call_target="tpu_custom_call" | custom-call | tf_op jit(solution)/shard_map/first/pallas_call | solution.py:338
  100.5 7.2 fusion.63.xz
  114.5 12.4 %plane_sum3.1 = f32[512,128]{1,0:T(8,128)S(1)} custom-call(f32[512,128]{1,0:T(8,128)S(1)} %copy-done.46), custom_call_target="tpu_custom_call" | custom-call | tf_op jit(solution)/shard_map/plane_sum3/pallas_call | solution.py:517
  135.1 9.8 %scan_one.1 = f32[16,768]{1,0:T(8,128)} custom-call(f32[512,768]{1,0:T(8,128)} %get-tuple-element.306.delta, f32[512,768]{1,0:T(8,128)} %get-tuple-element.119.u, f32[16,768]{1,0:T(8,128)} %fusion.22.a2.refs_1_, f32[8192,128]{1,0:T(8,128)} %broadcast_in_dim.88.brep, f32[512]{0:T(512)} %broadcast_select_fusion.first), custom_call_target="tpu_custom_call" | custom-call | tf_op jit(solution)/shard_map/scan_one/pallas_call | solution.py:1257
  146.0 11.8 %chain4.1.h_in = f32[16,768]{1,0:T(8,128)S(1)} custom-call(f32[24,768]{1,0:T(8,128)S(1)} %fusion.16.refs_0_, f32[16,768]{1,0:T(8,128)S(1)} %copy-done.4), custom_call_target="tpu_custom_call" | custom-call | tf_op jit(solution)/shard_map/chain4/pallas_call | solution.py:886
  160.4 16.7 %scan_two.1 = (f32[512,768]{1,0:T(8,128)}, f32[128,768]{1,0:T(8,128)}) custom-call(f32[512,768]{1,0:T(8,128)} %get-tuple-element.306.delta, f32[512,768]{1,0:T(8,128)} %get-tuple-element.119.u, f32[16,768]{1,0:T(8,128)} %fusion.22.a2.refs_1_, f32[8192,128]{1,0:T(8,128)} %broadcast_in_dim.88.brep, f32[8192,128]{1,0:T(8,128)} %broadcast_in_dim.90.crep, ...), custom_call_target="tpu_custom_call" | custom-call | tf_op jit(solution)/shard_map/scan_two/pallas_call | solution.py:1296
  185.9 36.5 %turn5.1 = (f32[128,1536]{1,0:T(8,128)S(1)}, bf16[512,1536]{1,0:T(8,128)(2,1)S(1)}) custom-call(bf16[512,1536]{1,0:T(8,128)(2,1)S(1)} %convolution_convert_fusion.15.refs_0_, f32[128,1536]{1,0:T(8,128)S(1)} %bitcast_convert_fusion.5.refs_1_), custom_call_target="tpu_custom_call" | custom-call | tf_op jit(solution)/shard_map/turn5/pallas_call | solution.py:813
  223.5 6.0 fusion.64
  237.3 44.8 %turn6.1 = (f32[128,1536]{1,0:T(8,128)S(1)}, bf16[512,1536]{1,0:T(8,128)(2,1)S(1)}, bf16[8,48,1536]{2,1,0:T(8,128)(2,1)S(1)}) custom-call(bf16[512,1536]{1,0:T(8,128)(2,1)S(1)} %convolution_convert_fusion.14.refs_0_, f32[128,1536]{1,0:T(8,128)S(1)} %get-tuple-element.123.refs_1_, bf16[48,1536]{1,0:T(8,128)(2,1)S(1)} %collective-permute-done.refs_2_), custom_call_target="tpu_custom_call" | custom-call | tf_op jit(solution)/shard_map/turn6/pallas_call | solution.py:813
  289.1 34.2 %keys.1 = (bf16[512,384]{1,0:T(8,128)(2,1)S(1)}, bf16[1536,384]{1,0:T(8,128)(2,1)S(1)}, bf16[1536,384]{1,0:T(8,128)(2,1)S(1)}, bf16[512,1536]{1,0:T(8,128)(2,1)S(1)}) custom-call(f32[512,1152]{1,0:T(8,128)S(1)} %fusion.65.qkv, f32[512,128]{1,0:T(8,128)S(1)} %get-tuple-element.319.cosine.refs_3_, f32[512,128]{1,0:T(8,128)S(1)} %get-tuple-element.320.sine.refs_4_, ...), custom_call_target="tpu_custom_call" | custom-call | tf_op jit(solution)/shard_map/keys/pallas_call | solution.py:984
  327.3 9.2 %attend.1 = (bf16[512,384]{1,0:T(8,128)(2,1)}, f32[512,384]{1,0:T(8,128)}) custom-call(bf16[512,384]{1,0:T(8,128)(2,1)} %copy-done.20, bf16[1536,384]{1,0:T(8,128)(2,1)} %copy-done, bf16[1536,384]{1,0:T(8,128)(2,1)} %copy-done.1, bf16[512,1536]{1,0:T(8,128)(2,1)} %select_convert_fusion.bias), custom_call_target="tpu_custom_call" | custom-call | tf_op jit(solution)/shard_map/attend/pallas_call | solution.py:1449
  338.5 34.2 %turn8.1 = (f32[128,1536]{1,0:T(8,128)S(1)}, bf16[512,1536]{1,0:T(8,128)(2,1)S(1)}) custom-call(bf16[512,1536]{1,0:T(8,128)(2,1)S(1)} %convolution_convert_fusion.13.refs_0_, f32[128,1536]{1,0:T(8,128)S(1)} %get-tuple-element.134.refs_1_), custom_call_target="tpu_custom_call" | custom-call | tf_op jit(solution)/shard_map/turn8/pallas_call | solution.py:813
  373.9 8.6 fusion.66
  382.5 7.2 multiply_convert_fusion.4
  396.6 8.0 convolution_convert_fusion.12.refs_0_
  407.5 33.3 %turn10.1 = (f32[128,1536]{1,0:T(8,128)S(1)}, bf16[512,1536]{1,0:T(8,128)(2,1)S(1)}) custom-call(bf16[512,1536]{1,0:T(8,128)(2,1)S(1)} %copy-done.16, f32[128,1536]{1,0:T(8,128)S(1)} %get-tuple-element.138.refs_1_.refs_6_, f32[128,1536]{1,0:T(8,128)S(1)} %bitcast_convert_fusion.refs_2_), custom_call_target="tpu_custom_call" | custom-call | tf_op jit(solution)/shard_map/turn10/pallas_call | solution.py:813
  444.4 13.2 %attend_back.1 = (f32[512,384]{1,0:T(8,128)}, f32[1536,384]{1,0:T(8,128)}, f32[1536,384]{1,0:T(8,128)}) custom-call(bf16[512,384]{1,0:T(8,128)(2,1)} %copy-done.20, bf16[1536,384]{1,0:T(8,128)(2,1)} %copy-done, bf16[1536,384]{1,0:T(8,128)(2,1)} %copy-done.1, bf16[512,1536]{1,0:T(8,128)(2,1)} %select_convert_fusion.bias, f32[512,384]{1,0:T(8,128)} %get-tuple-element.130.lse, ...), custom_call_target="tpu_custom_call" | custom-call | tf_op jit(solution)/shard_map/attend_back/pallas_call | solution.py:1497
  466.5 43.8 %reduce-scatter.9.cloned.1.call-done = bf16[192,2048]{1,0:T(8,128)(2,1)} async-done(((bf16[1536,2048]{1,0:T(8,128)(2,1)}), bf16[192,2048]{1,0:T(8,128)(2,1)}) %reduce-scatter.9.cloned.1.call-update) | async-done | bytes 786448 | tf_op jit(solution)/shard_map/reduce_scatter | solution.py:1549
  514.8 43.7 %keys_back.1 = (bf16[512,1152]{1,0:T(8,128)(2,1)S(1)}, bf16[128,1536]{1,0:T(8,128)(2,1)S(1)}) custom-call(f32[512,384]{1,0:T(8,128)S(1)} %copy-done.25, f32[1536,384]{1,0:T(8,128)} %get-tuple-element.144.refs_1_, f32[1536,384]{1,0:T(8,128)} %get-tuple-element.145.refs_2_, f32[512,128]{1,0:T(8,128)S(1)} %copy-done.7, f32[512,128]{1,0:T(8,128)S(1)} %copy-done.9, ...), custom_call_target="tpu_custom_call" | custom-call | tf_op jit(solution)/shard_map/keys_back/pallas_call | solution.py:1114
  575.7 36.1 %turn12.1 = (f32[128,1536]{1,0:T(8,128)S(1)}, bf16[512,1536]{1,0:T(8,128)(2,1)S(1)}, f32[48,1536]{1,0:T(8,128)S(1)}) custom-call(bf16[512,1536]{1,0:T(8,128)(2,1)S(1)} %copy-done.15, f32[128,1536]{1,0:T(8,128)S(1)} %get-tuple-element.134.refs_1_, f32[128,1536]{1,0:T(8,128)S(1)} %copy-done.35, bf16[8,48,1536]{2,1,0:T(8,128)(2,1)S(1)} %bitcast.101), custom_call_target="tpu_custom_call" | custom-call | tf_op jit(solution)/shard_map/turn12/pallas_call | solution.py:813
  623.0 7.0 convolution_convert_fusion
  630.0 7.0 convolution_convert_fusion.10.refs_0_
  638.2 35.2 %turn13.1 = (f32[128,1536]{1,0:T(8,128)S(1)}, bf16[512,1536]{1,0:T(8,128)(2,1)S(1)}) custom-call(bf16[512,1536]{1,0:T(8,128)(2,1)S(1)} %convolution_convert_fusion.10.refs_0_, f32[128,1536]{1,0:T(8,128)S(1)} %get-tuple-element.123.refs_1_, f32[128,1536]{1,0:T(8,128)S(1)} %copy-done.30), custom_call_target="tpu_custom_call" | custom-call | tf_op jit(solution)/shard_map/turn13/pallas_call | solution.py:813
  680.1 6.2 multiply_multiply_fusion
  690.8 9.7 %scan_three.1 = f32[16,768]{1,0:T(8,128)} custom-call(f32[512,768]{1,0:T(8,128)} %get-tuple-element.306.delta, f32[512,768]{1,0:T(8,128)} %get-tuple-element.161.dy, f32[16,768]{1,0:T(8,128)} %fusion.22.a2.refs_1_, f32[8192,128]{1,0:T(8,128)} %broadcast_in_dim.90.crep, f32[512]{0:T(512)} %broadcast_select_fusion.first), custom_call_target="tpu_custom_call" | custom-call | tf_op jit(solution)/shard_map/scan_three/pallas_call | solution.py:1326
  701.4 20.3 %chain14.1 = (f32[16,768]{1,0:T(8,128)S(1)}, bf16[4,48,2048]{2,1,0:T(8,128)(2,1)S(1)}, bf16[4,48,1152]{2,1,0:T(8,128)(2,1)S(1)}) custom-call(f32[24,768]{1,0:T(8,128)S(1)} %fusion.18.refs_0_, f32[16,768]{1,0:T(8,128)S(1)} %copy-done.5, bf16[4,48,2048]{2,1,0:T(8,128)(2,1)S(1)} %bitcast.103, bf16[4,48,1152]{2,1,0:T(8,128)(2,1)S(1)} %bitcast.105), custom_call_target="tpu_custom_call" | custom-call | tf_op jit(solution)/shard_map/chain14/pallas_call | solution.py:886
  723.9 39.3 %scan_four.1 = (f32[512,768]{1,0:T(8,128)}, f32[512,768]{1,0:T(8,128)}, f32[8192,128]{1,0:T(8,128)}, f32[8192,128]{1,0:T(8,128)}, f32[16,768]{1,0:T(8,128)}) custom-call(f32[512,768]{1,0:T(8,128)} %get-tuple-element.306.delta, f32[512,768]{1,0:T(8,128)} %get-tuple-element.119.u, f32[512,768]{1,0:T(8,128)} %get-tuple-element.161.dy, ...), custom_call_target="tpu_custom_call" | custom-call | tf_op jit(solution)/shard_map/scan_four/pallas_call | solution.py:1407
  774.5 9.3 %plane_sum15.1 = f32[512,128]{1,0:T(8,128)S(1)} custom-call(f32[512,128]{1,0:T(8,128)S(1)} %pad_maximum_fusion.7.x), custom_call_target="tpu_custom_call" | custom-call | tf_op jit(solution)/shard_map/plane_sum15/pallas_call | solution.py:517
  785.4 7.8 conv_back.1
  823.2 24.8 %reduce-scatter.21.cloned.1.call-done = bf16[192,768]{1,0:T(8,128)(2,1)} async-done(((bf16[1536,768]{1,0:T(8,128)(2,1)}), bf16[192,768]{1,0:T(8,128)(2,1)}) %reduce-scatter.21.cloned.1.call-update) | async-done | bytes 294928 | tf_op jit(solution)/shard_map/reduce_scatter | solution.py:1549
  853.6 33.2 %turn17.1 = (f32[128,1536]{1,0:T(8,128)S(1)}, f32[96,256]{1,0:T(8,128)S(1)}, bf16[4,48,2048]{2,1,0:T(8,128)(2,1)S(1)}) custom-call(bf16[512,1536]{1,0:T(8,128)(2,1)S(1)} %convolution_convert_fusion.9.refs_0_, f32[128,1536]{1,0:T(8,128)S(1)} %bitcast_convert_fusion.5.refs_1_, f32[128,1536]{1,0:T(8,128)S(1)} %copy-done.33, bf16[8,96,256]{2,1,0:T(8,128)(2,1)S(1)} %bitcast.97, ...), custom_call_target="tpu_custom_call" | custom-call | tf_op jit(solution)/shard_map/turn17/pallas_call | solution.py:813
  897.4 9.5 %jobs20.1 = (bf16[4,48,768]{2,1,0:T(8,128)(2,1)S(1)}, bf16[4,48,768]{2,1,0:T(8,128)(2,1)S(1)}) custom-call(bf16[4,48,768]{2,1,0:T(8,128)(2,1)S(1)} %bitcast.108, bf16[4,48,768]{2,1,0:T(8,128)(2,1)S(1)} %bitcast.107), custom_call_target="tpu_custom_call" | custom-call | tf_op jit(solution)/shard_map/jobs20/pallas_call | solution.py:485
  (368 shorter events, 207.0 us)
Async XLA Ops:
  7.2 175.6 %all-gather.7.cloned.1.call-start = ((), (), s32[]{:S(2)}) async-start(), calls=%async_computation.8 | async-start | bytes 2654208 | tf_op jit(solution)/shard_map/all_gather | solution.py:1537
  7.9 215.6 %all-gather.9.cloned.1.call-start = ((), (), s32[]{:S(2)}) async-start(), calls=%async_computation.9 | async-start | bytes 7077888 | tf_op jit(solution)/shard_map/all_gather | solution.py:1537
  17.8 77.4 %copy-start.96 = (bf16[48,1536]{1,0:T(8,128)(2,1)S(1)}, bf16[48,1536]{1,0:T(8,128)(2,1)}, u32[]{:S(2)}) copy-start(bf16[48,1536]{1,0:T(8,128)(2,1)} %param.40) | copy-start | bytes 442372
  93.2 33.9 %copy-start.12 = (bf16[8,96,256]{2,1,0:T(8,128)(2,1)}, bf16[8,96,256]{2,1,0:T(8,128)(2,1)S(1)}, u32[]{:S(2)}) copy-start(bf16[8,96,256]{2,1,0:T(8,128)(2,1)S(1)} %get-tuple-element.117) | copy-start | bytes 1179652
  93.2 140.1 %all-gather.11.cloned.1.call-start = ((), (), s32[]{:S(2)}) async-start(), calls=%async_computation.10 | async-start | bytes 3538944 | tf_op jit(solution)/shard_map/all_gather | solution.py:1537
  93.9 190.4 %all-gather.13.cloned.1.call-start = ((), (), s32[]{:S(2)}) async-start(), calls=%async_computation.11 | async-start | bytes 3981312 | tf_op jit(solution)/shard_map/all_gather | solution.py:1537
  94.5 279.4 %all-gather.17.cloned.1.call-start = ((), (), s32[]{:S(2)}) async-start(), calls=%async_computation.13 | async-start | bytes 7077888 | tf_op jit(solution)/shard_map/all_gather | solution.py:1537
  95.1 287.4 %all-gather.15.cloned.1.call-start = ((), (), s32[]{:S(2)}) async-start(), calls=%async_computation.12 | async-start | bytes 3538944 | tf_op jit(solution)/shard_map/all_gather | solution.py:1537
  95.2 142.2 %collective-permute-start = (bf16[48,1536]{1,0:T(8,128)(2,1)S(1)}, bf16[48,1536]{1,0:T(8,128)(2,1)S(1)}, u32[]{:S(2)}, u32[]{:S(2)}) collective-permute-start(bf16[48,1536]{1,0:T(8,128)(2,1)S(1)} %copy-done.96), channel_id=1, source_target_pairs={{0,0},{1,1},{2,8},{3,9},{4,16},{5,17},{6,24},{7,25},{8,2},{9,3},{1... | collective-permute-start | bytes 442376 | tf_op jit(solution)/shard_map/ppermute | solution.py:1607
  95.9 414.5 %reduce-scatter.9.cloned.1.call-start = ((), (), s32[]{:S(2)}) async-start(), calls=%async_computation.14 | async-start | bytes 7077888 | tf_op jit(solution)/shard_map/reduce_scatter | solution.py:1549
  96.8 80.6 %copy-start.85 = (f32[768]{0:T(1024)}, f32[768]{0:T(1024)S(1)}, u32[]{:S(2)}) copy-start(f32[768]{0:T(1024)S(1)} %get-tuple-element.292) | copy-start | bytes 9220
  130.6 14.3 %copy-start.83 = (f32[1,768]{1,0:T(1,128)}, f32[1,768]{1,0:T(1,128)S(1)}, u32[]{:S(2)}) copy-start(f32[1,768]{1,0:T(1,128)S(1)} %broadcast_in_dim.93) | copy-start | bytes 9220
  130.7 14.3 %copy-start.88 = (f32[24]{0:T(128)}, f32[24]{0:T(128)S(1)}, u32[]{:S(2)}) copy-start(f32[24]{0:T(128)S(1)} %pad.34.clone) | copy-start | bytes 292
  131.4 13.5 %copy-start.90 = (f32[24]{0:T(128)}, f32[24]{0:T(128)S(1)}, u32[]{:S(2)}) copy-start(f32[24]{0:T(128)S(1)} %pad.33.clone) | copy-start | bytes 292
  135.1 11.0 %copy-start.4 = (f32[16,768]{1,0:T(8,128)S(1)}, f32[16,768]{1,0:T(8,128)}, u32[]{:S(2)}) copy-start(f32[16,768]{1,0:T(8,128)} %fusion.22.a2.refs_1_) | copy-start | bytes 147460
  160.4 17.0 %copy-start.64 = (f32[512,768]{1,0:T(8,128)S(1)}, f32[512,768]{1,0:T(8,128)}, u32[]{:S(2)}) copy-start(f32[512,768]{1,0:T(8,128)} %get-tuple-element.119.u) | copy-start | bytes 4718596
  177.4 111.7 %copy-start.6 = (f32[512,128]{1,0:T(8,128)}, f32[512,128]{1,0:T(8,128)S(1)}, u32[]{:S(2)}) copy-start(f32[512,128]{1,0:T(8,128)S(1)} %get-tuple-element.319.cosine.refs_3_) | copy-start | bytes 786436
  177.4 111.7 %copy-start.8 = (f32[512,128]{1,0:T(8,128)}, f32[512,128]{1,0:T(8,128)S(1)}, u32[]{:S(2)}) copy-start(f32[512,128]{1,0:T(8,128)S(1)} %get-tuple-element.320.sine.refs_4_) | copy-start | bytes 786436
  404.7 232.3 %reduce-scatter.11.cloned.1.call-start = ((), (), s32[]{:S(2)}) async-start(), calls=%async_computation.15 | async-start | bytes 3538944 | tf_op jit(solution)/shard_map/reduce_scatter | solution.py:1549
  404.9 35.9 %copy-start.23 = (bf16[8,48,1536]{2,1,0:T(8,128)(2,1)S(1)}, bf16[8,48,1536]{2,1,0:T(8,128)(2,1)}, u32[]{:S(2)}) copy-start(bf16[8,48,1536]{2,1,0:T(8,128)(2,1)} %copy-done.21) | copy-start | bytes 3538948
  444.4 13.2 %copy-start.58 = (bf16[512,1536]{1,0:T(8,128)(2,1)S(1)}, bf16[512,1536]{1,0:T(8,128)(2,1)}, u32[]{:S(2)}) copy-start(bf16[512,1536]{1,0:T(8,128)(2,1)} %copy-done.57) | copy-start | bytes 4718596
  444.4 13.3 %copy-start.97 = (bf16[512,1024]{1,0:T(8,128)(2,1)S(1)}, bf16[512,1024]{1,0:T(8,128)(2,1)}, u32[]{:S(2)}) copy-start(bf16[512,1024]{1,0:T(8,128)(2,1)} %get-tuple-element.304) | copy-start | bytes 3145732
  560.2 115.2 %reduce-scatter.13.cloned.1.call-start = ((), (), s32[]{:S(2)}) async-start(), calls=%async_computation.16 | async-start | bytes 3981312 | tf_op jit(solution)/shard_map/reduce_scatter | solution.py:1549
  571.8 152.1 %reduce-scatter.15.cloned.1.call-start = ((), (), s32[]{:S(2)}) async-start(), calls=%async_computation.17 | async-start | bytes 3538944 | tf_op jit(solution)/shard_map/reduce_scatter | solution.py:1549
  575.7 36.1 %copy-start.70 = (f32[512,2048]{1,0:T(8,128)S(1)}, f32[512,2048]{1,0:T(8,128)}, u32[]{:S(2)}) copy-start(f32[512,2048]{1,0:T(8,128)} %copy-done.69) | copy-start | bytes 12582916
  621.6 152.9 %reduce-scatter.17.cloned.1.call-start = ((), (), s32[]{:S(2)}) async-start(), calls=%async_computation.18 | async-start | bytes 7077888 | tf_op jit(solution)/shard_map/reduce_scatter | solution.py:1549
  637.0 169.2 %reduce-scatter.19.cloned.1.call-start = ((), (), s32[]{:S(2)}) async-start(), calls=%async_computation.19 | async-start | bytes 2654208 | tf_op jit(solution)/shard_map/reduce_scatter | solution.py:1549
  689.9 158.0 %reduce-scatter.21.cloned.1.call-start = ((), (), s32[]{:S(2)}) async-start(), calls=%async_computation.20 | async-start | bytes 2654208 | tf_op jit(solution)/shard_map/reduce_scatter | solution.py:1549
  690.8 205.7 %reduce-scatter.23.cloned.1.call-start = ((), (), s32[]{:S(2)}) async-start(), calls=%async_computation.21 | async-start | bytes 2654208 | tf_op jit(solution)/shard_map/reduce_scatter | solution.py:1549
  808.4 1.6 collective-permute-start.1
  853.6 37.0 %copy-start.81 = (bf16[96,1536]{1,0:T(8,128)(2,1)S(1)}, bf16[96,1536]{1,0:T(8,128)(2,1)}, u32[]{:S(2)}) copy-start(bf16[96,1536]{1,0:T(8,128)(2,1)} %reduce-scatter.19.cloned.1.call-done) | copy-start | bytes 884740
  890.5 22.3 %copy-start.39 = (bf16[128,1536]{1,0:T(8,128)(2,1)S(1)}, bf16[128,1536]{1,0:T(8,128)(2,1)}, u32[]{:S(2)}) copy-start(bf16[128,1536]{1,0:T(8,128)(2,1)} %copy-done.38) | copy-start | bytes 1179652
  (84 other events, 291.7 us)
Sparse Core Ops, SparseCore 0:
  9.7 46.1 all-gather.6
  93.3 69.1 all-gather.8
  164.2 42.7 all-gather.10
  208.5 40.4 all-gather.12
  250.5 74.8 all-gather.16
  326.9 40.9 all-gather.14
  404.8 105.4 reduce-scatter.8
  560.4 48.2 reduce-scatter.10
  611.0 42.6 reduce-scatter.12
  655.9 38.4 reduce-scatter.14
  696.8 73.2 reduce-scatter.16
  772.4 33.7 reduce-scatter.18
  808.6 39.3 reduce-scatter.20
  850.3 40.7 reduce-scatter.22

commit v5 on v4

--- a/solution.py
+++ b/solution.py
@@ -468,6 +468,47 @@
     )
 
 
+def finish_body(n, chunk, scaled, *refs):
+    blocks, (w, gain, total, o) = refs[:n], refs[n:]
+    acc = jnp.zeros((w.shape[0], 1), F32)
+    at = 0
+    for b in blocks:
+        for k in range(b.shape[2] // chunk):
+            pieces = [b[q, :, k * chunk : (k + 1) * chunk] for q in range(W)]
+            value = jnp.concatenate(pieces, axis=1).astype(F32)
+            cut = pl.ds(at, W * chunk)
+            acc = acc + jnp.sum(w[:, cut].astype(F32) * value, axis=1, keepdims=True)
+            o[:, cut] = value * gain[...] if scaled else value.astype(BF)
+            at += W * chunk
+    total[...] = jnp.broadcast_to(acc, total.shape)
+
+
+def finish_job(blocks, w, gain, chunk, scaled=False):
+    rows = w.shape[0]
+    n = len(blocks)
+
+    def build(ins, outs, scratch):
+        return 0, lambda: finish_body(n, chunk, scaled, *ins, *outs), lambda: None
+
+    return Job(
+        build, tuple(blocks) + (w, gain.astype(F32).reshape(rows, 1)), [vmem()] * (n + 2),
+        [out((rows, 128)), out(w.shape, F32 if scaled else BF)], [vmem(), vmem()], [],
+    )
+
+
+def finish(blocks, w, gain, chunk):
+    job = finish_job(blocks, w, gain, chunk, True)
+    total, grad = pl.pallas_call(
+        functools.partial(finish_body, len(blocks), chunk, True),
+        out_shape=job.shapes,
+        in_specs=job.in_specs,
+        out_specs=job.specs,
+        compiler_params=alone(),
+        name="finish",
+    )(*job.inputs)
+    return total[:, 0], grad
+
+
 def jobs_body(counts, jobs, *refs):
     refs = list(refs)
     ins, outs = take(refs, counts[0]), take(refs, counts[1])
@@ -642,42 +683,6 @@
     )
 
 
-def small_job(T, x):
-    peers = [(dt, dc) for dt in range(T) for dc in range(2) if dt or dc]
-    n = len(peers)
-
-    def build(ins, outs, scratch):
-        (src,), (dst,) = ins, outs
-        recv, ss, rs = scratch
-        t, p, c = here()
-
-        def copy(i):
-            dt, dc = peers[i]
-            tt, cc = lax.rem(t + dt, T), flip(c, dc)
-            return remote(src.at[tt * 2 + cc], recv.at[i], ss.at[i], rs.at[i], (tt, p, cc))
-
-        for dt, dc in peers:
-            greet((lax.rem(t + dt, T), p, flip(c, dc)))
-
-        def begin():
-            for i in range(n):
-                copy(i).start()
-
-        def end():
-            total = src[t * 2 + c].astype(F32)
-            for i in range(n):
-                copy(i).wait()
-                total = total + recv[i].astype(F32)
-            dst[...] = total
-
-        return n, begin, end
-
-    return Job(
-        build, [x], [vmem()], [out(x.shape[1:])], [vmem()],
-        [pltpu.VMEM((n,) + x.shape[1:], x.dtype), dma(n), dma(n)],
-    )
-
-
 def sum_job(part, x, dtype):
     B, D = x.shape
 
@@ -726,7 +731,7 @@
     refs = list(refs)
     ins, outs = take(refs, counts[0]), take(refs, counts[1])
     part, x = take(ins, 2)
-    g = take(ins, 1)[0] if back else None
+    g = take(ins, 1)[0] if back and gather else None
     o = take(outs, 1)[0]
     gath = take(outs, 1)[0] if gather else None
     own, recv, sbuf, ss, rs, ls, ss2, rs2, ls2 = take(refs, 9)
@@ -766,7 +771,8 @@
         if back:
             r = lax.rsqrt(jnp.mean(value * value, axis=-1, keepdims=True) + EPS)
             hat = value * r
-            new = g[cut, :] + r * (total - hat * jnp.mean(total * hat, axis=-1, keepdims=True))
+            new = r * (total - hat * jnp.mean(total * hat, axis=-1, keepdims=True))
+            new = g[cut, :] + new if g is not None else new
         else:
             new = value + total
         o[cut, :] = new.astype(o.dtype)
@@ -791,7 +797,7 @@
 def turn(cid, part, x, g=None, gather=True, dtype=F32, parts=2, jobs=()):
     B, D = x.shape
     back = g is not None
-    args = (part, x) + ((g,) if back else ())
+    args = (part, x) + ((g,) if back and gather else ())
     in_specs = [hbm()] + [vmem()] * (len(args) - 1)
     shapes, specs = (out((B, D), dtype),), (vmem(),)
     if gather:
@@ -1505,34 +1511,6 @@
     )(q, k, v, bias, lse, do)
 
 
-def finish_body(n, chunk, *refs):
-    blocks, (w, gain, o, total) = refs[:n], refs[n:]
-    acc = jnp.zeros((w.shape[0], 1), F32)
-    at = 0
-    for b in blocks:
-        for k in range(b.shape[2] // chunk):
-            pieces = [b[q, :, k * chunk : (k + 1) * chunk] for q in range(W)]
-            value = jnp.concatenate(pieces, axis=1).astype(F32)
-            cut = pl.ds(at, W * chunk)
-            acc = acc + jnp.sum(w[:, cut].astype(F32) * value, axis=1, keepdims=True)
-            o[:, cut] = value * gain[...]
-            at += W * chunk
-    total[...] = jnp.broadcast_to(acc, total.shape)
-
-
-def finish(blocks, w, gain, chunk):
-    rows = w.shape[0]
-    grad, total = pl.pallas_call(
-        functools.partial(finish_body, len(blocks), chunk),
-        out_shape=(out(w.shape), out((rows, 128))),
-        in_specs=[vmem()] * (len(blocks) + 2),
-        out_specs=(vmem(), vmem()),
-        compiler_params=alone(),
-        name="finish",
-    )(*blocks, w, gain.astype(F32).reshape(rows, 1))
-    return total[:, 0], grad
-
-
 def gather_tc(x):
     return lax.all_gather(x.reshape(-1, x.shape[-1]), ("t", "c"), axis=0, tiled=True)
 
@@ -1709,7 +1687,7 @@
     dq, dk, dv = attend_back(q, k_all, v_all, bias, lse, do)
     dq, last_part, raw_gu2 = together(dq, last_part, raw_gu2)
     dqkv, final = keys_back_call(
-        11, T, hops, dq, dk, dv, cosine, sine, jobs=(sum_job(last_part, x3, BF),)
+        11, T, hops, dq, dk, dv, cosine, sine, jobs=(sum_job(last_part, x3, F32),)
     )
     dqkv, dw_d2 = together(dqkv, dw_d2)
     grad_d2 = scatter_tc(dw_d2)
@@ -1729,7 +1707,6 @@
     dz_low = (dgate * y * gate_s * (1.0 + zg * (1.0 - gate_s))).astype(BF)
     dy, dw_mix, dw_z = together(dy, tn(gated, gl1).astype(BF), tn(nh1, dz_low).astype(BF))
     grad_mix = scatter_tc(dw_mix)
-    raw_z = scatter_tc(dw_z)
     begin = scan_three(delta, dy, a2, crep, first)
     g_in, gu2_b, qkv_b = chain(
         14, T, True, packed(begin), a2, jobs=(spread_job(True, (blocks(raw_gu2), blocks(raw_qkv))),)
@@ -1748,7 +1725,8 @@
         ],
         axis=1,
     )
-    part_back, raw_gu1 = together(part_back, raw_gu1)
+    part_back, raw_gu1, dw_z = together(part_back, raw_gu1, dw_z)
+    raw_z = scatter_tc(dw_z)
     dpr_low = plane_sum(15, part_back).astype(BF)
     du = du_scan + nt(dpr_low, w_state)
     dxs_ext, conv_grads = conv_back_call(xz, conv_mask, taps, du)
@@ -1757,7 +1735,7 @@
         [dxs_ext[HALO : HALO + CH - 8], dxs_ext[HALO + CH - 8 :] + rim], axis=0
     ).astype(BF)
     dxz = jnp.concatenate([dxs_low, dz_low], axis=1)
-    dxz, dw_x, grad_mix = together(dxz, tn(nh1, dxs_low).astype(BF), grad_mix)
+    dxz, dw_x, grad_mix, raw_ao = together(dxz, tn(nh1, dxs_low).astype(BF), grad_mix, raw_ao)
     raw_x = scatter_tc(dw_x)
     small = jnp.concatenate(
         [
@@ -1771,24 +1749,27 @@
         axis=1,
     )
     small = jnp.pad(small, ((0, 0), (0, 256 - used))).astype(BF).reshape(2 * T, CB, 256)
-    small, raw_z = together(small, raw_z)
-    grad_x, small, gu1_b = turn(
+    grad_x, small, gu1_b, grad_n4, grad_gu2, grad_n3, grad_qkv = turn(
         17, nt(dxz, w_in).astype(BF), x0, g1, gather=False,
-        jobs=(small_job(T, small), spread_job(True, (blocks(raw_gu1),))),
-    )
-    x_b, z_b = run_jobs(20, spread_job(True, (blocks(raw_x), blocks(raw_z))))
-    grad_ao = lax.ppermute(raw_ao.astype(BF), ("t", "p", "c"), [(b, a) for a, b in pairs]).astype(F32)
-
-    grad_n1, grad_in = finish((x_b, z_b), in_proj, norm_mixer, chunks[0])
-    grad_n2, grad_gu1 = finish((gu1_b,), gate_up_one, norm_ffn_one, chunks[1])
-    grad_n3, grad_qkv = finish((qkv_b,), qkv_proj, norm_attn, chunks[2])
-    grad_n4, grad_gu2 = finish((gu2_b,), gate_up_two, norm_ffn_two, chunks[3])
+        jobs=(scatter_job(T, small.reshape(width, 256)), spread_job(True, (blocks(raw_gu1),)),
+            finish_job((gu2_b,), gate_up_two, norm_ffn_two, chunks[3]),
+            finish_job((qkv_b,), qkv_proj, norm_attn, chunks[2]),
+        ),
+    )
+    raw_z, grad_x = together(raw_z, grad_x)
+    grad_x = g1 + grad_x
+    final = final.astype(BF)
+
+    def scaled(value, gain):
+        return value.astype(F32) * gain.astype(F32)[:, None]
+
+    grad_gu2, grad_qkv = scaled(grad_gu2, norm_ffn_two), scaled(grad_qkv, norm_attn)
+    z_b, grad_n2, grad_gu1 = run_jobs(
+        22, spread_job(True, (blocks(raw_z),)),
+        finish_job((gu1_b,), gate_up_one, norm_ffn_one, chunks[1]),
+    )
     at = NR + R + N
-    return (
-        final[None],
-        grad_x[None],
-        grad_n1,
-        grad_in,
+    small_grads = (
         small[:, at : at + 4].T,
         small[:, at + 4],
         small[:, :NR],
@@ -1796,6 +1777,20 @@
         small[:, at + 5],
         small[:, NR + R : at],
         small[:, at + 6],
+    )
+    grad_gu1 = scaled(grad_gu1, norm_ffn_one)
+    grad_n2, grad_n3, grad_n4 = grad_n2[:, 0], grad_n3[:, 0], grad_n4[:, 0]
+    raw_x, z_b, small_grads = together(raw_x, z_b, small_grads)
+    (x_b,) = run_jobs(20, spread_job(True, (blocks(raw_x),)))
+    grad_ao = lax.ppermute(raw_ao.astype(BF), ("t", "p", "c"), [(b, a) for a, b in pairs]).astype(F32)
+
+    grad_n1, grad_in = finish((x_b, z_b), in_proj, norm_mixer, chunks[0])
+    return (
+        final[None],
+        grad_x[None],
+        grad_n1,
+        grad_in,
+        *small_grads,
         grad_mix.astype(F32),
         grad_n2,
         grad_gu1,

time: 931 us -> 934 us (level)
    pallas_call x1 -> x2, Pallas kernels: 9.45 us -> 19 us  [run_jobs(): pl.pallas_call(functools.partial(jobs_body, (len(inputs), len(shapes)), j...]
    unnamed x208 -> x210, local copies, waits for them, and re-layouts: 49.8 us -> 50.6 us
  transfers between devices with their start and end apart: 16 -> 16, of which waited for: 3 -> 2; matrix products, arithmetic and copies ran while one was open for 18% -> 18% of each run, Pallas kernels for 58% -> 58%
where the time goes in v5:
time: 934 us; the launch traced here: 924 us
  Pallas kernels  594 us (64%)
  matrix products  131 us (14%)
  local copies, waits for them, and re-layouts  73.7 us (8%)
  waiting for transfers between devices  68.4 us (7%)
  other arithmetic  37.9 us (4%)
  between operations  16.2 us (2%)
    pallas_call x7, Pallas kernels, turn(): pl.pallas_call(functools.partial(turn_body, back, gather, parts, jobs, (l...  253 us
    pallas_call x1, Pallas kernels, first_call(): pl.pallas_call(functools.partial(first_body, T, chunks), out_shape=(out((...  72.1 us
    reduce_scatter x8, waiting for transfers between devices, scatter_tc(): return lax.psum_scatter(x, ('t', 'c'), scatter_dimension=0, tiled=True)  65.8 us
    unnamed x210, local copies, waits for them, and re-layouts  50.6 us
    dot_general x10, matrix products, nt(): lax.dot_general(a, b, (((1,), (1,)), ((), ())), preferred_element_type=F32)  47.7 us
    pallas_call x1, Pallas kernels, keys_back_call(): pl.pallas_call(functools.partial(keys_back_body, T, hops, jobs, (len(args...  43.7 us
    dot_general x9, matrix products, nn(): return jnp.dot(a, b, preferred_element_type=F32)  43.7 us
    dot_general x11, matrix products, tn(): lax.dot_general(a, b, (((0,), (0,)), ((), ())), preferred_element_type=F32)  39.4 us
  transfers between devices with their start and end apart: 16, of which 2 were waited for; matrix products, arithmetic and copies ran while one was open for 18% of the time, Pallas kernels for 58%

profile of v5, /device:TPU:1, one launch (start us, length us, event | category | flops | bytes accessed | tf_op | source)
XLA Modules:
  0.0 924.0 jit_solution(1279496373641896259)
XLA Ops:
  17.8 72.1 %first.1 = (bf16[528,1536]{1,0:T(8,128)(2,1)S(1)}, s32[16,8,128]{2,1,0:T(8,128)S(1)}, bf16[8,96,256]{2,1,0:T(8,128)(2,1)S(1)}, bf16[8,4,48,1536]{3,2,1,0:T(8,128...) custom-call(bf16[128,1536]{1,0:T(8,128)(2,1)S(1)} %bitcast.103, ...), custom_call_target="tpu_custom_call" | custom-call | tf_op jit(solution)/shard_map/first/pallas_call | solution.py:338
  100.6 7.2 fusion.66.xz
  114.5 12.4 %plane_sum3.1 = f32[512,128]{1,0:T(8,128)S(1)} custom-call(f32[512,128]{1,0:T(8,128)S(1)} %copy-done.52), custom_call_target="tpu_custom_call" | custom-call | tf_op jit(solution)/shard_map/plane_sum3/pallas_call | solution.py:558
  135.1 9.8 %scan_one.1 = f32[16,768]{1,0:T(8,128)} custom-call(f32[512,768]{1,0:T(8,128)} %get-tuple-element.326.delta, f32[512,768]{1,0:T(8,128)} %get-tuple-element.129.u, f32[16,768]{1,0:T(8,128)} %fusion.22.a2.refs_1_, f32[8192,128]{1,0:T(8,128)} %broadcast_in_dim.91.brep, f32[512]{0:T(512)} %broadcast_select_fusion.first), custom_call_target="tpu_custom_call" | custom-call | tf_op jit(solution)/shard_map/scan_one/pallas_call | solution.py:1263
  146.1 11.8 %chain4.1.h_in = f32[16,768]{1,0:T(8,128)S(1)} custom-call(f32[24,768]{1,0:T(8,128)S(1)} %fusion.16.refs_0_, f32[16,768]{1,0:T(8,128)S(1)} %copy-done.6), custom_call_target="tpu_custom_call" | custom-call | tf_op jit(solution)/shard_map/chain4/pallas_call | solution.py:892
  161.0 16.7 %scan_two.1 = (f32[512,768]{1,0:T(8,128)}, f32[128,768]{1,0:T(8,128)}) custom-call(f32[512,768]{1,0:T(8,128)} %get-tuple-element.326.delta, f32[512,768]{1,0:T(8,128)} %get-tuple-element.129.u, f32[16,768]{1,0:T(8,128)} %fusion.22.a2.refs_1_, f32[8192,128]{1,0:T(8,128)} %broadcast_in_dim.91.brep, f32[8192,128]{1,0:T(8,128)} %broadcast_in_dim.93.crep, ...), custom_call_target="tpu_custom_call" | custom-call | tf_op jit(solution)/shard_map/scan_two/pallas_call | solution.py:1302
  186.4 36.5 %turn5.1 = (f32[128,1536]{1,0:T(8,128)S(1)}, bf16[512,1536]{1,0:T(8,128)(2,1)S(1)}) custom-call(bf16[512,1536]{1,0:T(8,128)(2,1)S(1)} %convolution_convert_fusion.15.refs_0_, f32[128,1536]{1,0:T(8,128)S(1)} %bitcast_convert_fusion.2.refs_1_), custom_call_target="tpu_custom_call" | custom-call | tf_op jit(solution)/shard_map/turn5/pallas_call | solution.py:819
  237.8 44.6 %turn6.1 = (f32[128,1536]{1,0:T(8,128)S(1)}, bf16[512,1536]{1,0:T(8,128)(2,1)S(1)}, bf16[8,48,1536]{2,1,0:T(8,128)(2,1)S(1)}) custom-call(bf16[512,1536]{1,0:T(8,128)(2,1)S(1)} %convolution_convert_fusion.14.refs_0_, f32[128,1536]{1,0:T(8,128)S(1)} %get-tuple-element.133.refs_1_, bf16[48,1536]{1,0:T(8,128)(2,1)S(1)} %collective-permute-done.refs_2_), custom_call_target="tpu_custom_call" | custom-call | tf_op jit(solution)/shard_map/turn6/pallas_call | solution.py:819
  289.4 34.3 %keys.1 = (bf16[512,384]{1,0:T(8,128)(2,1)S(1)}, bf16[1536,384]{1,0:T(8,128)(2,1)S(1)}, bf16[1536,384]{1,0:T(8,128)(2,1)S(1)}, bf16[512,1536]{1,0:T(8,128)(2,1)S(1)}) custom-call(f32[512,1152]{1,0:T(8,128)S(1)} %fusion.68.qkv, f32[512,128]{1,0:T(8,128)S(1)} %get-tuple-element.345.cosine.refs_3_, f32[512,128]{1,0:T(8,128)S(1)} %get-tuple-element.346.sine.refs_4_, ...), custom_call_target="tpu_custom_call" | custom-call | tf_op jit(solution)/shard_map/keys/pallas_call | solution.py:990
  327.6 9.2 attend.1
  338.9 34.3 %turn8.1 = (f32[128,1536]{1,0:T(8,128)S(1)}, bf16[512,1536]{1,0:T(8,128)(2,1)S(1)}) custom-call(bf16[512,1536]{1,0:T(8,128)(2,1)S(1)} %convolution_convert_fusion.13.refs_0_, f32[128,1536]{1,0:T(8,128)S(1)} %get-tuple-element.144.refs_1_), custom_call_target="tpu_custom_call" | custom-call | tf_op jit(solution)/shard_map/turn8/pallas_call | solution.py:819
  374.4 8.7 fusion.69
  383.1 7.2 multiply_convert_fusion.4
  397.2 8.1 convolution_convert_fusion.12.refs_0_
  408.3 33.4 %turn10.1 = (f32[128,1536]{1,0:T(8,128)S(1)}, bf16[512,1536]{1,0:T(8,128)(2,1)S(1)}) custom-call(bf16[512,1536]{1,0:T(8,128)(2,1)S(1)} %copy-done.19, f32[128,1536]{1,0:T(8,128)S(1)} %get-tuple-element.148.refs_1_.refs_6_, f32[128,1536]{1,0:T(8,128)S(1)} %bitcast_convert_fusion.refs_2_), custom_call_target="tpu_custom_call" | custom-call | tf_op jit(solution)/shard_map/turn10/pallas_call | solution.py:819
  445.4 13.4 %attend_back.1 = (f32[512,384]{1,0:T(8,128)}, f32[1536,384]{1,0:T(8,128)}, f32[1536,384]{1,0:T(8,128)}) custom-call(bf16[512,384]{1,0:T(8,128)(2,1)} %copy-done.23, bf16[1536,384]{1,0:T(8,128)(2,1)} %copy-done, bf16[1536,384]{1,0:T(8,128)(2,1)} %copy-done.1, bf16[512,1536]{1,0:T(8,128)(2,1)} %select_convert_fusion.bias, f32[512,384]{1,0:T(8,128)} %get-tuple-element.140.lse, ...), custom_call_target="tpu_custom_call" | custom-call | tf_op jit(solution)/shard_map/attend_back/pallas_call | solution.py:1503
  467.5 45.5 %reduce-scatter.9.cloned.1.call-done = bf16[192,2048]{1,0:T(8,128)(2,1)} async-done(((bf16[1536,2048]{1,0:T(8,128)(2,1)}), bf16[192,2048]{1,0:T(8,128)(2,1)}) %reduce-scatter.9.cloned.1.call-update) | async-done | bytes 786448 | tf_op jit(solution)/shard_map/reduce_scatter | solution.py:1527
  517.4 43.7 %keys_back.1 = (bf16[512,1152]{1,0:T(8,128)(2,1)S(1)}, f32[128,1536]{1,0:T(8,128)S(1)}) custom-call(f32[512,384]{1,0:T(8,128)S(1)} %copy-done.29, f32[1536,384]{1,0:T(8,128)} %get-tuple-element.154.refs_1_, f32[1536,384]{1,0:T(8,128)} %get-tuple-element.155.refs_2_, f32[512,128]{1,0:T(8,128)S(1)} %copy-done.9, f32[512,128]{1,0:T(8,128)S(1)} %copy-done.11, ...), custom_call_target="tpu_custom_call" | custom-call | tf_op jit(solution)/shard_map/keys_back/pallas_call | solution.py:1120
  578.4 36.1 %turn12.1 = (f32[128,1536]{1,0:T(8,128)S(1)}, bf16[512,1536]{1,0:T(8,128)(2,1)S(1)}, f32[48,1536]{1,0:T(8,128)S(1)}) custom-call(bf16[512,1536]{1,0:T(8,128)(2,1)S(1)} %copy-done.18, f32[128,1536]{1,0:T(8,128)S(1)} %get-tuple-element.144.refs_1_, f32[128,1536]{1,0:T(8,128)S(1)} %copy-done.43, bf16[8,48,1536]{2,1,0:T(8,128)(2,1)S(1)} %bitcast.106), custom_call_target="tpu_custom_call" | custom-call | tf_op jit(solution)/shard_map/turn12/pallas_call | solution.py:819
  625.7 7.1 convolution_convert_fusion
  632.8 7.0 convolution_convert_fusion.10.refs_0_
  641.2 35.2 %turn13.1 = (f32[128,1536]{1,0:T(8,128)S(1)}, bf16[512,1536]{1,0:T(8,128)(2,1)S(1)}) custom-call(bf16[512,1536]{1,0:T(8,128)(2,1)S(1)} %convolution_convert_fusion.10.refs_0_, f32[128,1536]{1,0:T(8,128)S(1)} %get-tuple-element.133.refs_1_, f32[128,1536]{1,0:T(8,128)S(1)} %copy-done.36), custom_call_target="tpu_custom_call" | custom-call | tf_op jit(solution)/shard_map/turn13/pallas_call | solution.py:819
  683.1 6.2 multiply_convert_fusion.6
  693.0 9.7 %scan_three.1 = f32[16,768]{1,0:T(8,128)} custom-call(f32[512,768]{1,0:T(8,128)} %get-tuple-element.326.delta, f32[512,768]{1,0:T(8,128)} %get-tuple-element.172.dy, f32[16,768]{1,0:T(8,128)} %fusion.22.a2.refs_1_, f32[8192,128]{1,0:T(8,128)} %broadcast_in_dim.93.crep, f32[512]{0:T(512)} %broadcast_select_fusion.first), custom_call_target="tpu_custom_call" | custom-call | tf_op jit(solution)/shard_map/scan_three/pallas_call | solution.py:1332
  703.6 20.3 %chain14.1 = (f32[16,768]{1,0:T(8,128)S(1)}, bf16[4,48,2048]{2,1,0:T(8,128)(2,1)S(1)}, bf16[4,48,1152]{2,1,0:T(8,128)(2,1)S(1)}) custom-call(f32[24,768]{1,0:T(8,128)S(1)} %fusion.18.refs_0_, f32[16,768]{1,0:T(8,128)S(1)} %copy-done.7, bf16[4,48,2048]{2,1,0:T(8,128)(2,1)S(1)} %bitcast.107, bf16[4,48,1152]{2,1,0:T(8,128)(2,1)S(1)} %bitcast.109), custom_call_target="tpu_custom_call" | custom-call | tf_op jit(solution)/shard_map/chain14/pallas_call | solution.py:892
  726.2 39.3 %scan_four.1 = (f32[512,768]{1,0:T(8,128)}, f32[512,768]{1,0:T(8,128)}, f32[8192,128]{1,0:T(8,128)}, f32[8192,128]{1,0:T(8,128)}, f32[16,768]{1,0:T(8,128)}) custom-call(f32[512,768]{1,0:T(8,128)} %get-tuple-element.326.delta, f32[512,768]{1,0:T(8,128)} %get-tuple-element.129.u, f32[512,768]{1,0:T(8,128)} %get-tuple-element.172.dy, ...), custom_call_target="tpu_custom_call" | custom-call | tf_op jit(solution)/shard_map/scan_four/pallas_call | solution.py:1413
  784.1 9.4 %plane_sum15.1 = f32[512,128]{1,0:T(8,128)S(1)} custom-call(f32[512,128]{1,0:T(8,128)S(1)} %pad_maximum_fusion.7.x), custom_call_target="tpu_custom_call" | custom-call | tf_op jit(solution)/shard_map/plane_sum15/pallas_call | solution.py:558
  795.0 7.8 conv_back.1
  824.0 33.0 %turn17.1 = (f32[128,1536]{1,0:T(8,128)S(1)}, f32[96,256]{1,0:T(8,128)S(1)}, bf16[4,48,2048]{2,1,0:T(8,128)(2,1)S(1)}, f32[48,128]{1,0:T(8,128)S(1)}, bf16[48,81...) custom-call(bf16[512,1536]{1,0:T(8,128)(2,1)S(1)} %convolution_convert_fusion.9.refs_0_, ...), custom_call_target="tpu_custom_call" | custom-call | tf_op jit(solution)/shard_map/turn17/pallas_call | solution.py:819
  865.9 9.2 jobs22.1
  875.8 20.3 %reduce-scatter.23.cloned.1.call-done = bf16[192,768]{1,0:T(8,128)(2,1)} async-done(((bf16[1536,768]{1,0:T(8,128)(2,1)}), bf16[192,768]{1,0:T(8,128)(2,1)}) %reduce-scatter.23.cloned.1.call-update) | async-done | bytes 294928 | tf_op jit(solution)/shard_map/reduce_scatter | solution.py:1527
  897.1 9.8 %jobs20.1.refs_0_ = bf16[4,48,768]{2,1,0:T(8,128)(2,1)S(1)} custom-call(bf16[4,48,768]{2,1,0:T(8,128)(2,1)S(1)} %bitcast.110), custom_call_target="tpu_custom_call" | custom-call | tf_op jit(solution)/shard_map/jobs20/pallas_call | solution.py:526
  (373 shorter events, 208.9 us)
Async XLA Ops:
  7.2 176.2 %all-gather.7.cloned.1.call-start = ((), (), s32[]{:S(2)}) async-start(), calls=%async_computation.8 | async-start | bytes 2654208 | tf_op jit(solution)/shard_map/all_gather | solution.py:1515
  7.9 216.2 %all-gather.9.cloned.1.call-start = ((), (), s32[]{:S(2)}) async-start(), calls=%async_computation.9 | async-start | bytes 7077888 | tf_op jit(solution)/shard_map/all_gather | solution.py:1515
  17.8 77.4 %copy-start.98 = (bf16[48,1536]{1,0:T(8,128)(2,1)S(1)}, bf16[48,1536]{1,0:T(8,128)(2,1)}, u32[]{:S(2)}) copy-start(bf16[48,1536]{1,0:T(8,128)(2,1)} %param.40) | copy-start | bytes 442372
  93.2 33.9 %copy-start.15 = (bf16[8,96,256]{2,1,0:T(8,128)(2,1)}, bf16[8,96,256]{2,1,0:T(8,128)(2,1)S(1)}, u32[]{:S(2)}) copy-start(bf16[8,96,256]{2,1,0:T(8,128)(2,1)S(1)} %get-tuple-element.127) | copy-start | bytes 1179652
  93.2 140.6 %all-gather.11.cloned.1.call-start = ((), (), s32[]{:S(2)}) async-start(), calls=%async_computation.10 | async-start | bytes 3538944 | tf_op jit(solution)/shard_map/all_gather | solution.py:1515
  94.0 190.6 %all-gather.13.cloned.1.call-start = ((), (), s32[]{:S(2)}) async-start(), calls=%async_computation.11 | async-start | bytes 3981312 | tf_op jit(solution)/shard_map/all_gather | solution.py:1515
  94.5 279.9 %all-gather.17.cloned.1.call-start = ((), (), s32[]{:S(2)}) async-start(), calls=%async_computation.13 | async-start | bytes 7077888 | tf_op jit(solution)/shard_map/all_gather | solution.py:1515
  95.1 288.0 %all-gather.15.cloned.1.call-start = ((), (), s32[]{:S(2)}) async-start(), calls=%async_computation.12 | async-start | bytes 3538944 | tf_op jit(solution)/shard_map/all_gather | solution.py:1515
  95.2 142.6 %collective-permute-start = (bf16[48,1536]{1,0:T(8,128)(2,1)S(1)}, bf16[48,1536]{1,0:T(8,128)(2,1)S(1)}, u32[]{:S(2)}, u32[]{:S(2)}) collective-permute-start(bf16[48,1536]{1,0:T(8,128)(2,1)S(1)} %copy-done.98), channel_id=1, source_target_pairs={{0,0},{1,1},{2,8},{3,9},{4,16},{5,17},{6,24},{7,25},{8,2},{9,3},{1... | collective-permute-start | bytes 442376 | tf_op jit(solution)/shard_map/ppermute | solution.py:1585
  95.9 417.1 %reduce-scatter.9.cloned.1.call-start = ((), (), s32[]{:S(2)}) async-start(), calls=%async_computation.14 | async-start | bytes 7077888 | tf_op jit(solution)/shard_map/reduce_scatter | solution.py:1527
  96.8 81.2 %copy-start.87 = (f32[768]{0:T(1024)}, f32[768]{0:T(1024)S(1)}, u32[]{:S(2)}) copy-start(f32[768]{0:T(1024)S(1)} %get-tuple-element.312) | copy-start | bytes 9220
  130.6 14.4 %copy-start.85 = (f32[1,768]{1,0:T(1,128)}, f32[1,768]{1,0:T(1,128)S(1)}, u32[]{:S(2)}) copy-start(f32[1,768]{1,0:T(1,128)S(1)} %broadcast_in_dim.96) | copy-start | bytes 9220
  130.7 14.3 %copy-start.90 = (f32[24]{0:T(128)}, f32[24]{0:T(128)S(1)}, u32[]{:S(2)}) copy-start(f32[24]{0:T(128)S(1)} %pad.34.clone) | copy-start | bytes 292
  131.4 13.5 %copy-start.92 = (f32[24]{0:T(128)}, f32[24]{0:T(128)S(1)}, u32[]{:S(2)}) copy-start(f32[24]{0:T(128)S(1)} %pad.33.clone) | copy-start | bytes 292
  135.1 10.9 %copy-start.6 = (f32[16,768]{1,0:T(8,128)S(1)}, f32[16,768]{1,0:T(8,128)}, u32[]{:S(2)}) copy-start(f32[16,768]{1,0:T(8,128)} %fusion.22.a2.refs_1_) | copy-start | bytes 147460
  161.0 16.9 %copy-start.70 = (f32[512,768]{1,0:T(8,128)S(1)}, f32[512,768]{1,0:T(8,128)}, u32[]{:S(2)}) copy-start(f32[512,768]{1,0:T(8,128)} %get-tuple-element.129.u) | copy-start | bytes 4718596
  177.9 111.4 %copy-start.8 = (f32[512,128]{1,0:T(8,128)}, f32[512,128]{1,0:T(8,128)S(1)}, u32[]{:S(2)}) copy-start(f32[512,128]{1,0:T(8,128)S(1)} %get-tuple-element.345.cosine.refs_3_) | copy-start | bytes 786436
  177.9 111.4 %copy-start.10 = (f32[512,128]{1,0:T(8,128)}, f32[512,128]{1,0:T(8,128)S(1)}, u32[]{:S(2)}) copy-start(f32[512,128]{1,0:T(8,128)S(1)} %get-tuple-element.346.sine.refs_4_) | copy-start | bytes 786436
  405.3 234.5 %reduce-scatter.11.cloned.1.call-start = ((), (), s32[]{:S(2)}) async-start(), calls=%async_computation.15 | async-start | bytes 3538944 | tf_op jit(solution)/shard_map/reduce_scatter | solution.py:1527
  405.7 36.0 %copy-start.26 = (bf16[8,48,1536]{2,1,0:T(8,128)(2,1)S(1)}, bf16[8,48,1536]{2,1,0:T(8,128)(2,1)}, u32[]{:S(2)}) copy-start(bf16[8,48,1536]{2,1,0:T(8,128)(2,1)} %copy-done.24) | copy-start | bytes 3538948
  445.4 13.4 %copy-start.64 = (bf16[512,1536]{1,0:T(8,128)(2,1)S(1)}, bf16[512,1536]{1,0:T(8,128)(2,1)}, u32[]{:S(2)}) copy-start(bf16[512,1536]{1,0:T(8,128)(2,1)} %copy-done.63) | copy-start | bytes 4718596
  445.4 13.4 %copy-start.99 = (bf16[512,1024]{1,0:T(8,128)(2,1)S(1)}, bf16[512,1024]{1,0:T(8,128)(2,1)}, u32[]{:S(2)}) copy-start(bf16[512,1024]{1,0:T(8,128)(2,1)} %get-tuple-element.324) | copy-start | bytes 3145732
  563.0 115.4 %reduce-scatter.13.cloned.1.call-start = ((), (), s32[]{:S(2)}) async-start(), calls=%async_computation.16 | async-start | bytes 3981312 | tf_op jit(solution)/shard_map/reduce_scatter | solution.py:1527
  574.6 151.6 %reduce-scatter.15.cloned.1.call-start = ((), (), s32[]{:S(2)}) async-start(), calls=%async_computation.17 | async-start | bytes 3538944 | tf_op jit(solution)/shard_map/reduce_scatter | solution.py:1527
  578.4 36.1 %copy-start.73 = (f32[512,2048]{1,0:T(8,128)S(1)}, f32[512,2048]{1,0:T(8,128)}, u32[]{:S(2)}) copy-start(f32[512,2048]{1,0:T(8,128)} %copy-done.72) | copy-start | bytes 12582916
  624.3 152.7 %reduce-scatter.17.cloned.1.call-start = ((), (), s32[]{:S(2)}) async-start(), calls=%async_computation.18 | async-start | bytes 7077888 | tf_op jit(solution)/shard_map/reduce_scatter | solution.py:1527
  639.8 172.5 %reduce-scatter.21.cloned.1.call-start = ((), (), s32[]{:S(2)}) async-start(), calls=%async_computation.20 | async-start | bytes 2654208 | tf_op jit(solution)/shard_map/reduce_scatter | solution.py:1527
  693.0 170.8 %reduce-scatter.19.cloned.1.call-start = ((), (), s32[]{:S(2)}) async-start(), calls=%async_computation.19 | async-start | bytes 2654208 | tf_op jit(solution)/shard_map/reduce_scatter | solution.py:1527
  777.0 119.1 %reduce-scatter.23.cloned.1.call-start = ((), (), s32[]{:S(2)}) async-start(), calls=%async_computation.21 | async-start | bytes 2654208 | tf_op jit(solution)/shard_map/reduce_scatter | solution.py:1527
  782.8 10.7 %copy-start.74 = (f32[512,768]{1,0:T(8,128)S(1)}, f32[512,768]{1,0:T(8,128)}, u32[]{:S(2)}) copy-start(f32[512,768]{1,0:T(8,128)} %get-tuple-element.185) | copy-start | bytes 4718596
  817.8 45.2 %collective-permute-start.1 = (bf16[48,1536]{1,0:T(8,128)(2,1)S(1)}, bf16[48,1536]{1,0:T(8,128)(2,1)S(1)}, u32[]{:S(2)}, u32[]{:S(2)}) collective-permute-start(bf16[48,1536]{1,0:T(8,128)(2,1)S(1)} %convert_element_type.180), channel_id=1, source_target_pairs={{0,0},{1,1},{8,2},{9,3},{16,4},{17,5},{24,6},{25,7},{2,8},{3,9},{1... | collective-permute-start | bytes 442376 | tf_op jit(solution)/shard_map/ppermute | solution.py:1785
  863.1 51.7 %copy-start.33 = (f32[128,1536]{1,0:T(8,128)S(1)}, f32[128,1536]{1,0:T(8,128)}, u32[]{:S(2)}) copy-start(f32[128,1536]{1,0:T(8,128)} %copy-done.32) | copy-start | bytes 2359300
  (86 other events, 261.7 us)
Sparse Core Ops, SparseCore 0:
  9.7 46.1 all-gather.6
  93.3 69.1 all-gather.8
  164.2 42.7 all-gather.10
  208.5 40.3 all-gather.12
  250.4 74.7 all-gather.16
  326.7 40.1 all-gather.14
  405.4 107.5 reduce-scatter.8
  563.1 48.3 reduce-scatter.10
  613.8 42.5 reduce-scatter.12
  658.7 38.5 reduce-scatter.14
  699.7 72.6 reduce-scatter.16
  774.6 33.8 reduce-scatter.20
  810.9 48.0 reduce-scatter.18
  861.3 34.7 reduce-scatter.22

commit v6 on v5

--- a/solution.py
+++ b/solution.py
@@ -1736,6 +1736,8 @@
     ).astype(BF)
     dxz = jnp.concatenate([dxs_low, dz_low], axis=1)
     dxz, dw_x, grad_mix, raw_ao = together(dxz, tn(nh1, dxs_low).astype(BF), grad_mix, raw_ao)
+    grad_ao = lax.ppermute(raw_ao.astype(BF), ("t", "p", "c"), [(b, a) for a, b in pairs]).astype(F32)
+    dxz, grad_ao = together(dxz, grad_ao)
     raw_x = scatter_tc(dw_x)
     small = jnp.concatenate(
         [
@@ -1782,7 +1784,6 @@
     grad_n2, grad_n3, grad_n4 = grad_n2[:, 0], grad_n3[:, 0], grad_n4[:, 0]
     raw_x, z_b, small_grads = together(raw_x, z_b, small_grads)
     (x_b,) = run_jobs(20, spread_job(True, (blocks(raw_x),)))
-    grad_ao = lax.ppermute(raw_ao.astype(BF), ("t", "p", "c"), [(b, a) for a, b in pairs]).astype(F32)
 
     grad_n1, grad_in = finish((x_b, z_b), in_proj, norm_mixer, chunks[0])
     return (

time: 934 us -> 929 us (level)
  waiting for transfers between devices: 68.4 us -> 54.6 us
    reduce_scatter x8, waiting for transfers between devices: 65.8 us -> 52 us  [scatter_tc(): return lax.psum_scatter(x, ('t', 'c'), scatter_dimension=0, tiled=True)]
    unnamed x210 -> x208, local copies, waits for them, and re-layouts: 50.6 us -> 50.7 us
  transfers between devices with their start and end apart: 16 -> 16, of which waited for: 2 -> 2; matrix products, arithmetic and copies ran while one was open for 18% -> 19% of each run, Pallas kernels for 58% -> 59%
where the time goes in v6:
time: 929 us; the launch traced here: 919 us
  Pallas kernels  598 us (64%)
  matrix products  130 us (14%)
  local copies, waits for them, and re-layouts  73.7 us (8%)
  waiting for transfers between devices  54.6 us (6%)
  other arithmetic  40.5 us (4%)
  between operations  16.1 us (2%)
    pallas_call x7, Pallas kernels, turn(): pl.pallas_call(functools.partial(turn_body, back, gather, parts, jobs, (l...  260 us
    pallas_call x1, Pallas kernels, first_call(): pl.pallas_call(functools.partial(first_body, T, chunks), out_shape=(out((...  72.1 us
    reduce_scatter x8, waiting for transfers between devices, scatter_tc(): return lax.psum_scatter(x, ('t', 'c'), scatter_dimension=0, tiled=True)  52 us
    unnamed x208, local copies, waits for them, and re-layouts  50.7 us
    dot_general x10, matrix products, nt(): lax.dot_general(a, b, (((1,), (1,)), ((), ())), preferred_element_type=F32)  47.5 us
    pallas_call x1, Pallas kernels, keys_back_call(): pl.pallas_call(functools.partial(keys_back_body, T, hops, jobs, (len(args...  43.8 us
    dot_general x9, matrix products, nn(): return jnp.dot(a, b, preferred_element_type=F32)  43.7 us
    dot_general x11, matrix products, tn(): lax.dot_general(a, b, (((0,), (0,)), ((), ())), preferred_element_type=F32)  39.3 us
  transfers between devices with their start and end apart: 16, of which 2 were waited for; matrix products, arithmetic and copies ran while one was open for 19% of the time, Pallas kernels for 59%

profile of v6, /device:TPU:1, one launch (start us, length us, event | category | flops | bytes accessed | tf_op | source)
XLA Modules:
  0.0 918.9 jit_solution(12211451002870399972)
XLA Ops:
  17.8 72.1 %first.1 = (bf16[528,1536]{1,0:T(8,128)(2,1)S(1)}, s32[16,8,128]{2,1,0:T(8,128)S(1)}, bf16[8,96,256]{2,1,0:T(8,128)(2,1)S(1)}, bf16[8,4,48,1536]{3,2,1,0:T(8,128...) custom-call(bf16[128,1536]{1,0:T(8,128)(2,1)S(1)} %bitcast.103, ...), custom_call_target="tpu_custom_call" | custom-call | tf_op jit(solution)/shard_map/first/pallas_call | solution.py:338
  100.5 7.2 fusion.66.xz
  114.5 12.4 %plane_sum3.1 = f32[512,128]{1,0:T(8,128)S(1)} custom-call(f32[512,128]{1,0:T(8,128)S(1)} %copy-done.52), custom_call_target="tpu_custom_call" | custom-call | tf_op jit(solution)/shard_map/plane_sum3/pallas_call | solution.py:558
  135.1 9.8 %scan_one.1 = f32[16,768]{1,0:T(8,128)} custom-call(f32[512,768]{1,0:T(8,128)} %get-tuple-element.330.delta, f32[512,768]{1,0:T(8,128)} %get-tuple-element.131.u, f32[16,768]{1,0:T(8,128)} %fusion.22.a2.refs_1_, f32[8192,128]{1,0:T(8,128)} %broadcast_in_dim.91.brep, f32[512]{0:T(512)} %broadcast_select_fusion.first), custom_call_target="tpu_custom_call" | custom-call | tf_op jit(solution)/shard_map/scan_one/pallas_call | solution.py:1263
  146.0 11.8 %chain4.1.h_in = f32[16,768]{1,0:T(8,128)S(1)} custom-call(f32[24,768]{1,0:T(8,128)S(1)} %fusion.16.refs_0_, f32[16,768]{1,0:T(8,128)S(1)} %copy-done.6), custom_call_target="tpu_custom_call" | custom-call | tf_op jit(solution)/shard_map/chain4/pallas_call | solution.py:892
  161.0 16.7 %scan_two.1 = (f32[512,768]{1,0:T(8,128)}, f32[128,768]{1,0:T(8,128)}) custom-call(f32[512,768]{1,0:T(8,128)} %get-tuple-element.330.delta, f32[512,768]{1,0:T(8,128)} %get-tuple-element.131.u, f32[16,768]{1,0:T(8,128)} %fusion.22.a2.refs_1_, f32[8192,128]{1,0:T(8,128)} %broadcast_in_dim.91.brep, f32[8192,128]{1,0:T(8,128)} %broadcast_in_dim.93.crep, ...), custom_call_target="tpu_custom_call" | custom-call | tf_op jit(solution)/shard_map/scan_two/pallas_call | solution.py:1302
  186.4 36.5 %turn5.1 = (f32[128,1536]{1,0:T(8,128)S(1)}, bf16[512,1536]{1,0:T(8,128)(2,1)S(1)}) custom-call(bf16[512,1536]{1,0:T(8,128)(2,1)S(1)} %convolution_convert_fusion.15.refs_0_, f32[128,1536]{1,0:T(8,128)S(1)} %bitcast_convert_fusion.2.refs_1_), custom_call_target="tpu_custom_call" | custom-call | tf_op jit(solution)/shard_map/turn5/pallas_call | solution.py:819
  237.8 44.6 %turn6.1 = (f32[128,1536]{1,0:T(8,128)S(1)}, bf16[512,1536]{1,0:T(8,128)(2,1)S(1)}, bf16[8,48,1536]{2,1,0:T(8,128)(2,1)S(1)}) custom-call(bf16[512,1536]{1,0:T(8,128)(2,1)S(1)} %convolution_convert_fusion.14.refs_0_, f32[128,1536]{1,0:T(8,128)S(1)} %get-tuple-element.135.refs_1_, bf16[48,1536]{1,0:T(8,128)(2,1)S(1)} %collective-permute-done.refs_2_), custom_call_target="tpu_custom_call" | custom-call | tf_op jit(solution)/shard_map/turn6/pallas_call | solution.py:819
  289.4 34.2 %keys.1 = (bf16[512,384]{1,0:T(8,128)(2,1)S(1)}, bf16[1536,384]{1,0:T(8,128)(2,1)S(1)}, bf16[1536,384]{1,0:T(8,128)(2,1)S(1)}, bf16[512,1536]{1,0:T(8,128)(2,1)S(1)}) custom-call(f32[512,1152]{1,0:T(8,128)S(1)} %fusion.68.qkv, f32[512,128]{1,0:T(8,128)S(1)} %get-tuple-element.349.cosine.refs_3_, f32[512,128]{1,0:T(8,128)S(1)} %get-tuple-element.350.sine.refs_4_, ...), custom_call_target="tpu_custom_call" | custom-call | tf_op jit(solution)/shard_map/keys/pallas_call | solution.py:990
  327.6 9.2 %attend.1 = (bf16[512,384]{1,0:T(8,128)(2,1)}, f32[512,384]{1,0:T(8,128)}) custom-call(bf16[512,384]{1,0:T(8,128)(2,1)} %copy-done.23, bf16[1536,384]{1,0:T(8,128)(2,1)} %copy-done, bf16[1536,384]{1,0:T(8,128)(2,1)} %copy-done.1, bf16[512,1536]{1,0:T(8,128)(2,1)} %select_convert_fusion.bias), custom_call_target="tpu_custom_call" | custom-call | tf_op jit(solution)/shard_map/attend/pallas_call | solution.py:1455
  338.9 34.3 %turn8.1 = (f32[128,1536]{1,0:T(8,128)S(1)}, bf16[512,1536]{1,0:T(8,128)(2,1)S(1)}) custom-call(bf16[512,1536]{1,0:T(8,128)(2,1)S(1)} %convolution_convert_fusion.13.refs_0_, f32[128,1536]{1,0:T(8,128)S(1)} %get-tuple-element.146.refs_1_), custom_call_target="tpu_custom_call" | custom-call | tf_op jit(solution)/shard_map/turn8/pallas_call | solution.py:819
  374.4 8.7 fusion.69
  383.0 7.2 multiply_convert_fusion.4
  397.1 8.0 convolution_convert_fusion.12.refs_0_
  408.2 33.4 %turn10.1 = (f32[128,1536]{1,0:T(8,128)S(1)}, bf16[512,1536]{1,0:T(8,128)(2,1)S(1)}) custom-call(bf16[512,1536]{1,0:T(8,128)(2,1)S(1)} %copy-done.19, f32[128,1536]{1,0:T(8,128)S(1)} %get-tuple-element.150.refs_1_.refs_6_, f32[128,1536]{1,0:T(8,128)S(1)} %bitcast_convert_fusion.refs_2_), custom_call_target="tpu_custom_call" | custom-call | tf_op jit(solution)/shard_map/turn10/pallas_call | solution.py:819
  445.2 13.3 %attend_back.1 = (f32[512,384]{1,0:T(8,128)}, f32[1536,384]{1,0:T(8,128)}, f32[1536,384]{1,0:T(8,128)}) custom-call(bf16[512,384]{1,0:T(8,128)(2,1)} %copy-done.23, bf16[1536,384]{1,0:T(8,128)(2,1)} %copy-done, bf16[1536,384]{1,0:T(8,128)(2,1)} %copy-done.1, bf16[512,1536]{1,0:T(8,128)(2,1)} %select_convert_fusion.bias, f32[512,384]{1,0:T(8,128)} %get-tuple-element.142.lse, ...), custom_call_target="tpu_custom_call" | custom-call | tf_op jit(solution)/shard_map/attend_back/pallas_call | solution.py:1503
  467.3 45.5 %reduce-scatter.9.cloned.1.call-done = bf16[192,2048]{1,0:T(8,128)(2,1)} async-done(((bf16[1536,2048]{1,0:T(8,128)(2,1)}), bf16[192,2048]{1,0:T(8,128)(2,1)}) %reduce-scatter.9.cloned.1.call-update) | async-done | bytes 786448 | tf_op jit(solution)/shard_map/reduce_scatter | solution.py:1527
  517.3 43.8 %keys_back.1 = (bf16[512,1152]{1,0:T(8,128)(2,1)S(1)}, f32[128,1536]{1,0:T(8,128)S(1)}) custom-call(f32[512,384]{1,0:T(8,128)S(1)} %copy-done.29, f32[1536,384]{1,0:T(8,128)} %get-tuple-element.156.refs_1_, f32[1536,384]{1,0:T(8,128)} %get-tuple-element.157.refs_2_, f32[512,128]{1,0:T(8,128)S(1)} %copy-done.9, f32[512,128]{1,0:T(8,128)S(1)} %copy-done.11, ...), custom_call_target="tpu_custom_call" | custom-call | tf_op jit(solution)/shard_map/keys_back/pallas_call | solution.py:1120
  578.4 36.2 %turn12.1 = (f32[128,1536]{1,0:T(8,128)S(1)}, bf16[512,1536]{1,0:T(8,128)(2,1)S(1)}, f32[48,1536]{1,0:T(8,128)S(1)}) custom-call(bf16[512,1536]{1,0:T(8,128)(2,1)S(1)} %copy-done.18, f32[128,1536]{1,0:T(8,128)S(1)} %get-tuple-element.146.refs_1_, f32[128,1536]{1,0:T(8,128)S(1)} %copy-done.43, bf16[8,48,1536]{2,1,0:T(8,128)(2,1)S(1)} %bitcast.106), custom_call_target="tpu_custom_call" | custom-call | tf_op jit(solution)/shard_map/turn12/pallas_call | solution.py:819
  625.9 7.1 convolution_convert_fusion
  633.0 6.9 convolution_convert_fusion.10.refs_0_
  641.4 35.1 %turn13.1 = (f32[128,1536]{1,0:T(8,128)S(1)}, bf16[512,1536]{1,0:T(8,128)(2,1)S(1)}) custom-call(bf16[512,1536]{1,0:T(8,128)(2,1)S(1)} %convolution_convert_fusion.10.refs_0_, f32[128,1536]{1,0:T(8,128)S(1)} %get-tuple-element.135.refs_1_, f32[128,1536]{1,0:T(8,128)S(1)} %copy-done.36), custom_call_target="tpu_custom_call" | custom-call | tf_op jit(solution)/shard_map/turn13/pallas_call | solution.py:819
  683.2 6.2 multiply_convert_fusion.6
  693.2 9.7 %scan_three.1 = f32[16,768]{1,0:T(8,128)} custom-call(f32[512,768]{1,0:T(8,128)} %get-tuple-element.330.delta, f32[512,768]{1,0:T(8,128)} %get-tuple-element.174.dy, f32[16,768]{1,0:T(8,128)} %fusion.22.a2.refs_1_, f32[8192,128]{1,0:T(8,128)} %broadcast_in_dim.93.crep, f32[512]{0:T(512)} %broadcast_select_fusion.first), custom_call_target="tpu_custom_call" | custom-call | tf_op jit(solution)/shard_map/scan_three/pallas_call | solution.py:1332
  703.8 20.2 %chain14.1 = (f32[16,768]{1,0:T(8,128)S(1)}, bf16[4,48,2048]{2,1,0:T(8,128)(2,1)S(1)}, bf16[4,48,1152]{2,1,0:T(8,128)(2,1)S(1)}) custom-call(f32[24,768]{1,0:T(8,128)S(1)} %fusion.18.refs_0_, f32[16,768]{1,0:T(8,128)S(1)} %copy-done.7, bf16[4,48,2048]{2,1,0:T(8,128)(2,1)S(1)} %bitcast.107, bf16[4,48,1152]{2,1,0:T(8,128)(2,1)S(1)} %bitcast.109), custom_call_target="tpu_custom_call" | custom-call | tf_op jit(solution)/shard_map/chain14/pallas_call | solution.py:892
  726.3 39.3 %scan_four.1 = (f32[512,768]{1,0:T(8,128)}, f32[512,768]{1,0:T(8,128)}, f32[8192,128]{1,0:T(8,128)}, f32[8192,128]{1,0:T(8,128)}, f32[16,768]{1,0:T(8,128)}) custom-call(f32[512,768]{1,0:T(8,128)} %get-tuple-element.330.delta, f32[512,768]{1,0:T(8,128)} %get-tuple-element.131.u, f32[512,768]{1,0:T(8,128)} %get-tuple-element.174.dy, ...), custom_call_target="tpu_custom_call" | custom-call | tf_op jit(solution)/shard_map/scan_four/pallas_call | solution.py:1413
  784.2 9.3 %plane_sum15.1 = f32[512,128]{1,0:T(8,128)S(1)} custom-call(f32[512,128]{1,0:T(8,128)S(1)} %pad_maximum_fusion.7.x), custom_call_target="tpu_custom_call" | custom-call | tf_op jit(solution)/shard_map/plane_sum15/pallas_call | solution.py:558
  795.0 7.8 conv_back.1
  829.9 39.9 %turn17.1 = (f32[128,1536]{1,0:T(8,128)S(1)}, f32[96,256]{1,0:T(8,128)S(1)}, bf16[4,48,2048]{2,1,0:T(8,128)(2,1)S(1)}, f32[48,128]{1,0:T(8,128)S(1)}, bf16[48,81...) custom-call(bf16[512,1536]{1,0:T(8,128)(2,1)S(1)} %convolution_convert_fusion.9.refs_0_, ...), custom_call_target="tpu_custom_call" | custom-call | tf_op jit(solution)/shard_map/turn17/pallas_call | solution.py:819
  877.1 6.6 jobs22.1
  884.5 6.4 reduce-scatter.23.cloned.1.call-done
  891.9 9.9 %jobs20.1.refs_0_ = bf16[4,48,768]{2,1,0:T(8,128)(2,1)S(1)} custom-call(bf16[4,48,768]{2,1,0:T(8,128)(2,1)S(1)} %bitcast.110), custom_call_target="tpu_custom_call" | custom-call | tf_op jit(solution)/shard_map/jobs20/pallas_call | solution.py:526
  (371 shorter events, 213.2 us)
Async XLA Ops:
  7.2 176.2 %all-gather.7.cloned.1.call-start = ((), (), s32[]{:S(2)}) async-start(), calls=%async_computation.8 | async-start | bytes 2654208 | tf_op jit(solution)/shard_map/all_gather | solution.py:1515
  7.9 216.2 %all-gather.9.cloned.1.call-start = ((), (), s32[]{:S(2)}) async-start(), calls=%async_computation.9 | async-start | bytes 7077888 | tf_op jit(solution)/shard_map/all_gather | solution.py:1515
  17.8 77.4 %copy-start.97 = (bf16[48,1536]{1,0:T(8,128)(2,1)S(1)}, bf16[48,1536]{1,0:T(8,128)(2,1)}, u32[]{:S(2)}) copy-start(bf16[48,1536]{1,0:T(8,128)(2,1)} %param.40) | copy-start | bytes 442372
  93.2 33.9 %copy-start.15 = (bf16[8,96,256]{2,1,0:T(8,128)(2,1)}, bf16[8,96,256]{2,1,0:T(8,128)(2,1)S(1)}, u32[]{:S(2)}) copy-start(bf16[8,96,256]{2,1,0:T(8,128)(2,1)S(1)} %get-tuple-element.129) | copy-start | bytes 1179652
  93.2 140.6 %all-gather.11.cloned.1.call-start = ((), (), s32[]{:S(2)}) async-start(), calls=%async_computation.10 | async-start | bytes 3538944 | tf_op jit(solution)/shard_map/all_gather | solution.py:1515
  93.9 190.7 %all-gather.13.cloned.1.call-start = ((), (), s32[]{:S(2)}) async-start(), calls=%async_computation.11 | async-start | bytes 3981312 | tf_op jit(solution)/shard_map/all_gather | solution.py:1515
  94.5 279.9 %all-gather.17.cloned.1.call-start = ((), (), s32[]{:S(2)}) async-start(), calls=%async_computation.13 | async-start | bytes 7077888 | tf_op jit(solution)/shard_map/all_gather | solution.py:1515
  95.1 287.9 %all-gather.15.cloned.1.call-start = ((), (), s32[]{:S(2)}) async-start(), calls=%async_computation.12 | async-start | bytes 3538944 | tf_op jit(solution)/shard_map/all_gather | solution.py:1515
  95.2 142.6 %collective-permute-start = (bf16[48,1536]{1,0:T(8,128)(2,1)S(1)}, bf16[48,1536]{1,0:T(8,128)(2,1)S(1)}, u32[]{:S(2)}, u32[]{:S(2)}) collective-permute-start(bf16[48,1536]{1,0:T(8,128)(2,1)S(1)} %copy-done.97), channel_id=1, source_target_pairs={{0,0},{1,1},{2,8},{3,9},{4,16},{5,17},{6,24},{7,25},{8,2},{9,3},{1... | collective-permute-start | bytes 442376 | tf_op jit(solution)/shard_map/ppermute | solution.py:1585
  95.9 417.0 %reduce-scatter.9.cloned.1.call-start = ((), (), s32[]{:S(2)}) async-start(), calls=%async_computation.14 | async-start | bytes 7077888 | tf_op jit(solution)/shard_map/reduce_scatter | solution.py:1527
  96.8 81.2 %copy-start.86 = (f32[768]{0:T(1024)}, f32[768]{0:T(1024)S(1)}, u32[]{:S(2)}) copy-start(f32[768]{0:T(1024)S(1)} %get-tuple-element.316) | copy-start | bytes 9220
  130.6 14.3 %copy-start.84 = (f32[1,768]{1,0:T(1,128)}, f32[1,768]{1,0:T(1,128)S(1)}, u32[]{:S(2)}) copy-start(f32[1,768]{1,0:T(1,128)S(1)} %broadcast_in_dim.96) | copy-start | bytes 9220
  130.7 14.3 %copy-start.89 = (f32[24]{0:T(128)}, f32[24]{0:T(128)S(1)}, u32[]{:S(2)}) copy-start(f32[24]{0:T(128)S(1)} %pad.34.clone) | copy-start | bytes 292
  131.4 13.5 %copy-start.91 = (f32[24]{0:T(128)}, f32[24]{0:T(128)S(1)}, u32[]{:S(2)}) copy-start(f32[24]{0:T(128)S(1)} %pad.33.clone) | copy-start | bytes 292
  135.1 10.9 %copy-start.6 = (f32[16,768]{1,0:T(8,128)S(1)}, f32[16,768]{1,0:T(8,128)}, u32[]{:S(2)}) copy-start(f32[16,768]{1,0:T(8,128)} %fusion.22.a2.refs_1_) | copy-start | bytes 147460
  161.0 16.9 %copy-start.70 = (f32[512,768]{1,0:T(8,128)S(1)}, f32[512,768]{1,0:T(8,128)}, u32[]{:S(2)}) copy-start(f32[512,768]{1,0:T(8,128)} %get-tuple-element.131.u) | copy-start | bytes 4718596
  177.9 111.4 %copy-start.8 = (f32[512,128]{1,0:T(8,128)}, f32[512,128]{1,0:T(8,128)S(1)}, u32[]{:S(2)}) copy-start(f32[512,128]{1,0:T(8,128)S(1)} %get-tuple-element.349.cosine.refs_3_) | copy-start | bytes 786436
  177.9 111.4 %copy-start.10 = (f32[512,128]{1,0:T(8,128)}, f32[512,128]{1,0:T(8,128)S(1)}, u32[]{:S(2)}) copy-start(f32[512,128]{1,0:T(8,128)S(1)} %get-tuple-element.350.sine.refs_4_) | copy-start | bytes 786436
  405.1 234.8 %reduce-scatter.11.cloned.1.call-start = ((), (), s32[]{:S(2)}) async-start(), calls=%async_computation.15 | async-start | bytes 3538944 | tf_op jit(solution)/shard_map/reduce_scatter | solution.py:1527
  405.6 36.0 %copy-start.26 = (bf16[8,48,1536]{2,1,0:T(8,128)(2,1)S(1)}, bf16[8,48,1536]{2,1,0:T(8,128)(2,1)}, u32[]{:S(2)}) copy-start(bf16[8,48,1536]{2,1,0:T(8,128)(2,1)} %copy-done.24) | copy-start | bytes 3538948
  445.2 13.3 %copy-start.64 = (bf16[512,1536]{1,0:T(8,128)(2,1)S(1)}, bf16[512,1536]{1,0:T(8,128)(2,1)}, u32[]{:S(2)}) copy-start(bf16[512,1536]{1,0:T(8,128)(2,1)} %copy-done.63) | copy-start | bytes 4718596
  445.2 13.3 %copy-start.98 = (bf16[512,1024]{1,0:T(8,128)(2,1)S(1)}, bf16[512,1024]{1,0:T(8,128)(2,1)}, u32[]{:S(2)}) copy-start(bf16[512,1024]{1,0:T(8,128)(2,1)} %get-tuple-element.328) | copy-start | bytes 3145732
  563.0 115.5 %reduce-scatter.13.cloned.1.call-start = ((), (), s32[]{:S(2)}) async-start(), calls=%async_computation.16 | async-start | bytes 3981312 | tf_op jit(solution)/shard_map/reduce_scatter | solution.py:1527
  574.6 151.7 %reduce-scatter.15.cloned.1.call-start = ((), (), s32[]{:S(2)}) async-start(), calls=%async_computation.17 | async-start | bytes 3538944 | tf_op jit(solution)/shard_map/reduce_scatter | solution.py:1527
  578.4 36.3 %copy-start.73 = (f32[512,2048]{1,0:T(8,128)S(1)}, f32[512,2048]{1,0:T(8,128)}, u32[]{:S(2)}) copy-start(f32[512,2048]{1,0:T(8,128)} %copy-done.72) | copy-start | bytes 12582916
  624.5 152.6 %reduce-scatter.17.cloned.1.call-start = ((), (), s32[]{:S(2)}) async-start(), calls=%async_computation.18 | async-start | bytes 7077888 | tf_op jit(solution)/shard_map/reduce_scatter | solution.py:1527
  640.0 172.3 %reduce-scatter.21.cloned.1.call-start = ((), (), s32[]{:S(2)}) async-start(), calls=%async_computation.20 | async-start | bytes 2654208 | tf_op jit(solution)/shard_map/reduce_scatter | solution.py:1527
  693.1 10.6 %copy-start.7 = (f32[16,768]{1,0:T(8,128)S(1)}, f32[16,768]{1,0:T(8,128)}, u32[]{:S(2)}) copy-start(f32[16,768]{1,0:T(8,128)} %fusion.22.a2.refs_1_) | copy-start | bytes 147460
  693.2 181.8 %reduce-scatter.19.cloned.1.call-start = ((), (), s32[]{:S(2)}) async-start(), calls=%async_computation.19 | async-start | bytes 2654208 | tf_op jit(solution)/shard_map/reduce_scatter | solution.py:1527
  777.1 113.8 %reduce-scatter.23.cloned.1.call-start = ((), (), s32[]{:S(2)}) async-start(), calls=%async_computation.21 | async-start | bytes 2654208 | tf_op jit(solution)/shard_map/reduce_scatter | solution.py:1527
  813.0 10.0 %collective-permute-start.1 = (bf16[48,1536]{1,0:T(8,128)(2,1)}, bf16[48,1536]{1,0:T(8,128)(2,1)}, u32[]{:S(2)}, u32[]{:S(2)}) collective-permute-start(bf16[48,1536]{1,0:T(8,128)(2,1)} %convert_element_type.172), channel_id=1, source_target_pairs={{0,0},{1,1},{8,2},{9,3},{16,4},{17,5},{24,6},{25,7},{2,8},{3,9},{1... | collective-permute-start | bytes 442376 | tf_op jit(solution)/shard_map/ppermute | solution.py:1739
  875.0 34.7 %copy-start.33 = (f32[128,1536]{1,0:T(8,128)S(1)}, f32[128,1536]{1,0:T(8,128)}, u32[]{:S(2)}) copy-start(f32[128,1536]{1,0:T(8,128)} %copy-done.32) | copy-start | bytes 2359300
  (85 other events, 251.4 us)
Sparse Core Ops, SparseCore 0:
  9.7 46.1 all-gather.6
  93.3 69.1 all-gather.8
  164.2 42.7 all-gather.10
  208.5 40.3 all-gather.12
  250.4 74.7 all-gather.16
  326.7 40.1 all-gather.14
  405.2 107.5 reduce-scatter.8
  563.1 48.0 reduce-scatter.10
  613.6 42.7 reduce-scatter.12
  658.6 38.4 reduce-scatter.14
  699.5 72.8 reduce-scatter.16
  774.6 33.9 reduce-scatter.20
  811.1 45.8 reduce-scatter.18
  859.3 31.6 reduce-scatter.22
